TPU v7x, 32 devices: a whole 2x2x4 slice. The times are simulated.
32 devices in a mesh: member: 2 (over x), patch: 16 (over z, y, core).
Axes of the slice: x: 2, y: 2, z: 4, core: 2. Of those that a mesh axis runs over, the one named last changes fastest.
Arguments:
- log_rate: float32 [65536, 128], P(('member', 'patch')), parts along dimension 0, may hold values from -3 to 3
- log_state: float32 [65536, 128], P(('member', 'patch')), parts along dimension 0, may hold values from -3 to 3
- near_blocks: bfloat16 [512, 12, 128, 128], P(('member', 'patch')), parts along dimension 0, may hold values from -0.15625 to 0.15625
- near_columns: int32 [512, 12], P(('member', 'patch')), parts along dimension 0, may hold values from 0 to 255, as said below
- far_basis: bfloat16 [8, 32, 32768], P('member', None, 'patch'), parts along dimension 0, may hold values from -0.0625 to 0.0625
- far_coupling: bfloat16 [8, 32, 32768], P('member', None, 'patch'), parts along dimension 0, may hold values from -0.5 to 0.5
- self_stiffness: float32 [65536], P(('member', 'patch')), parts along dimension 0, may hold values from 1 to 3
- plate_rate: float32 [65536], P(('member', 'patch')), parts along dimension 0, may hold values from 0.5 to 2
- direct_effect: float32 [65536], P(('member', 'patch')), parts along dimension 0, may hold values from 0.3 to 1
- evolution_effect: float32 [65536], P(('member', 'patch')), parts along dimension 0, may hold values from 0.5 to 1.5
- triangle_area: float32 [65536], P(('member', 'patch')), parts along dimension 0, may hold values from 0.5 to 10.5
Outputs:
- new_log_rate: float32 [65536, 128], P(('member', 'patch')), parts along dimension 0
- new_log_state: float32 [65536, 128], P(('member', 'patch')), parts along dimension 0
- error_norm: float32 [256], P('member'), parts along dimension 0
There are 2 independent parts, one for each index of `member`. A program takes and returns all parts, laid end to end along the dimension named above; each array names one. Nothing has to cross between parts.
Inputs may be any that keep to these rules, and one draw needn't show every extreme that they name: `near_columns`: row block r's 12 column blocks are distinct, each is (r + o) mod 256 with -6 <= o <= 6, and they include r itself and both blocks at distance 6.
All inputs are finite; a program needn't handle non-finite values.
Results may differ from a plain program's by a relative error of at most 0.0012.
Values may be sent and summed in bfloat16 or wider, within the bound.
No kernel may reach another device: no remote copies, remote signals or barrier semaphores. Data moves between devices by JAX's collectives and lax.ppermute only.
A program may use at most 128 MiB of HBM per device.

v0:
```python
import jax
import jax.numpy as jnp
from jax import lax
from jax.sharding import PartitionSpec as P

REACH = 6


step_size = 0.1
damping = 0.5
error_scale = 0.01


def partner_2(value, axis, stride):
    mask = 2**stride
    pairs = [(source, source ^ mask) for source in range(lax.axis_size(axis))]
    return lax.ppermute(value, axis, pairs)


def padded(cells, sides, width):
    for axis, dim in sides:
        count = lax.axis_size(axis)
        head = lax.slice_in_dim(cells, 0, width, axis=dim)
        tail = lax.slice_in_dim(cells, cells.shape[dim] - width, cells.shape[dim], axis=dim)
        cells = jnp.concatenate(
            [
                lax.ppermute(tail, axis, [(i, (i + 1) % count) for i in range(count)]),
                cells,
                lax.ppermute(head, axis, [((i + 1) % count, i) for i in range(count)]),
            ],
            axis=dim,
        )
    return cells


def partner_sums(projected, levels):
    coupled = []
    current = projected
    for tree_level in range(levels):
        partner = partner_2(current, "patch", tree_level)
        coupled.append(partner[0])
        current = current[1:] + partner[1:]
    return jnp.stack(coupled)


def on_device(
    log_rate,
    log_state,
    near_blocks,
    near_columns,
    far_basis,
    far_coupling,
    self_stiffness,
    plate_rate,
    direct_effect,
    evolution_effect,
    triangle_area,
):
    row_count, col_count = log_rate.shape
    row_blocks, near_count, block_size, _ = near_blocks.shape
    devices = lax.axis_size("patch")
    levels = devices.bit_length() - 1
    total_blocks = devices * row_blocks
    halo_rows = REACH * block_size
    first_block = lax.axis_index("patch") * row_blocks
    local_index = jnp.arange(row_blocks, dtype=jnp.int32)
    offset = (
        near_columns - (first_block + local_index)[:, None] + total_blocks // 2
    ) % total_blocks - total_blocks // 2
    position = local_index[:, None] + REACH + offset
    basis_flat = far_basis.reshape(-1, row_count)
    coupling = far_coupling.reshape(-1, row_count)

    def section_rates(rate_now, state_now):
        velocity = jnp.exp(rate_now)
        rate_bf = velocity.astype(jnp.bfloat16)
        extended = padded(rate_bf, (("patch", 0),), halo_rows)
        column_blocks = extended.reshape(-1, block_size, col_count)
        chosen = column_blocks[position]
        near_term = jnp.einsum(
            "rkij,rkjb->rib", near_blocks, chosen, preferred_element_type=jnp.float32
        ).reshape(row_count, col_count)
        projected = jnp.dot(basis_flat, rate_bf, preferred_element_type=jnp.float32).reshape(
            levels, -1
        )
        coupled = partner_sums(projected, levels).reshape(-1, col_count).astype(jnp.bfloat16)
        far_term = lax.dot_general(
            coupling, coupled, (((0,), (0,)), ((), ())), preferred_element_type=jnp.float32
        )
        stress_rate = (
            self_stiffness[:, None] * (plate_rate[:, None] - velocity) - near_term - far_term
        )
        state_rate = jnp.exp(-state_now) - velocity
        log_rate_rate = (stress_rate - evolution_effect[:, None] * state_rate) / (
            direct_effect[:, None] + damping * velocity
        )
        return (log_rate_rate, state_rate)

    rate_one, state_one = section_rates(log_rate, log_state)
    rate_two, state_two = section_rates(
        log_rate + step_size * rate_one, log_state + step_size * state_one
    )
    half_step = 0.5 * step_size
    new_log_rate = log_rate + half_step * (rate_one + rate_two)
    new_log_state = log_state + half_step * (state_one + state_two)
    rate_error = half_step * (rate_two - rate_one) / error_scale
    state_error = half_step * (state_two - state_one) / error_scale
    area_terms = jnp.sum(
        triangle_area[:, None] * (rate_error * rate_error + state_error * state_error), axis=0
    )
    totals, area_total = lax.psum((area_terms, jnp.sum(triangle_area)), "patch")
    error_norm = jnp.sqrt(totals / area_total + 1e-06)
    return (new_log_rate, new_log_state, error_norm)


def solution(mesh):
    in_specs = (
        P(("member", "patch"), None),
        P(("member", "patch"), None),
        P(("member", "patch"), None, None, None),
        P(("member", "patch"), None),
        P("member", None, "patch"),
        P("member", None, "patch"),
        P(("member", "patch")),
        P(("member", "patch")),
        P(("member", "patch")),
        P(("member", "patch")),
        P(("member", "patch")),
    )
    out_specs = (P(("member", "patch"), None), P(("member", "patch"), None), P("member"))
    return jax.shard_map(
        on_device, mesh=mesh, in_specs=in_specs, out_specs=out_specs, check_vma=False
    )
```

profile of v0, /device:TPU:0, one launch (start us, length us, event | category | flops | bytes accessed | tf_op | source)
XLA Modules:
  0.0 121.1 jit_solution(16478524655796271360)
XLA Ops:
  0.6 1.6 %copy.34 = f32[2048,128]{0,1:T(8,128)S(1)} copy(f32[2048,128]{1,0:T(8,128)} %param.11) | data formatting | bytes 2097152 | tf_op args[0]
  2.4 1.3 %fusion.14 = f32[128,128]{1,0:T(8,128)S(1)} fusion(bf16[128,2048]{1,0:T(8,128)(2,1)} %bitcast.56, bf16[2048,128]{0,1:T(8,128)(2,1)S(1)} %exponential_convert_fusion), kind=kOutput, calls=%fused_computation.50 | convolution fusion | flops 67108864 | bytes 1114112 | tf_op jit(solution)/shard_map/dot_general | solution.py:83
  4.4 5.7 %collective-permute-start.1 = (bf16[768,128]{0,1:T(8,128)(2,1)S(1)}, bf16[768,128]{0,1:T(8,128)(2,1)S(1)}, u32[]{:S(2)}, u32[]{:S(2)}) collective-permute-start(bf16[768,128]{0,1:T(8,128)(2,1)S(1)} %get-tuple-element.17), channel_id=1, source_target_pairs={{1,0},{2,1},{3,2},{4,3},{5,4},{6,5},{7,6},{8,7},{9,8},{10,9},{11,1... | collective-permute-start | bytes 589832 | tf_op jit(solution)/shard_map/ppermute | solution.py:29
  10.3 4.2 %collective-permute-done.3 = f32[3,4096]{1,0:T(4,128)S(1)} collective-permute-done((f32[3,4096]{1,0:T(4,128)S(1)}, f32[3,4096]{1,0:T(4,128)S(1)}, u32[]{:S(2)}, u32[]{:S(2)}) %collective-permute-start.3) | collective-permute-done | bytes 49184 | tf_op jit(solution)/shard_map/ppermute | solution.py:17
  14.6 1.8 %collective-permute-start.4 = (f32[2,4096]{1,0:T(2,128)S(1)}, f32[2,4096]{1,0:T(2,128)S(1)}, u32[]{:S(2)}, u32[]{:S(2)}) collective-permute-start(f32[2,4096]{1,0:T(2,128)S(1)} %slice_add_fusion.3), channel_id=1, source_target_pairs={{0,4},{1,5},{2,6},{3,7},{4,0},{5,1},{6,2},{7,3},{8,12},{9,13},{10,... | collective-permute-start | bytes 98312 | tf_op jit(solution)/shard_map/ppermute | solution.py:17
  16.4 0.8 compare_select_fusion
  17.3 1.3 %collective-permute-done.4 = f32[2,4096]{1,0:T(2,128)S(1)} collective-permute-done((f32[2,4096]{1,0:T(2,128)S(1)}, f32[2,4096]{1,0:T(2,128)S(1)}, u32[]{:S(2)}, u32[]{:S(2)}) %collective-permute-start.4) | collective-permute-done | bytes 32800 | tf_op jit(solution)/shard_map/ppermute | solution.py:17
  18.6 2.9 %collective-permute-start.5 = (bf16[1,4096]{1,0:T(2,128)(2,1)S(1)}, bf16[1,4096]{1,0:T(2,128)(2,1)S(1)}, u32[]{:S(2)}, u32[]{:S(2)}) collective-permute-start(bf16[1,4096]{1,0:T(2,128)(2,1)S(1)} %get-tuple-element.21), channel_id=1, source_target_pairs={{0,8},{1,9},{2,10},{3,11},{4,12},{5,13},{6,14},{7,15},{8,0},{9,1},... | collective-permute-start | bytes 24584 | tf_op jit(solution)/shard_map/ppermute | solution.py:17
  21.4 2.5 %copy.29 = f32[2048,128]{0,1:T(8,128)} copy(f32[2048,128]{1,0:T(8,128)} %param.12) | data formatting | bytes 2097152 | tf_op args[1]
  24.1 0.7 convert_element_type.27
  24.8 0.6 copy.27
  25.5 8.1 %gather_fusion = bf16[192,128,128]{2,1,0:T(8,128)(2,1)} fusion(bf16[28,128,128]{2,1,0:T(8,128)(2,1)S(1)} %bitcast.51, s32[1024]{0:T(1024)S(1)} %pad_clamp_fusion), kind=kCustom, calls=%fused_computation | custom fusion | bytes 12583680 | tf_op jit(solution)/shard_map/gather | solution.py:79
  33.5 6.4 %fusion.15 = f32[16,128,128,1]{1,2,3,0:T(8,128)S(1)} fusion(bf16[16,12,128,128]{3,2,1,0:T(8,128)(2,1)} %param.13, bf16[16,12,128,128]{3,2,1,0:T(8,128)(2,1)} %bitcast.53), kind=kOutput, calls=%fused_computation.51 | convolution fusion | flops 805306368 | bytes 13631488 | tf_op jit(solution)/shard_map/rkij,rkjb->rib/dot_general | solution.py:80
  40.0 1.3 %copy.28 = f32[2048,128]{0,1:T(8,128)} copy(f32[2048,128]{1,0:T(8,128)S(1)} %bitcast.54) | data formatting | bytes 2097152 | tf_op jit(solution)/shard_map/reshape | solution.py:82
  41.4 3.4 %fusion.9 = (bf16[2048,128]{0,1:T(8,128)(2,1)S(1)}, f32[2048,128]{0,1:T(8,128)}) fusion(f32[2048,128]{0,1:T(8,128)S(1)} %copy.34, f32[2048]{0:T(1024)S(1)} %copy-done.5, f32[2048,128]{0,1:T(8,128)} %copy.29, f32[2048]{0:T(1024)S(1)} %copy-done.7, bf16[128,128]{1,0:T(8,128)(2,1)S(1)} %copy-done.3, bf16[128,2048]{1,0:T(8,128)(2,1)S(1)} %bitcast.48, ...), kind=kOutput, calls=%fused_computation.45 | convolution fusion | flops 70778880 | bytes 5308416 | tf_op jit(solution)/shard_map/dot_general | solution.py:87
  45.2 1.2 collective-permute-done.8
  46.4 0.7 collective-permute-start.9
  47.1 3.6 %collective-permute-done.9 = f32[3,4096]{1,0:T(4,128)S(1)} collective-permute-done((f32[3,4096]{1,0:T(4,128)S(1)}, f32[3,4096]{1,0:T(4,128)S(1)}, u32[]{:S(2)}, u32[]{:S(2)}) %collective-permute-start.9) | collective-permute-done | bytes 49184 | tf_op jit(solution)/shard_map/ppermute | solution.py:17
  50.8 1.6 %collective-permute-start.10 = (f32[2,4096]{1,0:T(2,128)S(1)}, f32[2,4096]{1,0:T(2,128)S(1)}, u32[]{:S(2)}, u32[]{:S(2)}) collective-permute-start(f32[2,4096]{1,0:T(2,128)S(1)} %slice_add_fusion.2), channel_id=1, source_target_pairs={{0,4},{1,5},{2,6},{3,7},{4,0},{5,1},{6,2},{7,3},{8,12},{9,13},{10,... | collective-permute-start | bytes 98312 | tf_op jit(solution)/shard_map/ppermute | solution.py:17
  53.0 1.7 %collective-permute-done.10 = f32[2,4096]{1,0:T(2,128)S(1)} collective-permute-done((f32[2,4096]{1,0:T(2,128)S(1)}, f32[2,4096]{1,0:T(2,128)S(1)}, u32[]{:S(2)}, u32[]{:S(2)}) %collective-permute-start.10) | collective-permute-done | bytes 32800 | tf_op jit(solution)/shard_map/ppermute | solution.py:17
  54.8 2.1 %collective-permute-start.11 = (bf16[1,4096]{1,0:T(2,128)(2,1)S(1)}, bf16[1,4096]{1,0:T(2,128)(2,1)S(1)}, u32[]{:S(2)}, u32[]{:S(2)}) collective-permute-start(bf16[1,4096]{1,0:T(2,128)(2,1)S(1)} %get-tuple-element.19), channel_id=1, source_target_pairs={{0,8},{1,9},{2,10},{3,11},{4,12},{5,13},{6,14},{7,15},{8,0},{9,1},... | collective-permute-start | bytes 24584 | tf_op jit(solution)/shard_map/ppermute | solution.py:17
  57.6 1.9 %collective-permute-done.11 = bf16[1,4096]{1,0:T(2,128)(2,1)S(1)} collective-permute-done((bf16[1,4096]{1,0:T(2,128)(2,1)S(1)}, bf16[1,4096]{1,0:T(2,128)(2,1)S(1)}, u32[]{:S(2)}, u32[]{:S(2)}) %collective-permute-start.11) | collective-permute-done | bytes 8224 | tf_op jit(solution)/shard_map/ppermute | solution.py:17
  59.6 0.7 convert_element_type.29
  60.3 4.7 %collective-permute-done.6 = bf16[768,128]{0,1:T(8,128)(2,1)S(1)} collective-permute-done((bf16[768,128]{0,1:T(8,128)(2,1)S(1)}, bf16[768,128]{0,1:T(8,128)(2,1)S(1)}, u32[]{:S(2)}, u32[]{:S(2)}) %collective-permute-start.6) | collective-permute-done | bytes 196640 | tf_op jit(solution)/shard_map/ppermute | solution.py:27
  65.7 8.1 %gather_fusion.1 = bf16[192,128,128]{2,1,0:T(8,128)(2,1)} fusion(bf16[28,128,128]{2,1,0:T(8,128)(2,1)S(1)} %bitcast.50, s32[1024]{0:T(1024)S(1)} %pad_clamp_fusion), kind=kCustom, calls=%fused_computation.1 | custom fusion | bytes 12583680 | tf_op jit(solution)/shard_map/gather | solution.py:79
  73.8 6.4 %fusion.16 = f32[16,128,128,1]{1,2,3,0:T(8,128)S(1)} fusion(bf16[16,12,128,128]{3,2,1,0:T(8,128)(2,1)} %param.13, bf16[16,12,128,128]{3,2,1,0:T(8,128)(2,1)} %bitcast.52), kind=kOutput, calls=%fused_computation.52 | convolution fusion | flops 805306368 | bytes 13631488 | tf_op jit(solution)/shard_map/rkij,rkjb->rib/dot_general | solution.py:80
  80.3 1.3 %copy.40 = f32[2048,128]{0,1:T(8,128)} copy(f32[2048,128]{1,0:T(8,128)S(1)} %bitcast.55) | data formatting | bytes 2097152 | tf_op jit(solution)/shard_map/reshape | solution.py:82
  81.6 4.3 %multiply_reduce_fusion = (f32[128]{0:T(128)S(1)}, f32[2048,128]{0,1:T(8,128)S(1)}, f32[2048,128]{0,1:T(8,128)}) fusion(f32[2048,128]{0,1:T(8,128)} %get-tuple-element.23, f32[2048]{0:T(1024)S(1)} %copy-done.4, f32[2048,128]{0,1:T(8,128)} %copy.29, f32[2048,128]{0,1:T(8,128)S(1)} %copy.34, f32[2048]{0:T(1024)S(1)} %copy-done.6, f32[2048]{0:T(1024)S(1)} %copy-done.8, ...), kind=kOutput, calls=%fused_computation.11 | convolution fusion | flops 75497344 | bytes 6889984 | tf_op jit(solution)/shard_map/dot_general | solution.py:87
  86.0 2.5 %copy.36 = f32[2048,128]{1,0:T(8,128)} copy(f32[2048,128]{0,1:T(8,128)} %get-tuple-element.13) | data formatting | bytes 2097152
  88.5 1.3 %copy.37 = f32[2048,128]{1,0:T(8,128)} copy(f32[2048,128]{0,1:T(8,128)S(1)} %get-tuple-element.12) | data formatting | bytes 2097152
  89.8 30.1 %all-reduce = (f32[128]{0:T(128)S(1)}, f32[]{:T(128)}) all-reduce(f32[128]{0:T(128)S(1)} %get-tuple-element.11, f32[]{:T(128)} %reduce_sum.19), channel_id=1, replica_groups=mesh['member'=2,'patch'=16] {'patch'}, use_global_device_ids=true, to_apply=%region_1.2 | all-reduce | flops 129 | bytes 1032 | tf_op jit(solution)/shard_map/psum | solution.py:111
  119.9 1.1 add_sqrt_fusion
  (66 shorter events, 3.9 us)
Async XLA Ops:
  0.6 40.7 %copy-start = (bf16[4,32,2048]{2,1,0:T(8,128)(2,1)S(1)}, bf16[4,32,2048]{2,1,0:T(8,128)(2,1)}, u32[]{:S(2)}) copy-start(bf16[4,32,2048]{2,1,0:T(8,128)(2,1)} %param.16) | copy-start | bytes 1572868
  3.8 6.3 %collective-permute-start.2 = (f32[4,4096]{1,0:T(4,128)S(1)}, f32[4,4096]{1,0:T(4,128)S(1)}, u32[]{:S(2)}, u32[]{:S(2)}) collective-permute-start(f32[4,4096]{1,0:T(4,128)S(1)} %reshape.65), channel_id=1, source_target_pairs={{0,1},{1,0},{2,3},{3,2},{4,5},{5,4},{6,7},{7,6},{8,9},{9,8},{10,11... | collective-permute-start | bytes 196616 | tf_op jit(solution)/shard_map/ppermute | solution.py:17
  4.4 20.4 %collective-permute-start.1 = (bf16[768,128]{0,1:T(8,128)(2,1)S(1)}, bf16[768,128]{0,1:T(8,128)(2,1)S(1)}, u32[]{:S(2)}, u32[]{:S(2)}) collective-permute-start(bf16[768,128]{0,1:T(8,128)(2,1)S(1)} %get-tuple-element.17), channel_id=1, source_target_pairs={{1,0},{2,1},{3,2},{4,3},{5,4},{6,5},{7,6},{8,7},{9,8},{10,9},{11,1... | collective-permute-start | bytes 589832 | tf_op jit(solution)/shard_map/ppermute | solution.py:29
  10.1 14.7 %collective-permute-start = (bf16[768,128]{0,1:T(8,128)(2,1)S(1)}, bf16[768,128]{0,1:T(8,128)(2,1)S(1)}, u32[]{:S(2)}, u32[]{:S(2)}) collective-permute-start(bf16[768,128]{0,1:T(8,128)(2,1)S(1)} %get-tuple-element.16), channel_id=1, source_target_pairs={{0,1},{1,2},{2,3},{3,4},{4,5},{5,6},{6,7},{7,8},{8,9},{9,10},{10,1... | collective-permute-start | bytes 589832 | tf_op jit(solution)/shard_map/ppermute | solution.py:27
  10.2 4.3 %collective-permute-start.3 = (f32[3,4096]{1,0:T(4,128)S(1)}, f32[3,4096]{1,0:T(4,128)S(1)}, u32[]{:S(2)}, u32[]{:S(2)}) collective-permute-start(f32[3,4096]{1,0:T(4,128)S(1)} %slice_add_fusion.1), channel_id=1, source_target_pairs={{0,2},{1,3},{2,0},{3,1},{4,6},{5,7},{6,4},{7,5},{8,10},{9,11},{10,... | collective-permute-start | bytes 147464 | tf_op jit(solution)/shard_map/ppermute | solution.py:17
  14.6 4.0 %collective-permute-start.4 = (f32[2,4096]{1,0:T(2,128)S(1)}, f32[2,4096]{1,0:T(2,128)S(1)}, u32[]{:S(2)}, u32[]{:S(2)}) collective-permute-start(f32[2,4096]{1,0:T(2,128)S(1)} %slice_add_fusion.3), channel_id=1, source_target_pairs={{0,4},{1,5},{2,6},{3,7},{4,0},{5,1},{6,2},{7,3},{8,12},{9,13},{10,... | collective-permute-start | bytes 98312 | tf_op jit(solution)/shard_map/ppermute | solution.py:17
  18.6 5.4 %collective-permute-start.5 = (bf16[1,4096]{1,0:T(2,128)(2,1)S(1)}, bf16[1,4096]{1,0:T(2,128)(2,1)S(1)}, u32[]{:S(2)}, u32[]{:S(2)}) collective-permute-start(bf16[1,4096]{1,0:T(2,128)(2,1)S(1)} %get-tuple-element.21), channel_id=1, source_target_pairs={{0,8},{1,9},{2,10},{3,11},{4,12},{5,13},{6,14},{7,15},{8,0},{9,1},... | collective-permute-start | bytes 24584 | tf_op jit(solution)/shard_map/ppermute | solution.py:17
  33.5 7.8 %copy-start.3 = (bf16[128,128]{1,0:T(8,128)(2,1)S(1)}, bf16[128,128]{1,0:T(8,128)(2,1)}, u32[]{:S(2)}) copy-start(bf16[128,128]{1,0:T(8,128)(2,1)} %convert_element_type.27) | copy-start | bytes 98308
  33.5 7.8 %copy-start.5 = (f32[2048]{0:T(1024)S(1)}, f32[2048]{0:T(1024)}, u32[]{:S(2)}) copy-start(f32[2048]{0:T(1024)} %param.19) | copy-start | bytes 24580
  33.5 7.8 %copy-start.7 = (f32[2048]{0:T(1024)S(1)}, f32[2048]{0:T(1024)}, u32[]{:S(2)}) copy-start(f32[2048]{0:T(1024)} %param.20) | copy-start | bytes 24580
  33.5 7.8 %copy-start.9 = (f32[2048]{0:T(1024)S(1)}, f32[2048]{0:T(1024)}, u32[]{:S(2)}) copy-start(f32[2048]{0:T(1024)} %param.18) | copy-start | bytes 24580
  33.5 7.8 %copy-start.11 = (f32[2048]{0:T(1024)S(1)}, f32[2048]{0:T(1024)}, u32[]{:S(2)}) copy-start(f32[2048]{0:T(1024)} %param.17) | copy-start | bytes 24580
  40.0 4.7 %copy-start.1 = (bf16[4,32,2048]{2,1,0:T(8,128)(2,1)S(1)}, bf16[4,32,2048]{2,1,0:T(8,128)(2,1)}, u32[]{:S(2)}) copy-start(bf16[4,32,2048]{2,1,0:T(8,128)(2,1)} %param.15) | copy-start | bytes 1572868
  40.0 12.4 %copy-start.4 = (f32[2048]{0:T(1024)S(1)}, f32[2048]{0:T(1024)}, u32[]{:S(2)}) copy-start(f32[2048]{0:T(1024)} %param.21) | copy-start | bytes 24580
  45.1 1.3 %collective-permute-start.8 = (f32[4,4096]{1,0:T(4,128)S(1)}, f32[4,4096]{1,0:T(4,128)S(1)}, u32[]{:S(2)}, u32[]{:S(2)}) collective-permute-start(f32[4,4096]{1,0:T(4,128)S(1)} %reshape.69), channel_id=1, source_target_pairs={{0,1},{1,0},{2,3},{3,2},{4,5},{5,4},{6,7},{7,6},{8,9},{9,8},{10,11... | collective-permute-start | bytes 196616 | tf_op jit(solution)/shard_map/ppermute | solution.py:17
  46.4 4.3 %collective-permute-start.9 = (f32[3,4096]{1,0:T(4,128)S(1)}, f32[3,4096]{1,0:T(4,128)S(1)}, u32[]{:S(2)}, u32[]{:S(2)}) collective-permute-start(f32[3,4096]{1,0:T(4,128)S(1)} %slice_add_fusion), channel_id=1, source_target_pairs={{0,2},{1,3},{2,0},{3,1},{4,6},{5,7},{6,4},{7,5},{8,10},{9,11},{10,... | collective-permute-start | bytes 147464 | tf_op jit(solution)/shard_map/ppermute | solution.py:17
  50.8 4.0 %collective-permute-start.10 = (f32[2,4096]{1,0:T(2,128)S(1)}, f32[2,4096]{1,0:T(2,128)S(1)}, u32[]{:S(2)}, u32[]{:S(2)}) collective-permute-start(f32[2,4096]{1,0:T(2,128)S(1)} %slice_add_fusion.2), channel_id=1, source_target_pairs={{0,4},{1,5},{2,6},{3,7},{4,0},{5,1},{6,2},{7,3},{8,12},{9,13},{10,... | collective-permute-start | bytes 98312 | tf_op jit(solution)/shard_map/ppermute | solution.py:17
  54.8 4.7 %collective-permute-start.11 = (bf16[1,4096]{1,0:T(2,128)(2,1)S(1)}, bf16[1,4096]{1,0:T(2,128)(2,1)S(1)}, u32[]{:S(2)}, u32[]{:S(2)}) collective-permute-start(bf16[1,4096]{1,0:T(2,128)(2,1)S(1)} %get-tuple-element.19), channel_id=1, source_target_pairs={{0,8},{1,9},{2,10},{3,11},{4,12},{5,13},{6,14},{7,15},{8,0},{9,1},... | collective-permute-start | bytes 24584 | tf_op jit(solution)/shard_map/ppermute | solution.py:17
  57.0 3.4 %collective-permute-start.7 = (bf16[768,128]{0,1:T(8,128)(2,1)S(1)}, bf16[768,128]{0,1:T(8,128)(2,1)S(1)}, u32[]{:S(2)}, u32[]{:S(2)}) collective-permute-start(bf16[768,128]{0,1:T(8,128)(2,1)S(1)} %get-tuple-element.15), channel_id=1, source_target_pairs={{1,0},{2,1},{3,2},{4,3},{5,4},{6,5},{7,6},{8,7},{9,8},{10,9},{11,1... | collective-permute-start | bytes 589832 | tf_op jit(solution)/shard_map/ppermute | solution.py:29
  57.0 8.0 %collective-permute-start.6 = (bf16[768,128]{0,1:T(8,128)(2,1)S(1)}, bf16[768,128]{0,1:T(8,128)(2,1)S(1)}, u32[]{:S(2)}, u32[]{:S(2)}) collective-permute-start(bf16[768,128]{0,1:T(8,128)(2,1)S(1)} %get-tuple-element.14), channel_id=1, source_target_pairs={{0,1},{1,2},{2,3},{3,4},{4,5},{5,6},{6,7},{7,8},{8,9},{9,10},{10,1... | collective-permute-start | bytes 589832 | tf_op jit(solution)/shard_map/ppermute | solution.py:27
  73.8 7.8 %copy-start.2 = (bf16[128,128]{1,0:T(8,128)(2,1)S(1)}, bf16[128,128]{1,0:T(8,128)(2,1)}, u32[]{:S(2)}) copy-start(bf16[128,128]{1,0:T(8,128)(2,1)} %convert_element_type.29) | copy-start | bytes 98308
  73.8 7.8 %copy-start.6 = (f32[2048]{0:T(1024)S(1)}, f32[2048]{0:T(1024)}, u32[]{:S(2)}) copy-start(f32[2048]{0:T(1024)} %param.19) | copy-start | bytes 24580
  73.8 7.8 %copy-start.8 = (f32[2048]{0:T(1024)S(1)}, f32[2048]{0:T(1024)}, u32[]{:S(2)}) copy-start(f32[2048]{0:T(1024)} %param.20) | copy-start | bytes 24580
  73.8 7.8 %copy-start.10 = (f32[2048]{0:T(1024)S(1)}, f32[2048]{0:T(1024)}, u32[]{:S(2)}) copy-start(f32[2048]{0:T(1024)} %param.18) | copy-start | bytes 24580
  73.8 7.8 %copy-start.12 = (f32[2048]{0:T(1024)S(1)}, f32[2048]{0:T(1024)}, u32[]{:S(2)}) copy-start(f32[2048]{0:T(1024)} %param.17) | copy-start | bytes 24580
where the time goes:
time: 121 us
  blocking collectives  30.1 us (25%)
  local copies, waits for them, and re-layouts  29.6 us (24%)
  matrix products  22.2 us (18%)
  waiting for transfers between devices  18.8 us (16%)
  starting transfers between devices  16.2 us (13%)
  other arithmetic  3.17 us (3%)
    psum x1, blocking collectives, on_device(): totals, area_total = lax.psum((area_terms, jnp.sum(triangle_area)), 'patch')  30.1 us
    gather x2, local copies, waits for them, and re-layouts, section_rates(): chosen = column_blocks[position]  16.1 us
    ppermute x8, waiting for transfers between devices, partner_2(): return lax.ppermute(value, axis, pairs)  14 us
    dot_general x2, matrix products, section_rates(): jnp.einsum('rkij,rkjb->rib', near_blocks, chosen, preferred_element_type=...  12.9 us
    ppermute x8, starting transfers between devices, partner_2(): return lax.ppermute(value, axis, pairs)  9.9 us
    unnamed x30, local copies, waits for them, and re-layouts  8.04 us
    dot_general x2, matrix products, section_rates(): lax.dot_general(coupling, coupled, (((0,), (0,)), ((), ())), preferred_el...  7.7 us
    ppermute x2, starting transfers between devices, padded(): lax.ppermute(head, axis, [((i + 1) % count, i) for i in range(count)])  5.77 us
  transfers between devices with their start and end apart: 12, of which 8 were waited for; matrix products, arithmetic and copies ran while one was open for 5% of the time, Pallas kernels for 0%

commit v1 on v0

v1 whole, which is shorter than its diff:
```python
import functools

import jax
import jax.numpy as jnp
from jax import lax
from jax.experimental import pallas as pl
from jax.experimental.pallas import tpu as pltpu
from jax.sharding import PartitionSpec as P

REACH = 6

step_size = 0.1
damping = 0.5
error_scale = 0.01
half_step = 0.5 * step_size

AXIS = "patch"
F32 = jnp.float32
BF16 = jnp.bfloat16
WHOLE = pl.BlockSpec(memory_space=pltpu.VMEM)
SCALARS = pl.BlockSpec(memory_space=pltpu.SMEM)


def on_chip(*shapes):
    return tuple(pltpu.VMEM(shape, dtype) for shape, dtype in shapes)


def params(limit_mib):
    return pltpu.CompilerParams(vmem_limit_bytes=limit_mib * 1024 * 1024)


def cost(flops, moved, exps=0):
    return pl.CostEstimate(flops=flops, bytes_accessed=moved, transcendentals=exps)


def send_out(me, x, projected, slots, side_a, side_b):
    row_blocks = x.shape[0] - 1
    devices, rank, _ = slots.shape
    odd = lax.rem(me, 2)
    start_a = (1 - odd) * (row_blocks - REACH)
    start_b = odd * (row_blocks - REACH)
    for t in range(REACH):
        side_a[t] = x[start_a + t]
        side_b[t] = x[start_b + t]
    for m in range(devices):
        level = max(m.bit_length() - 1, 0)
        slots[me ^ m] = projected[level * rank : (level + 1) * rank].astype(slots.dtype)


def open_kernel(me_ref, p_ref, basis_ref, x, slots, side_a, side_b):
    row_blocks, size, cols = p_ref.shape
    group = 2 if row_blocks % 2 == 0 else 1
    projected = jnp.zeros((basis_ref.shape[0], cols), F32)
    for r in range(0, row_blocks, group):
        rates = jnp.exp(p_ref[r : r + group]).astype(BF16)
        x[r : r + group] = rates
        projected += jnp.dot(
            basis_ref[:, r * size : (r + group) * size],
            rates.reshape(group * size, cols),
            preferred_element_type=F32,
        )
    x[row_blocks] = jnp.zeros((size, cols), BF16)
    send_out(me_ref[0], x, projected, slots, side_a, side_b)


def local_products(me_ref, columns, x, near, acc, place=None):
    row_blocks, near_count, size, _ = near.shape
    total = row_blocks * me_ref[1]
    first = row_blocks * me_ref[0]

    def row(r, carry):
        picked = []
        for k in range(near_count):
            offset = columns[r, k] - first - r
            offset = jnp.where(offset > REACH, offset - total, offset)
            offset = jnp.where(offset < -REACH, offset + total, offset)
            if place is not None:
                place[r, offset + REACH] = k
            index = r + offset
            inside = jnp.logical_and(index >= 0, index < row_blocks)
            picked.append(x[jnp.where(inside, index, row_blocks)])
        left = jnp.concatenate([near[r, k] for k in range(near_count)], axis=1)
        acc[r] = jnp.dot(left, jnp.concatenate(picked, axis=0), preferred_element_type=F32)
        return carry

    lax.fori_loop(0, row_blocks, row, 0)


def local_kernel(me_ref, columns, x, near, acc):
    local_products(me_ref, columns, x, near, acc)


def edge_rows(row_blocks):
    left = [(r, r) for r in range(min(REACH, row_blocks))]
    right = [(r, r + REACH + 1 - row_blocks) for r in range(max(row_blocks - REACH, 0), row_blocks)]
    return left, right


def first_local_kernel(
    me_ref, columns, x, near, coupling, stiff, plate, direct, evolve, area,
    acc, left_near, right_near, coupling_t, per_row, place,
):
    row_blocks, near_count, size, _ = near.shape
    for r in range(row_blocks):
        for o in range(2 * REACH + 1):
            place[r, o] = -1
    local_products(me_ref, columns, x, near, acc, place)
    left, right = edge_rows(row_blocks)

    def halo_block(r, offset):
        k = place[r, offset + REACH]
        block = near[r, jnp.maximum(k, 0)]
        return jnp.where(k >= 0, block, jnp.zeros_like(block))

    for n, (r, low) in enumerate(left):
        for t in range(low, REACH):
            left_near[n, :, t * size : (t + 1) * size] = halo_block(r, t - REACH - r)
    for n, (r, count) in enumerate(right):
        for t in range(count):
            right_near[n, :, t * size : (t + 1) * size] = halo_block(r, row_blocks + t - r)
    for r in range(row_blocks):
        rows = slice(r * size, (r + 1) * size)
        coupling_t[r] = coupling[:, rows].T
        stacked = jnp.concatenate(
            [v[r : r + 1] for v in (stiff, plate, direct, evolve, area, area, area, area)], axis=0
        )
        per_row[r] = stacked.T


def add_halo(me, got_a, got_b, halo, left_near, right_near, acc):
    row_blocks, size, cols = acc.shape
    odd = lax.rem(me, 2)
    at_a = (1 - odd) * REACH
    at_b = odd * REACH
    for t in range(REACH):
        halo[at_a + t] = got_a[t]
        halo[at_b + t] = got_b[t]
    left, right = edge_rows(row_blocks)
    for n, (r, low) in enumerate(left):
        blocks = halo[low:REACH].reshape((REACH - low) * size, cols)
        acc[r] += jnp.dot(left_near[n, :, low * size :], blocks, preferred_element_type=F32)
    for n, (r, count) in enumerate(right):
        blocks = halo[REACH : REACH + count].reshape(count * size, cols)
        acc[r] += jnp.dot(right_near[n, :, : count * size], blocks, preferred_element_type=F32)


def couple(me, got, levels):
    devices = got.shape[0]
    sums = []
    for level in range(levels):
        total = got[me ^ (1 << level)].astype(F32)
        for m in range((1 << level) + 1, min(2 << level, devices)):
            total += got[me ^ m].astype(F32)
        sums.append(total.astype(BF16))
    return jnp.concatenate(sums, axis=0)


def rates_of(p, s, near_far, rows):
    stiff, plate, direct, evolve = (rows[:, q : q + 1] for q in range(4))
    velocity = jnp.exp(p)
    stress = stiff * (plate - velocity) - near_far
    state = jnp.exp(-s) - velocity
    return (stress - evolve * state) / (direct + damping * velocity), state


def middle_kernel(
    me_ref, acc_in, got_a, got_b, got, left_near, right_near, coupling_t, per_row, p_ref, s_ref, basis_ref,
    rate_one, state_one, x, slots, side_a, side_b, halo, acc, proj, coupled,
):
    row_blocks, size, cols = p_ref.shape
    me = me_ref[0]
    levels = basis_ref.shape[0] // got.shape[1]
    acc[...] = acc_in[...]
    add_halo(me, got_a, got_b, halo, left_near, right_near, acc)
    coupled[...] = couple(me, got, levels)

    def row(r, carry):
        p, s = p_ref[r], s_ref[r]
        near_far = acc[r] + jnp.dot(coupling_t[r], coupled[...], preferred_element_type=F32)
        rate, state = rates_of(p, s, near_far, per_row[r])
        rate_one[r] = rate
        state_one[r] = state
        x[r] = jnp.exp(p + step_size * rate).astype(BF16)
        return carry

    lax.fori_loop(0, row_blocks, row, 0)
    x[row_blocks] = jnp.zeros((size, cols), BF16)
    projected = jnp.zeros((basis_ref.shape[0], cols), F32)
    group = 2 if row_blocks % 2 == 0 else 1
    for r in range(0, row_blocks, group):
        projected += jnp.dot(
            basis_ref[:, r * size : (r + group) * size],
            x[r : r + group].reshape(group * size, cols),
            preferred_element_type=F32,
        )
    send_out(me, x, projected, slots, side_a, side_b)


def close_kernel(
    me_ref, acc_in, got_a, got_b, got, left_near, right_near, coupling_t, per_row, p_ref, s_ref, rate_one, state_one,
    new_p, new_s, parts, halo, acc, coupled,
):
    row_blocks, size, cols = p_ref.shape
    me = me_ref[0]
    levels = coupling_t.shape[2] // got.shape[1]
    acc[...] = acc_in[...]
    add_halo(me, got_a, got_b, halo, left_near, right_near, acc)
    coupled[...] = couple(me, got, levels)

    def row(r, carry):
        errors, areas = carry
        p, s = p_ref[r], s_ref[r]
        rate_a, state_a = rate_one[r], state_one[r]
        rows = per_row[r]
        near_far = acc[r] + jnp.dot(coupling_t[r], coupled[...], preferred_element_type=F32)
        rate_b, state_b = rates_of(p + step_size * rate_a, s + step_size * state_a, near_far, rows)
        new_p[r] = p + half_step * (rate_a + rate_b)
        new_s[r] = s + half_step * (state_a + state_b)
        rate_error = half_step * (rate_b - rate_a) / error_scale
        state_error = half_step * (state_b - state_a) / error_scale
        area = jnp.broadcast_to(rows[:, 4:5], (size, cols))
        weighted = area * (rate_error * rate_error + state_error * state_error)
        errors += jnp.sum(weighted.reshape(size // 8, 8, cols), axis=0)
        areas += jnp.sum(area.reshape(size // 8, 8, cols), axis=0)
        return errors, areas

    zero = jnp.zeros((8, cols), F32)
    errors, areas = lax.fori_loop(0, row_blocks, row, (zero, zero))
    both = jnp.concatenate(
        [jnp.sum(errors, axis=0, keepdims=True), jnp.sum(areas, axis=0, keepdims=True)], axis=0
    )
    for j in range(parts.shape[0]):
        parts[j] = both


def exchange(x, side_a, side_b, slots):
    count = lax.axis_size(AXIS)
    got_a = lax.ppermute(side_a, AXIS, [(i, i ^ 1) for i in range(count)])
    pairs = [(i, (i - 1) % count if i % 2 == 0 else (i + 1) % count) for i in range(count)]
    got_b = lax.ppermute(side_b, AXIS, pairs)
    got = lax.all_to_all(slots, AXIS, 0, 0)
    return got_a, got_b, got


def on_device(
    log_rate,
    log_state,
    near_blocks,
    near_columns,
    far_basis,
    far_coupling,
    self_stiffness,
    plate_rate,
    direct_effect,
    evolution_effect,
    triangle_area,
):
    rows, cols = log_rate.shape
    row_blocks, near_count, size, _ = near_blocks.shape
    levels, rank, _ = far_basis.shape
    devices = lax.axis_size(AXIS)
    me = jnp.stack([lax.axis_index(AXIS), jnp.int32(devices)]).astype(jnp.int32)
    p = log_rate.reshape(row_blocks, size, cols)
    s = log_state.reshape(row_blocks, size, cols)
    basis = far_basis.reshape(levels * rank, rows)
    coupling = far_coupling.reshape(levels * rank, rows)
    vectors = [
        v.reshape(row_blocks, size)
        for v in (self_stiffness, plate_rate, direct_effect, evolution_effect, triangle_area)
    ]
    state = (row_blocks, size, cols)
    outgoing = (
        ((row_blocks + 1, size, cols), BF16),
        ((devices, rank, cols), BF16),
        ((REACH, size, cols), BF16),
        ((REACH, size, cols), BF16),
    )
    near_flops = 2 * rows * near_count * size * cols

    x, slots, side_a, side_b = pl.pallas_call(
        open_kernel,
        out_shape=on_chip(*outgoing),
        in_specs=[SCALARS, WHOLE, WHOLE],
        out_specs=(WHOLE,) * 4,
        compiler_params=params(16),
        name="open",
    )(me, p, basis)

    got_a, got_b, got = exchange(x, side_a, side_b, slots)
    acc, left_near, right_near, coupling_t, per_row = pl.pallas_call(
        first_local_kernel,
        out_shape=on_chip(
            (state, F32),
            ((min(REACH, row_blocks), size, REACH * size), BF16),
            ((min(REACH, row_blocks), size, REACH * size), BF16),
            ((row_blocks, size, levels * rank), BF16),
            ((row_blocks, size, 8), F32),
        ),
        in_specs=[SCALARS, SCALARS] + [WHOLE] * 8,
        out_specs=(WHOLE,) * 5,
        scratch_shapes=[pltpu.SMEM((row_blocks, 2 * REACH + 1), jnp.int32)],
        compiler_params=params(16),
        cost_estimate=cost(near_flops, near_blocks.size * 2),
        name="local_one",
    )(me, near_columns, x, near_blocks, coupling, *vectors)

    rate_one, state_one, x, slots, side_a, side_b = pl.pallas_call(
        middle_kernel,
        out_shape=on_chip((state, F32), (state, F32), *outgoing),
        in_specs=[SCALARS] + [WHOLE] * 11,
        out_specs=(WHOLE,) * 6,
        scratch_shapes=[
            pltpu.VMEM((2 * REACH, size, cols), BF16),
            pltpu.VMEM(state, F32),
            pltpu.VMEM((levels * rank, cols), F32),
            pltpu.VMEM((levels * rank, cols), BF16),
        ],
        compiler_params=params(16),
        name="middle",
    )(me, acc, got_a, got_b, got, left_near, right_near, coupling_t, per_row, p, s, basis)

    got_a, got_b, got = exchange(x, side_a, side_b, slots)
    acc = pl.pallas_call(
        local_kernel,
        out_shape=on_chip((state, F32))[0],
        in_specs=[SCALARS, SCALARS, WHOLE, WHOLE],
        out_specs=WHOLE,
        compiler_params=params(16),
        cost_estimate=cost(near_flops, near_blocks.size * 2),
        name="local_two",
    )(me, near_columns, x, near_blocks)

    new_p, new_s, parts = pl.pallas_call(
        close_kernel,
        out_shape=on_chip((state, F32), (state, F32), ((devices, 2, cols), F32)),
        in_specs=[SCALARS] + [WHOLE] * 12,
        out_specs=(WHOLE,) * 3,
        scratch_shapes=[
            pltpu.VMEM((2 * REACH, size, cols), BF16),
            pltpu.VMEM(state, F32),
            pltpu.VMEM((levels * rank, cols), BF16),
        ],
        compiler_params=params(16),
        name="close",
    )(me, acc, got_a, got_b, got, left_near, right_near, coupling_t, per_row, p, s, rate_one, state_one)

    totals = lax.all_to_all(parts, AXIS, 0, 0).sum(axis=0)
    error_norm = jnp.sqrt(totals[0] / totals[1] + 1e-06)
    return new_p.reshape(rows, cols), new_s.reshape(rows, cols), error_norm


def solution(mesh):
    split = P(("member", "patch"))
    in_specs = (
        P(("member", "patch"), None),
        P(("member", "patch"), None),
        P(("member", "patch"), None, None, None),
        P(("member", "patch"), None),
        P("member", None, "patch"),
        P("member", None, "patch"),
        split,
        split,
        split,
        split,
        split,
    )
    out_specs = (P(("member", "patch"), None), P(("member", "patch"), None), P("member"))
    return jax.shard_map(
        on_device, mesh=mesh, in_specs=in_specs, out_specs=out_specs, check_vma=False
    )
```

time: 121 us -> 93.2 us (0.77); the launches traced: 121 us -> 92 us
  blocking collectives: 30.1 us -> 0 us
  Pallas kernels: 0 us -> 22.4 us
  matrix products: 22.2 us -> 0 us
  waiting for transfers between devices: 18.8 us -> 4.54 us
  local copies, waits for them, and re-layouts: 29.6 us -> 39.8 us
  starting transfers between devices: 16.2 us -> 23.8 us
  other arithmetic: 3.17 us -> 0.63 us
    unnamed x30 -> x84, local copies, waits for them, and re-layouts: 8.04 us -> 39.8 us
    psum x1 -> x0, blocking collectives: 30.1 us -> none  [on_device(): totals, area_total = lax.psum((area_terms, jnp.sum(triangle_area)), 'patch')]
    pallas_call x0 -> x5, Pallas kernels: none -> 22.4 us  [the longest x1 6.17 us: on_device(): pl.pallas_call(first_local_kernel, out_shape=on_chip((state, F32), ((min(...]
    dot_general x6 -> x0, matrix products: 22.2 us -> none  [the longest x2 12.9 us: section_rates(): jnp.einsum('rkij,rkjb->rib', near_blocks, chosen, preferred_element_type=...]
    ppermute x12 -> x4, waiting for transfers between devices: 18.8 us -> 0.01 us  [the longest x2 0.01 us: exchange(): got_a = lax.ppermute(side_a, AXIS, [(i, i ^ 1) for i in range(count)])]
    gather x2 -> x0, local copies, waits for them, and re-layouts: 16.1 us -> none  [section_rates(): chosen = column_blocks[position]]
    all_to_all x0 -> x3, starting transfers between devices: none -> 14.4 us  [the longest x2 10.9 us: exchange(): got = lax.all_to_all(slots, AXIS, 0, 0)]
    ppermute x12 -> x4, starting transfers between devices: 16.2 us -> 9.45 us  [the longest x2 8.75 us: exchange(): got_b = lax.ppermute(side_b, AXIS, pairs)]
  transfers between devices with their start and end apart: 12 -> 7, of which waited for: 8 -> 1; matrix products, arithmetic and copies ran while one was open for 5% -> 2% of each run, Pallas kernels for 0% -> 12%
where the time goes in v1:
time: 93.2 us; the launch traced here: 92 us
  local copies, waits for them, and re-layouts  39.8 us (43%)
  starting transfers between devices  23.8 us (26%)
  Pallas kernels  22.4 us (24%)
  waiting for transfers between devices  4.54 us (5%)
    unnamed x84, local copies, waits for them, and re-layouts  39.8 us
    all_to_all x2, starting transfers between devices, exchange(): got = lax.all_to_all(slots, AXIS, 0, 0)  10.9 us
    ppermute x2, starting transfers between devices, exchange(): got_b = lax.ppermute(side_b, AXIS, pairs)  8.75 us
    pallas_call x1, Pallas kernels, on_device(): pl.pallas_call(first_local_kernel, out_shape=on_chip((state, F32), ((min(...  6.17 us
    pallas_call x1, Pallas kernels, on_device(): pl.pallas_call(local_kernel, out_shape=on_chip((state, F32))[0], in_specs...  5.04 us
    pallas_call x1, Pallas kernels, on_device(): pl.pallas_call(middle_kernel, out_shape=on_chip((state, F32), (state, F32...  4.81 us
    pallas_call x1, Pallas kernels, on_device(): pl.pallas_call(close_kernel, out_shape=on_chip((state, F32), (state, F32)...  4.79 us
    all_to_all x1, waiting for transfers between devices, on_device(): totals = lax.all_to_all(parts, AXIS, 0, 0).sum(axis=0)  4.52 us
  transfers between devices with their start and end apart: 7, of which 1 were waited for; matrix products, arithmetic and copies ran while one was open for 2% of the time, Pallas kernels for 12%

profile of v1, /device:TPU:0, one launch (start us, length us, event | category | flops | bytes accessed | tf_op | source)
XLA Modules:
  0.0 92.0 jit_solution(1229451577389579784)
XLA Ops:
  0.7 1.2 %copy-done.2 = f32[2048,128]{1,0:T(8,128)S(1)} copy-done((f32[2048,128]{1,0:T(8,128)S(1)}, f32[2048,128]{1,0:T(8,128)}, u32[]{:S(2)}) %copy-start.2) | copy-done | bytes 1048600
  1.9 1.0 %copy-done.18 = bf16[4,32,2048]{2,1,0:T(8,128)(2,1)S(1)} copy-done((bf16[4,32,2048]{2,1,0:T(8,128)(2,1)S(1)}, bf16[4,32,2048]{2,1,0:T(8,128)(2,1)}, u32[]{:S(2)}) %copy-start.18) | copy-done | bytes 524312
  3.0 1.6 %open.1 = (bf16[17,128,128]{2,1,0:T(8,128)(2,1)S(1)}, bf16[16,32,128]{2,1,0:T(8,128)(2,1)}, bf16[6,128,128]{2,1,0:T(8,128)(2,1)}, bf16[6,128,128]{2,1,0:T(8,128)(2,1)}) custom-call(s32[2]{0:T(128)S(1)} %pad_add_fusion.me_ref, f32[16,128,128]{2,1,0:T(8,128)S(1)} %bitcast.16, bf16[128,2048]{1,0:T(8,128)(2,1)S(1)} %bitcast.21), custom_call_target="tpu_custom_call" | custom-call | tf_op jit(solution)/shard_map/open/pallas_call | solution.py:280
  5.5 7.4 %all-to-all-start = ((bf16[16,32,128]{2,1,0:T(8,128)(2,1)}), bf16[16,32,128]{2,1,0:T(8,128)(2,1)S(1)}, u32[]{:S(2)}, u32[]{:S(2)}) async-start(bf16[16,32,128]{2,1,0:T(8,128)(2,1)} %get-tuple-element.25), calls=%async_computation | async-start | bytes 262144 | tf_op jit(solution)/shard_map/all_to_all | solution.py:241
  13.3 4.3 %collective-permute-start.1 = (bf16[6,128,128]{2,1,0:T(8,128)(2,1)}, bf16[6,128,128]{2,1,0:T(8,128)(2,1)S(1)}, u32[]{:S(2)}, u32[]{:S(2)}) collective-permute-start(bf16[6,128,128]{2,1,0:T(8,128)(2,1)} %get-tuple-element.24), channel_id=1, source_target_pairs={{0,15},{1,2},{2,1},{3,4},{4,3},{5,6},{6,5},{7,8},{8,7},{9,10},{10,... | collective-permute-start | bytes 589832 | tf_op jit(solution)/shard_map/ppermute | solution.py:240
  17.7 2.8 %copy-done = bf16[16,12,128,128]{3,2,1,0:T(8,128)(2,1)S(1)} copy-done((bf16[16,12,128,128]{3,2,1,0:T(8,128)(2,1)S(1)}, bf16[16,12,128,128]{3,2,1,0:T(8,128)(2,1)}, u32[]{:S(2)}) %copy-start) | copy-done | bytes 6291480
  20.4 1.1 %copy-done.29 = bf16[17,128,128]{2,1,0:T(8,128)(2,1)S(1)} copy-done((bf16[17,128,128]{2,1,0:T(8,128)(2,1)S(1)}, bf16[17,128,128]{2,1,0:T(8,128)(2,1)}, u32[]{:S(2)}) %copy-start.29) | copy-done | bytes 557080
  21.5 1.0 %copy-done.30 = bf16[4,32,2048]{2,1,0:T(8,128)(2,1)S(1)} copy-done((bf16[4,32,2048]{2,1,0:T(8,128)(2,1)S(1)}, bf16[4,32,2048]{2,1,0:T(8,128)(2,1)}, u32[]{:S(2)}) %copy-start.30) | copy-done | bytes 524312
  22.5 6.2 %local_one.1 = (f32[16,128,128]{2,1,0:T(8,128)S(1)}, bf16[6,128,768]{2,1,0:T(8,128)(2,1)S(1)}, bf16[6,128,768]{2,1,0:T(8,128)(2,1)S(1)}, bf16[16,128,128]{2,1,0:T(8,128)(2,1)S(1)}, f32[16,128,8]{2,1,0:T(8,128)S(1)}) custom-call(s32[2]{0:T(128)S(1)} %pad_add_fusion.me_ref, s32[16,12]{1,0:T(8,128)S(1)} %copy-done.33, bf16[17,128,128]{2,1,0:T(8,128)(2,1)S(1)} %copy-done.29, ...), custom_call_target="tpu_custom_call" | custom-call | flops 805306368 | bytes 6291456 | tf_op jit(solution)/shard_map/local_one/pallas_call | solution.py:290
  28.7 1.0 %copy-done.6 = bf16[6,128,768]{2,1,0:T(8,128)(2,1)} copy-done((bf16[6,128,768]{2,1,0:T(8,128)(2,1)}, bf16[6,128,768]{2,1,0:T(8,128)(2,1)S(1)}, u32[]{:S(2)}) %copy-start.6) | copy-done | bytes 1179672
  31.8 1.9 %copy-done.7 = bf16[6,128,768]{2,1,0:T(8,128)(2,1)S(1)} copy-done((bf16[6,128,768]{2,1,0:T(8,128)(2,1)S(1)}, bf16[6,128,768]{2,1,0:T(8,128)(2,1)}, u32[]{:S(2)}) %copy-start.7) | copy-done | bytes 1179672
  33.6 1.2 %copy-done.11 = f32[2048,128]{1,0:T(8,128)S(1)} copy-done((f32[2048,128]{1,0:T(8,128)S(1)}, f32[2048,128]{1,0:T(8,128)}, u32[]{:S(2)}) %copy-start.11) | copy-done | bytes 1048600
  34.8 1.2 %copy-done.14 = f32[16,128,8]{2,1,0:T(8,128)S(1)} copy-done((f32[16,128,8]{2,1,0:T(8,128)S(1)}, f32[16,128,8]{2,1,0:T(8,128)}, u32[]{:S(2)}) %copy-start.14) | copy-done | bytes 65560
  36.1 1.0 %copy-done.19 = bf16[4,32,2048]{2,1,0:T(8,128)(2,1)S(1)} copy-done((bf16[4,32,2048]{2,1,0:T(8,128)(2,1)S(1)}, bf16[4,32,2048]{2,1,0:T(8,128)(2,1)}, u32[]{:S(2)}) %copy-start.19) | copy-done | bytes 524312
  37.1 1.2 %copy-done.25 = f32[16,128,128]{2,1,0:T(8,128)S(1)} copy-done((f32[16,128,128]{2,1,0:T(8,128)S(1)}, f32[16,128,128]{2,1,0:T(8,128)}, u32[]{:S(2)}) %copy-start.25) | copy-done | bytes 1048600
  38.3 4.8 %middle.1 = (f32[16,128,128]{2,1,0:T(8,128)S(1)}, f32[16,128,128]{2,1,0:T(8,128)S(1)}, bf16[17,128,128]{2,1,0:T(8,128)(2,1)S(1)}, bf16[16,32,128]{2,1,0:T(8,128)...) custom-call(s32[2]{0:T(128)S(1)} %pad_add_fusion.me_ref, f32[16,128,128]{2,1,0:T(8,128)S(1)} %copy-done.25, ...), custom_call_target="tpu_custom_call" | custom-call | tf_op jit(solution)/shard_map/middle/pallas_call | solution.py:307
  47.3 3.5 %all-to-all-start.1 = ((bf16[16,32,128]{2,1,0:T(8,128)(2,1)}), bf16[16,32,128]{2,1,0:T(8,128)(2,1)S(1)}, u32[]{:S(2)}, u32[]{:S(2)}) async-start(bf16[16,32,128]{2,1,0:T(8,128)(2,1)} %get-tuple-element.33), calls=%async_computation.1 | async-start | bytes 262144 | tf_op jit(solution)/shard_map/all_to_all | solution.py:241
  51.1 4.4 %collective-permute-start.3 = (bf16[6,128,128]{2,1,0:T(8,128)(2,1)}, bf16[6,128,128]{2,1,0:T(8,128)(2,1)S(1)}, u32[]{:S(2)}, u32[]{:S(2)}) collective-permute-start(bf16[6,128,128]{2,1,0:T(8,128)(2,1)} %copy-done.39), channel_id=1, source_target_pairs={{0,15},{1,2},{2,1},{3,4},{4,3},{5,6},{6,5},{7,8},{8,7},{9,10},{10,... | collective-permute-start | bytes 589832 | tf_op jit(solution)/shard_map/ppermute | solution.py:240
  55.5 2.8 %copy-done.1 = bf16[16,12,128,128]{3,2,1,0:T(8,128)(2,1)S(1)} copy-done((bf16[16,12,128,128]{3,2,1,0:T(8,128)(2,1)S(1)}, bf16[16,12,128,128]{3,2,1,0:T(8,128)(2,1)}, u32[]{:S(2)}) %copy-start.1) | copy-done | bytes 6291480
  58.3 1.1 %copy-done.27 = bf16[17,128,128]{2,1,0:T(8,128)(2,1)S(1)} copy-done((bf16[17,128,128]{2,1,0:T(8,128)(2,1)S(1)}, bf16[17,128,128]{2,1,0:T(8,128)(2,1)}, u32[]{:S(2)}) %copy-start.27) | copy-done | bytes 557080
  59.4 5.0 %local_two.1.acc_in = f32[16,128,128]{2,1,0:T(8,128)S(1)} custom-call(s32[2]{0:T(128)S(1)} %pad_add_fusion.me_ref, s32[16,12]{1,0:T(8,128)S(1)} %copy-done.33, bf16[17,128,128]{2,1,0:T(8,128)(2,1)S(1)} %copy-done.27, bf16[16,12,128,128]{3,2,1,0:T(8,128)(2,1)S(1)} %copy-done.1), custom_call_target="tpu_custom_call" | custom-call | flops 805306368 | bytes 6291456 | tf_op jit(solution)/shard_map/local_two/pallas_call | solution.py:323
  66.1 1.3 %copy-done.5 = bf16[6,128,768]{2,1,0:T(8,128)(2,1)S(1)} copy-done((bf16[6,128,768]{2,1,0:T(8,128)(2,1)S(1)}, bf16[6,128,768]{2,1,0:T(8,128)(2,1)}, u32[]{:S(2)}) %copy-start.5) | copy-done | bytes 1179672
  67.4 1.3 %copy-done.8 = bf16[6,128,768]{2,1,0:T(8,128)(2,1)S(1)} copy-done((bf16[6,128,768]{2,1,0:T(8,128)(2,1)S(1)}, bf16[6,128,768]{2,1,0:T(8,128)(2,1)}, u32[]{:S(2)}) %copy-start.8) | copy-done | bytes 1179672
  68.6 1.2 %copy-done.10 = f32[16,128,128]{2,1,0:T(8,128)S(1)} copy-done((f32[16,128,128]{2,1,0:T(8,128)S(1)}, f32[16,128,128]{2,1,0:T(8,128)}, u32[]{:S(2)}) %copy-start.10) | copy-done | bytes 1048600
  69.9 1.2 %copy-done.12 = f32[2048,128]{1,0:T(8,128)S(1)} copy-done((f32[2048,128]{1,0:T(8,128)S(1)}, f32[2048,128]{1,0:T(8,128)}, u32[]{:S(2)}) %copy-start.12) | copy-done | bytes 1048600
  71.1 1.2 %copy-done.15 = f32[16,128,8]{2,1,0:T(8,128)S(1)} copy-done((f32[16,128,8]{2,1,0:T(8,128)S(1)}, f32[16,128,8]{2,1,0:T(8,128)}, u32[]{:S(2)}) %copy-start.15) | copy-done | bytes 65560
  72.3 1.0 %copy-done.17 = bf16[16,128,128]{2,1,0:T(8,128)(2,1)S(1)} copy-done((bf16[16,128,128]{2,1,0:T(8,128)(2,1)S(1)}, bf16[16,128,128]{2,1,0:T(8,128)(2,1)}, u32[]{:S(2)}) %copy-start.17) | copy-done | bytes 524312
  73.4 1.2 %copy-done.21 = f32[16,128,128]{2,1,0:T(8,128)S(1)} copy-done((f32[16,128,128]{2,1,0:T(8,128)S(1)}, f32[16,128,128]{2,1,0:T(8,128)}, u32[]{:S(2)}) %copy-start.21) | copy-done | bytes 1048600
  74.6 1.2 %copy-done.23 = f32[16,128,128]{2,1,0:T(8,128)S(1)} copy-done((f32[16,128,128]{2,1,0:T(8,128)S(1)}, f32[16,128,128]{2,1,0:T(8,128)}, u32[]{:S(2)}) %copy-start.23) | copy-done | bytes 1048600
  76.7 4.8 %close.1 = (f32[16,128,128]{2,1,0:T(8,128)S(1)}, f32[16,128,128]{2,1,0:T(8,128)S(1)}, f32[16,2,128]{2,1,0:T(2,128)}) custom-call(s32[2]{0:T(128)S(1)} %pad_add_fusion.me_ref, f32[16,128,128]{2,1,0:T(8,128)S(1)} %copy-done.10, bf16[6,128,128]{2,1,0:T(8,128)(2,1)S(1)} %collective-permute-done.2.got_a, bf16[6,128,128]{2,1,0:T(8,128)(2,1)S(1)} %copy-done.32, ...), custom_call_target="tpu_custom_call" | custom-call | tf_op jit(solution)/shard_map/close/pallas_call | solution.py:333
  81.5 3.5 %all-to-all-start.2 = ((f32[16,2,128]{2,1,0:T(2,128)}), f32[16,2,128]{2,1,0:T(2,128)S(1)}, u32[]{:S(2)}, u32[]{:S(2)}) async-start(f32[16,2,128]{2,1,0:T(2,128)} %get-tuple-element.38), calls=%async_computation.2 | async-start | bytes 32768 | tf_op jit(solution)/shard_map/all_to_all | solution.py:347
  86.9 4.5 %all-to-all-done.2 = f32[16,2,128]{2,1,0:T(2,128)S(1)} async-done(((f32[16,2,128]{2,1,0:T(2,128)}), f32[16,2,128]{2,1,0:T(2,128)S(1)}, u32[]{:S(2)}, u32[]{:S(2)}) %all-to-all-start.2) | async-done | bytes 16416 | tf_op jit(solution)/shard_map/all_to_all | solution.py:347
  (74 shorter events, 12.8 us)
Async XLA Ops:
  0.6 17.0 %copy-start.33 = (s32[16,12]{1,0:T(8,128)S(1)}, s32[16,12]{1,0:T(8,128)}, u32[]{:S(2)}) copy-start(s32[16,12]{1,0:T(8,128)} %columns.3) | copy-start | bytes 2308
  0.7 1.2 %copy-start.2 = (f32[2048,128]{1,0:T(8,128)S(1)}, f32[2048,128]{1,0:T(8,128)}, u32[]{:S(2)}) copy-start(f32[2048,128]{1,0:T(8,128)} %param.11) | copy-start | bytes 3145732
  3.0 14.6 %copy-start.34 = (f32[2048]{0:T(1024)S(1)}, f32[2048]{0:T(1024)}, u32[]{:S(2)}) copy-start(f32[2048]{0:T(1024)} %param.17) | copy-start | bytes 24580
  3.0 14.6 %copy-start.35 = (f32[2048]{0:T(1024)S(1)}, f32[2048]{0:T(1024)}, u32[]{:S(2)}) copy-start(f32[2048]{0:T(1024)} %param.18) | copy-start | bytes 24580
  3.0 14.6 %copy-start.36 = (f32[2048]{0:T(1024)S(1)}, f32[2048]{0:T(1024)}, u32[]{:S(2)}) copy-start(f32[2048]{0:T(1024)} %param.19) | copy-start | bytes 24580
  3.0 14.6 %copy-start.37 = (f32[2048]{0:T(1024)S(1)}, f32[2048]{0:T(1024)}, u32[]{:S(2)}) copy-start(f32[2048]{0:T(1024)} %param.20) | copy-start | bytes 24580
  3.0 14.6 %copy-start.38 = (f32[2048]{0:T(1024)S(1)}, f32[2048]{0:T(1024)}, u32[]{:S(2)}) copy-start(f32[2048]{0:T(1024)} %param.21) | copy-start | bytes 24580
  5.5 26.3 %all-to-all-start = ((bf16[16,32,128]{2,1,0:T(8,128)(2,1)}), bf16[16,32,128]{2,1,0:T(8,128)(2,1)S(1)}, u32[]{:S(2)}, u32[]{:S(2)}) async-start(bf16[16,32,128]{2,1,0:T(8,128)(2,1)} %get-tuple-element.25), calls=%async_computation | async-start | bytes 262144 | tf_op jit(solution)/shard_map/all_to_all | solution.py:241
  12.9 18.8 %collective-permute-start = (bf16[6,128,128]{2,1,0:T(8,128)(2,1)}, bf16[6,128,128]{2,1,0:T(8,128)(2,1)S(1)}, u32[]{:S(2)}, u32[]{:S(2)}) collective-permute-start(bf16[6,128,128]{2,1,0:T(8,128)(2,1)} %get-tuple-element.23), channel_id=1, source_target_pairs={{0,1},{1,0},{2,3},{3,2},{4,5},{5,4},{6,7},{7,6},{8,9},{9,8},{10,11... | collective-permute-start | bytes 589832 | tf_op jit(solution)/shard_map/ppermute | solution.py:238
  13.3 18.4 %collective-permute-start.1 = (bf16[6,128,128]{2,1,0:T(8,128)(2,1)}, bf16[6,128,128]{2,1,0:T(8,128)(2,1)S(1)}, u32[]{:S(2)}, u32[]{:S(2)}) collective-permute-start(bf16[6,128,128]{2,1,0:T(8,128)(2,1)} %get-tuple-element.24), channel_id=1, source_target_pairs={{0,15},{1,2},{2,1},{3,4},{4,3},{5,6},{6,5},{7,8},{8,7},{9,10},{10,... | collective-permute-start | bytes 589832 | tf_op jit(solution)/shard_map/ppermute | solution.py:240
  17.7 2.8 %copy-start = (bf16[16,12,128,128]{3,2,1,0:T(8,128)(2,1)S(1)}, bf16[16,12,128,128]{3,2,1,0:T(8,128)(2,1)}, u32[]{:S(2)}) copy-start(bf16[16,12,128,128]{3,2,1,0:T(8,128)(2,1)} %near.3) | copy-start | bytes 18874372
  20.4 1.1 %copy-start.29 = (bf16[17,128,128]{2,1,0:T(8,128)(2,1)S(1)}, bf16[17,128,128]{2,1,0:T(8,128)(2,1)}, u32[]{:S(2)}) copy-start(bf16[17,128,128]{2,1,0:T(8,128)(2,1)} %copy-done.28) | copy-start | bytes 1671172
  22.5 9.2 %copy-start.3 = (f32[2048,128]{1,0:T(8,128)S(1)}, f32[2048,128]{1,0:T(8,128)}, u32[]{:S(2)}) copy-start(f32[2048,128]{1,0:T(8,128)} %param.11) | copy-start | bytes 3145732
  28.7 1.1 %copy-start.6 = (bf16[6,128,768]{2,1,0:T(8,128)(2,1)}, bf16[6,128,768]{2,1,0:T(8,128)(2,1)S(1)}, u32[]{:S(2)}) copy-start(bf16[6,128,768]{2,1,0:T(8,128)(2,1)S(1)} %get-tuple-element.27.right_near) | copy-start | bytes 3538948
  31.7 11.4 %copy-start.4 = (bf16[6,128,768]{2,1,0:T(8,128)(2,1)}, bf16[6,128,768]{2,1,0:T(8,128)(2,1)S(1)}, u32[]{:S(2)}) copy-start(bf16[6,128,768]{2,1,0:T(8,128)(2,1)S(1)} %get-tuple-element.26.left_near) | copy-start | bytes 3538948
  31.7 11.4 %copy-start.16 = (bf16[16,128,128]{2,1,0:T(8,128)(2,1)}, bf16[16,128,128]{2,1,0:T(8,128)(2,1)S(1)}, u32[]{:S(2)}) copy-start(bf16[16,128,128]{2,1,0:T(8,128)(2,1)S(1)} %get-tuple-element.28.coupling_t) | copy-start | bytes 1572868
  31.7 1.9 %copy-start.7 = (bf16[6,128,768]{2,1,0:T(8,128)(2,1)S(1)}, bf16[6,128,768]{2,1,0:T(8,128)(2,1)}, u32[]{:S(2)}) copy-start(bf16[6,128,768]{2,1,0:T(8,128)(2,1)} %copy-done.6) | copy-start | bytes 3538948
  33.6 1.2 %copy-start.11 = (f32[2048,128]{1,0:T(8,128)S(1)}, f32[2048,128]{1,0:T(8,128)}, u32[]{:S(2)}) copy-start(f32[2048,128]{1,0:T(8,128)} %param.12) | copy-start | bytes 3145732
  34.8 1.2 %copy-start.14 = (f32[16,128,8]{2,1,0:T(8,128)S(1)}, f32[16,128,8]{2,1,0:T(8,128)}, u32[]{:S(2)}) copy-start(f32[16,128,8]{2,1,0:T(8,128)} %copy-done.13) | copy-start | bytes 196612
  37.1 1.2 %copy-start.25 = (f32[16,128,128]{2,1,0:T(8,128)S(1)}, f32[16,128,128]{2,1,0:T(8,128)}, u32[]{:S(2)}) copy-start(f32[16,128,128]{2,1,0:T(8,128)} %copy-done.24) | copy-start | bytes 3145732
  47.3 18.8 %all-to-all-start.1 = ((bf16[16,32,128]{2,1,0:T(8,128)(2,1)}), bf16[16,32,128]{2,1,0:T(8,128)(2,1)S(1)}, u32[]{:S(2)}, u32[]{:S(2)}) async-start(bf16[16,32,128]{2,1,0:T(8,128)(2,1)} %get-tuple-element.33), calls=%async_computation.1 | async-start | bytes 262144 | tf_op jit(solution)/shard_map/all_to_all | solution.py:241
  50.8 14.6 %collective-permute-start.2 = (bf16[6,128,128]{2,1,0:T(8,128)(2,1)}, bf16[6,128,128]{2,1,0:T(8,128)(2,1)S(1)}, u32[]{:S(2)}, u32[]{:S(2)}) collective-permute-start(bf16[6,128,128]{2,1,0:T(8,128)(2,1)} %copy-done.40), channel_id=1, source_target_pairs={{0,1},{1,0},{2,3},{3,2},{4,5},{5,4},{6,7},{7,6},{8,9},{9,8},{10,11... | collective-permute-start | bytes 589832 | tf_op jit(solution)/shard_map/ppermute | solution.py:238
  51.1 14.3 %collective-permute-start.3 = (bf16[6,128,128]{2,1,0:T(8,128)(2,1)}, bf16[6,128,128]{2,1,0:T(8,128)(2,1)S(1)}, u32[]{:S(2)}, u32[]{:S(2)}) collective-permute-start(bf16[6,128,128]{2,1,0:T(8,128)(2,1)} %copy-done.39), channel_id=1, source_target_pairs={{0,15},{1,2},{2,1},{3,4},{4,3},{5,6},{6,5},{7,8},{8,7},{9,10},{10,... | collective-permute-start | bytes 589832 | tf_op jit(solution)/shard_map/ppermute | solution.py:240
  55.5 2.8 %copy-start.1 = (bf16[16,12,128,128]{3,2,1,0:T(8,128)(2,1)S(1)}, bf16[16,12,128,128]{3,2,1,0:T(8,128)(2,1)}, u32[]{:S(2)}) copy-start(bf16[16,12,128,128]{3,2,1,0:T(8,128)(2,1)} %near.3) | copy-start | bytes 18874372
  66.1 1.3 %copy-start.5 = (bf16[6,128,768]{2,1,0:T(8,128)(2,1)S(1)}, bf16[6,128,768]{2,1,0:T(8,128)(2,1)}, u32[]{:S(2)}) copy-start(bf16[6,128,768]{2,1,0:T(8,128)(2,1)} %copy-done.4) | copy-start | bytes 3538948
  67.4 1.3 %copy-start.8 = (bf16[6,128,768]{2,1,0:T(8,128)(2,1)S(1)}, bf16[6,128,768]{2,1,0:T(8,128)(2,1)}, u32[]{:S(2)}) copy-start(bf16[6,128,768]{2,1,0:T(8,128)(2,1)} %copy-done.6) | copy-start | bytes 3538948
  68.6 1.2 %copy-start.10 = (f32[16,128,128]{2,1,0:T(8,128)S(1)}, f32[16,128,128]{2,1,0:T(8,128)}, u32[]{:S(2)}) copy-start(f32[16,128,128]{2,1,0:T(8,128)} %copy-done.9) | copy-start | bytes 3145732
  69.9 1.2 %copy-start.12 = (f32[2048,128]{1,0:T(8,128)S(1)}, f32[2048,128]{1,0:T(8,128)}, u32[]{:S(2)}) copy-start(f32[2048,128]{1,0:T(8,128)} %param.12) | copy-start | bytes 3145732
  71.1 1.2 %copy-start.15 = (f32[16,128,8]{2,1,0:T(8,128)S(1)}, f32[16,128,8]{2,1,0:T(8,128)}, u32[]{:S(2)}) copy-start(f32[16,128,8]{2,1,0:T(8,128)} %copy-done.13) | copy-start | bytes 196612
  73.4 1.2 %copy-start.21 = (f32[16,128,128]{2,1,0:T(8,128)S(1)}, f32[16,128,128]{2,1,0:T(8,128)}, u32[]{:S(2)}) copy-start(f32[16,128,128]{2,1,0:T(8,128)} %copy-done.20) | copy-start | bytes 3145732
  74.6 1.2 %copy-start.23 = (f32[16,128,128]{2,1,0:T(8,128)S(1)}, f32[16,128,128]{2,1,0:T(8,128)}, u32[]{:S(2)}) copy-start(f32[16,128,128]{2,1,0:T(8,128)} %copy-done.22) | copy-start | bytes 3145732
  81.5 9.9 %all-to-all-start.2 = ((f32[16,2,128]{2,1,0:T(2,128)}), f32[16,2,128]{2,1,0:T(2,128)S(1)}, u32[]{:S(2)}, u32[]{:S(2)}) async-start(f32[16,2,128]{2,1,0:T(2,128)} %get-tuple-element.38), calls=%async_computation.2 | async-start | bytes 32768 | tf_op jit(solution)/shard_map/all_to_all | solution.py:347
  (16 other events, 14.7 us)

commit v2 on v0

v2 whole, which is shorter than its diff:
```python
import jax
import jax.numpy as jnp
from jax import lax
from jax.experimental import pallas as pl
from jax.experimental.pallas import tpu as pltpu
from jax.sharding import PartitionSpec as P

REACH = 6

step_size = 0.1
damping = 0.5
error_scale = 0.01
half_step = 0.5 * step_size

AXIS = "patch"
F32 = jnp.float32
BF16 = jnp.bfloat16
PLAIN = pl.BlockSpec(memory_space=pltpu.HBM)
LOOSE = pl.BlockSpec(memory_space=pl.ANY)
WHOLE = pl.BlockSpec(memory_space=pltpu.VMEM)
SCALARS = pl.BlockSpec(memory_space=pltpu.SMEM)
SEMS = pltpu.SemaphoreType.DMA


def cost(flops, moved, exps=0):
    return pl.CostEstimate(flops=flops, bytes_accessed=moved, transcendentals=exps)


def like(*shapes):
    return tuple(jax.ShapeDtypeStruct(shape, dtype) for shape, dtype in shapes)


def part(src, dst, sems, c, group):
    at = pl.ds(c * group, group)
    return pltpu.make_async_copy(src.at[at], dst.at[at], sems.at[c])


def edge_rows(row_blocks):
    left = [(r, r) for r in range(min(REACH, row_blocks))]
    right = [(r, r + REACH + 1 - row_blocks) for r in range(max(row_blocks - REACH, 0), row_blocks)]
    return left, right


def edge_list(row_blocks):
    left, right = edge_rows(row_blocks)
    return (
        [(r, t - REACH - r) for r, low in left for t in range(low, REACH)],
        [(r, row_blocks + t - r) for r, count in right for t in range(count)],
    )


def fill_slots(me, projected, slots):
    devices, rank, _ = slots.shape
    for m in range(devices):
        level = max(m.bit_length() - 1, 0)
        slots[me ^ m] = projected[level * rank : (level + 1) * rank].astype(slots.dtype)


def send_copies(me, x, slots, side_a, side_b, slots_out, a_out, b_out, sems):
    row_blocks = x.shape[0] - 1
    odd = lax.rem(me, 2)
    start_a = (1 - odd) * (row_blocks - REACH)
    start_b = odd * (row_blocks - REACH)
    return [
        pltpu.make_async_copy(slots, slots_out, sems.at[0]),
        pltpu.make_async_copy(x.at[pl.ds(start_a, REACH)], a_out, sems.at[1]),
        pltpu.make_async_copy(x.at[pl.ds(start_b, REACH)], b_out, sems.at[2]),
    ]


def open_kernel(
    me_ref, p_in, basis_in, x_out, slots_out, a_out, b_out,
    p, basis, x, slots, p_sems, x_sems, basis_sem, send_sems,
):
    row_blocks, size, cols = p.shape
    chunks = p_sems.shape[0]
    group = row_blocks // chunks
    me = me_ref[0]
    for c in range(chunks):
        part(p_in, p, p_sems, c, group).start()
        if c == 0:
            pltpu.make_async_copy(basis_in, basis, basis_sem).start()
    projected = jnp.zeros((basis.shape[0], cols), F32)
    for c in range(chunks):
        part(p_in, p, p_sems, c, group).wait()
        rows = slice(c * group, (c + 1) * group)
        rates = jnp.exp(p[rows]).astype(BF16)
        x[rows] = rates
        if c == 0:
            pltpu.make_async_copy(basis_in, basis, basis_sem).wait()
        projected += jnp.dot(
            basis[:, c * group * size : (c + 1) * group * size],
            rates.reshape(group * size, cols),
            preferred_element_type=F32,
        )
    x[row_blocks] = jnp.zeros((size, cols), BF16)
    fill_slots(me, projected, slots)
    copies = send_copies(me, x, slots, None, None, slots_out, a_out, b_out, send_sems)
    copies.append(pltpu.make_async_copy(x, x_out, x_sems))
    for copy in copies:
        copy.start()
    for copy in copies:
        copy.wait()


def column_blocks(me_ref, columns, x, r, near_count, row_blocks, place=None):
    total = row_blocks * me_ref[1]
    first = row_blocks * me_ref[0]
    picked = []
    for k in range(near_count):
        offset = columns[r, k] - first - r
        offset = jnp.where(offset > REACH, offset - total, offset)
        offset = jnp.where(offset < -REACH, offset + total, offset)
        if place is not None:
            place[r, offset + REACH] = k
        index = r + offset
        inside = jnp.logical_and(index >= 0, index < row_blocks)
        picked.append(x[jnp.where(inside, index, row_blocks)])
    return jnp.concatenate(picked, axis=0)


def near_product(me_ref, columns, x, near, r, place=None):
    row_blocks, near_count, size, _ = near.shape
    left = jnp.concatenate([near[r, k] for k in range(near_count)], axis=1)
    right = column_blocks(me_ref, columns, x, r, near_count, row_blocks, place)
    return jnp.dot(left, right, preferred_element_type=F32)


def per_row(vectors, r):
    rows = [v[pl.ds(r, 1), :] for v in vectors]
    rows += [rows[0]] * (8 - len(rows))
    stacked = jnp.concatenate(rows, axis=0).T
    return [stacked[:, q : q + 1] for q in range(len(vectors))]


def known_rates(p, s, near_term, vectors, r):
    stiff, plate, direct, evolve = per_row(vectors, r)
    velocity = jnp.exp(p)
    state = jnp.exp(-s) - velocity
    factor = 1.0 / (direct + damping * velocity)
    return (stiff * (plate - velocity) - near_term - evolve * state) * factor, factor, state


def first_local_kernel(
    me_ref, columns, x_in, near_in, p_in, s_in, coupling, stiff, plate, direct, evolve,
    known_out, factor_out, edge_out, coupling_t_out,
    x, near, p, s, known, factor, edge, coupling_t, place,
    x_sem, near_sems, p_sems, s_sems, known_sems, factor_sems, edge_sems, ct_sem,
):
    row_blocks, near_count, size, _ = near.shape
    chunks = near_sems.shape[0]
    group = row_blocks // chunks
    load_x = pltpu.make_async_copy(x_in, x, x_sem)
    load_x.start()

    def loads(c):
        return [
            part(near_in, near, near_sems, c, group),
            part(p_in, p, p_sems, c, group),
            part(s_in, s, s_sems, c, group),
        ]

    def stores(c):
        return [
            part(known, known_out, known_sems, c, group),
            part(factor, factor_out, factor_sems, c, group),
        ]

    for c in range(chunks):
        for copy in loads(c):
            copy.start()
    for r in range(row_blocks):
        for o in range(2 * REACH + 1):
            place[r, o] = -1
    for r in range(row_blocks):
        coupling_t[r] = coupling[:, r * size : (r + 1) * size].T
    store_ct = pltpu.make_async_copy(coupling_t, coupling_t_out, ct_sem)
    store_ct.start()
    load_x.wait()

    def chunk(c, carry):
        for copy in loads(c):
            copy.wait()
        for i in range(group):
            r = c * group + i
            product = near_product(me_ref, columns, x, near, r, place)
            rate, scale, _ = known_rates(p[r], s[r], product, (stiff, plate, direct, evolve), r)
            known[r] = p[r] + step_size * rate
            factor[r] = step_size * scale
        for copy in stores(c):
            copy.start()
        return carry

    lax.fori_loop(0, chunks, chunk, 0)
    n = 0
    store_edges = []
    for side, blocks in enumerate(edge_list(row_blocks)):
        first = n
        for r, offset in blocks:
            k = place[r, offset + REACH]
            block = near[r, jnp.maximum(k, 0)]
            edge[n] = jnp.where(k >= 0, block, jnp.zeros_like(block))
            n += 1
        at = pl.ds(first, n - first)
        store_edges.append(pltpu.make_async_copy(edge.at[at], edge_out.at[at], edge_sems.at[side]))
        store_edges[-1].start()
    lax.fori_loop(0, chunks, lambda c, carry: [copy.wait() for copy in stores(c)] and carry, 0)
    for copy in store_edges + [store_ct]:
        copy.wait()


def second_local_kernel(
    me_ref, columns, x_in, near_in, p_in, s_in, p2_in, stiff, plate, direct, evolve, area,
    known_out, change_out, factor_out, new_s_out, parts,
    x, near, p, s, p2, known, change, factor, new_s,
    x_sem, near_sems, p_sems, s_sems, p2_sems, known_sems, change_sems, factor_sems, new_s_sems,
):
    row_blocks, near_count, size, cols = near.shape
    chunks = near_sems.shape[0]
    group = row_blocks // chunks
    load_x = pltpu.make_async_copy(x_in, x, x_sem)
    load_x.start()

    def loads(c):
        return [
            part(near_in, near, near_sems, c, group),
            part(p_in, p, p_sems, c, group),
            part(s_in, s, s_sems, c, group),
            part(p2_in, p2, p2_sems, c, group),
        ]

    def stores(c):
        return [
            part(known, known_out, known_sems, c, group),
            part(change, change_out, change_sems, c, group),
            part(factor, factor_out, factor_sems, c, group),
            part(new_s, new_s_out, new_s_sems, c, group),
        ]

    for c in range(chunks):
        for copy in loads(c):
            copy.start()
    load_x.wait()

    def chunk(c, carry):
        errors, areas = carry
        for copy in loads(c):
            copy.wait()
        for i in range(group):
            r = c * group + i
            product = near_product(me_ref, columns, x, near, r)
            rate_a = (p2[r] - p[r]) * (1.0 / step_size)
            state_a = jnp.exp(-s[r]) - jnp.exp(p[r])
            rate, scale, state_b = known_rates(
                p2[r], s[r] + step_size * state_a, product, (stiff, plate, direct, evolve), r
            )
            known[r] = p[r] + half_step * (rate_a + rate)
            change[r] = half_step * (rate - rate_a)
            factor[r] = half_step * scale
            new_s[r] = s[r] + half_step * (state_a + state_b)
            state_error = (half_step / error_scale) * (state_b - state_a)
            weight = jnp.broadcast_to(per_row((area,), r)[0], (size, cols))
            weighted = weight * (state_error * state_error)
            errors += jnp.sum(weighted.reshape(size // 8, 8, cols), axis=0)
            areas += jnp.sum(weight.reshape(size // 8, 8, cols), axis=0)
        for copy in stores(c):
            copy.start()
        return errors, areas

    zero = jnp.zeros((8, cols), F32)
    errors, areas = lax.fori_loop(0, chunks, chunk, (zero, zero))
    parts[0] = errors
    parts[1] = areas
    lax.fori_loop(0, chunks, lambda c, carry: [copy.wait() for copy in stores(c)] and carry, 0)


def couple(me, got, levels):
    devices = got.shape[0]
    sums = []
    for level in range(levels):
        total = got[me ^ (1 << level)].astype(F32)
        for m in range((1 << level) + 1, min(2 << level, devices)):
            total += got[me ^ m].astype(F32)
        sums.append(total.astype(BF16))
    return jnp.concatenate(sums, axis=0)


def row_order(row_blocks, chunks):
    group = row_blocks // chunks
    inner = [
        c for c in range(chunks) if c * group >= REACH and (c + 1) * group <= row_blocks - REACH
    ]
    return inner + [c for c in range(chunks) if c not in inner]


def outer_terms(coupled, coupling_t, halo, edge, r):
    row_blocks, size, _ = coupling_t.shape
    left, right = edge_rows(row_blocks)
    lhs, rhs = [coupling_t[r]], [coupled]
    n = 0
    for row, low in left:
        for t in range(low, REACH):
            if row == r:
                lhs.append(edge[n])
                rhs.append(halo[t])
            n += 1
    for row, count in right:
        for t in range(count):
            if row == r:
                lhs.append(edge[n])
                rhs.append(halo[REACH + t])
            n += 1
    return jnp.dot(
        jnp.concatenate(lhs, axis=1), jnp.concatenate(rhs, axis=0), preferred_element_type=F32
    )


def outer_loads(me, a_in, b_in, got_in, edge_in, ct_in, halo, got, edge, coupling_t, sems):
    odd = lax.rem(me, 2)
    return [
        pltpu.make_async_copy(got_in, got, sems.at[0]),
        pltpu.make_async_copy(ct_in, coupling_t, sems.at[1]),
        pltpu.make_async_copy(a_in, halo.at[pl.ds((1 - odd) * REACH, REACH)], sems.at[2]),
        pltpu.make_async_copy(b_in, halo.at[pl.ds(odd * REACH, REACH)], sems.at[3]),
        pltpu.make_async_copy(edge_in, edge, sems.at[4]),
    ]


def middle_kernel(
    me_ref, a_in, b_in, got_in, edge_in, ct_in, basis_in, known_in, factor_in,
    p2_out, x_out, slots_out, a_out, b_out,
    halo, got, edge, coupling_t, basis, known, factor, p2, x, slots,
    outer_sems, basis_sem, known_sems, factor_sems, p2_sems, x_sem, send_sems,
):
    row_blocks, size, cols = known.shape
    chunks = known_sems.shape[0]
    group = row_blocks // chunks
    me = me_ref[0]
    order = row_order(row_blocks, chunks)
    outer = outer_loads(me, a_in, b_in, got_in, edge_in, ct_in, halo, got, edge, coupling_t, outer_sems)

    def loads(c):
        return [part(known_in, known, known_sems, c, group), part(factor_in, factor, factor_sems, c, group)]

    load_basis = pltpu.make_async_copy(basis_in, basis, basis_sem)
    for copy in outer[:2] + loads(order[0]) + outer[2:] + [load_basis]:
        copy.start()
    for c in order[1:]:
        for copy in loads(c):
            copy.start()
    outer[0].wait()
    coupled = couple(me, got, basis.shape[0] // got.shape[1])
    outer[1].wait()
    projected = jnp.zeros((basis.shape[0], cols), F32)
    waited = False
    for n, c in enumerate(order):
        edged = c * group < REACH or (c + 1) * group > row_blocks - REACH
        if edged and not waited:
            for copy in outer[2:]:
                copy.wait()
            waited = True
        for copy in loads(c):
            copy.wait()
        for r in range(c * group, (c + 1) * group):
            terms = outer_terms(coupled, coupling_t, halo, edge, r)
            value = known[r] - factor[r] * terms
            p2[r] = value
            x[r] = jnp.exp(value).astype(BF16)
        part(p2, p2_out, p2_sems, c, group).start()
        if n == 0:
            load_basis.wait()
        projected += jnp.dot(
            basis[:, c * group * size : (c + 1) * group * size],
            x[c * group : (c + 1) * group].reshape(group * size, cols),
            preferred_element_type=F32,
        )
    x[row_blocks] = jnp.zeros((size, cols), BF16)
    fill_slots(me, projected, slots)
    copies = send_copies(me, x, slots, None, None, slots_out, a_out, b_out, send_sems)
    copies.append(pltpu.make_async_copy(x, x_out, x_sem))
    for copy in copies:
        copy.start()
    for copy in copies + [part(p2, p2_out, p2_sems, c, group) for c in range(chunks)]:
        copy.wait()


def close_kernel(
    me_ref, a_in, b_in, got_in, edge_in, ct_in, known_in, change_in, factor_in, area, parts_in,
    new_p_out, parts_out,
    halo, got, edge, coupling_t, known, change, factor, new_p,
    outer_sems, known_sems, change_sems, factor_sems, new_p_sems,
):
    row_blocks, size, cols = known.shape
    chunks = known_sems.shape[0]
    group = row_blocks // chunks
    me = me_ref[0]
    order = row_order(row_blocks, chunks)
    outer = outer_loads(me, a_in, b_in, got_in, edge_in, ct_in, halo, got, edge, coupling_t, outer_sems)

    def loads(c):
        return [
            part(known_in, known, known_sems, c, group),
            part(change_in, change, change_sems, c, group),
            part(factor_in, factor, factor_sems, c, group),
        ]

    for copy in outer[:2] + loads(order[0]) + outer[2:]:
        copy.start()
    for c in order[1:]:
        for copy in loads(c):
            copy.start()
    outer[0].wait()
    coupled = couple(me, got, coupling_t.shape[2] // got.shape[1])
    outer[1].wait()
    errors = parts_in[0]
    waited = False
    for c in order:
        edged = c * group < REACH or (c + 1) * group > row_blocks - REACH
        if edged and not waited:
            for copy in outer[2:]:
                copy.wait()
            waited = True
        for copy in loads(c):
            copy.wait()
        for r in range(c * group, (c + 1) * group):
            outside = factor[r] * outer_terms(coupled, coupling_t, halo, edge, r)
            new_p[r] = known[r] - outside
            rate_error = (1.0 / error_scale) * (change[r] - outside)
            weighted = per_row((area,), r)[0] * (rate_error * rate_error)
            errors += jnp.sum(weighted.reshape(size // 8, 8, cols), axis=0)
        part(new_p, new_p_out, new_p_sems, c, group).start()
    both = jnp.concatenate(
        [jnp.sum(errors, axis=0, keepdims=True), jnp.sum(parts_in[1], axis=0, keepdims=True)], axis=0
    )
    for j in range(parts_out.shape[0]):
        parts_out[j] = both
    for c in range(chunks):
        part(new_p, new_p_out, new_p_sems, c, group).wait()


def exchange(side_a, side_b, slots):
    count = lax.axis_size(AXIS)
    got_a = lax.ppermute(side_a, AXIS, [(i, i ^ 1) for i in range(count)])
    pairs = [(i, (i - 1) % count if i % 2 == 0 else (i + 1) % count) for i in range(count)]
    got_b = lax.ppermute(side_b, AXIS, pairs)
    got = lax.all_to_all(slots, AXIS, 0, 0)
    return got_a, got_b, got


def on_device(
    log_rate,
    log_state,
    near_blocks,
    near_columns,
    far_basis,
    far_coupling,
    self_stiffness,
    plate_rate,
    direct_effect,
    evolution_effect,
    triangle_area,
):
    rows, cols = log_rate.shape
    row_blocks, near_count, size, _ = near_blocks.shape
    levels, rank, _ = far_basis.shape
    devices = lax.axis_size(AXIS)
    me = jnp.stack([lax.axis_index(AXIS), jnp.int32(devices)]).astype(jnp.int32)
    p = log_rate.reshape(row_blocks, size, cols)
    s = log_state.reshape(row_blocks, size, cols)
    basis = far_basis.reshape(levels * rank, rows)
    coupling = far_coupling.reshape(levels * rank, rows)
    stiff, plate, direct, evolve, area = (
        v.reshape(row_blocks, size)
        for v in (self_stiffness, plate_rate, direct_effect, evolution_effect, triangle_area)
    )
    edges = sum(len(blocks) for blocks in edge_list(row_blocks))
    state = ((row_blocks, size, cols), F32)
    x_kind = ((row_blocks + 1, size, cols), BF16)
    slots_kind = ((devices, rank, cols), BF16)
    side_kind = ((REACH, size, cols), BF16)
    edge_kind = ((edges, size, size), BF16)
    ct_kind = ((row_blocks, size, levels * rank), BF16)
    basis_kind = ((levels * rank, rows), BF16)
    near_kind = (near_blocks.shape, BF16)
    halo_kind = ((2 * REACH, size, cols), BF16)
    chunks = 8 if row_blocks % 8 == 0 else row_blocks
    loads = 4 if row_blocks % 4 == 0 else row_blocks
    near_flops = 2 * rows * near_count * size * cols

    def vmem(*kinds):
        return [pltpu.VMEM(shape, dtype) for shape, dtype in kinds]

    x, slots, side_a, side_b = pl.pallas_call(
        open_kernel,
        out_shape=like(x_kind, slots_kind, side_kind, side_kind),
        in_specs=[SCALARS, PLAIN, PLAIN],
        out_specs=(PLAIN,) * 4,
        scratch_shapes=vmem(state, basis_kind, x_kind, slots_kind)
        + [SEMS((loads,)), SEMS(()), SEMS(()), SEMS((3,))],
        name="open",
    )(me, p, basis)

    got_a, got_b, got = exchange(side_a, side_b, slots)
    known, factor, edge, coupling_t = pl.pallas_call(
        first_local_kernel,
        out_shape=like(state, state, edge_kind, ct_kind),
        in_specs=[SCALARS, SCALARS] + [PLAIN] * 4 + [WHOLE] * 5,
        out_specs=(PLAIN,) * 4,
        scratch_shapes=vmem(x_kind, near_kind, state, state, state, state, edge_kind, ct_kind)
        + [pltpu.SMEM((row_blocks, 2 * REACH + 1), jnp.int32), SEMS(())]
        + [SEMS((chunks,))] * 5
        + [SEMS((2,)), SEMS(())],
        cost_estimate=cost(near_flops, near_blocks.size * 2),
        name="local_one",
    )(me, near_columns, x, near_blocks, p, s, coupling, stiff, plate, direct, evolve)

    p2, x, slots, side_a, side_b = pl.pallas_call(
        middle_kernel,
        out_shape=like(state, x_kind, slots_kind, side_kind, side_kind),
        in_specs=[SCALARS] + [LOOSE] * 3 + [PLAIN] * 5,
        out_specs=(PLAIN,) * 5,
        scratch_shapes=vmem(
            halo_kind, slots_kind, edge_kind, ct_kind, basis_kind, state, state, state, x_kind, slots_kind
        )
        + [SEMS((5,)), SEMS(()), SEMS((chunks,)), SEMS((chunks,)), SEMS((chunks,)), SEMS(()), SEMS((3,))],
        name="middle",
    )(me, got_a, got_b, got, edge, coupling_t, basis, known, factor)

    got_a, got_b, got = exchange(side_a, side_b, slots)
    known, change, factor, new_s, parts = pl.pallas_call(
        second_local_kernel,
        out_shape=like(state, state, state, state, ((2, 8, cols), F32)),
        in_specs=[SCALARS, SCALARS] + [PLAIN] * 5 + [WHOLE] * 5,
        out_specs=(PLAIN,) * 4 + (WHOLE,),
        scratch_shapes=vmem(x_kind, near_kind, state, state, state, state, state, state, state)
        + [SEMS(())]
        + [SEMS((chunks,))] * 8,
        cost_estimate=cost(near_flops, near_blocks.size * 2),
        name="local_two",
    )(me, near_columns, x, near_blocks, p, s, p2, stiff, plate, direct, evolve, area)

    new_p, parts = pl.pallas_call(
        close_kernel,
        out_shape=like(state, ((devices, 2, cols), F32)),
        in_specs=[SCALARS] + [LOOSE] * 3 + [PLAIN] * 5 + [WHOLE] * 2,
        out_specs=(PLAIN, WHOLE),
        scratch_shapes=vmem(halo_kind, slots_kind, edge_kind, ct_kind, state, state, state, state)
        + [SEMS((5,))]
        + [SEMS((chunks,))] * 4,
        name="close",
    )(me, got_a, got_b, got, edge, coupling_t, known, change, factor, area, parts)

    totals = lax.all_to_all(parts, AXIS, 0, 0).sum(axis=0)
    error_norm = jnp.sqrt(totals[0] / totals[1] + 1e-06)
    return new_p.reshape(rows, cols), new_s.reshape(rows, cols), error_norm


def solution(mesh):
    split = P(("member", "patch"))
    in_specs = (
        P(("member", "patch"), None),
        P(("member", "patch"), None),
        P(("member", "patch"), None, None, None),
        P(("member", "patch"), None),
        P("member", None, "patch"),
        P("member", None, "patch"),
        split,
        split,
        split,
        split,
        split,
    )
    out_specs = (P(("member", "patch"), None), P(("member", "patch"), None), P("member"))
    return jax.shard_map(
        on_device, mesh=mesh, in_specs=in_specs, out_specs=out_specs, check_vma=False
    )
```

time: 121 us -> 71.5 us (0.59)
  Pallas kernels: 0 us -> 37.1 us
  local copies, waits for them, and re-layouts: 29.6 us -> 1.51 us
  matrix products: 22.2 us -> 0 us
  blocking collectives: 30.1 us -> 9.94 us
  waiting for transfers between devices: 18.8 us -> 0.02 us
  starting transfers between devices: 16.2 us -> 20.4 us
  other arithmetic: 3.17 us -> 1.21 us
    pallas_call x0 -> x5, Pallas kernels: none -> 37.1 us  [the longest x1 10.2 us: on_device(): pl.pallas_call(second_local_kernel, out_shape=like(state, state, state, s...]
    psum x1 -> x0, blocking collectives: 30.1 us -> none  [on_device(): totals, area_total = lax.psum((area_terms, jnp.sum(triangle_area)), 'patch')]
    dot_general x6 -> x0, matrix products: 22.2 us -> none  [the longest x2 12.9 us: section_rates(): jnp.einsum('rkij,rkjb->rib', near_blocks, chosen, preferred_element_type=...]
    ppermute x12 -> x4, waiting for transfers between devices: 18.8 us -> 0.01 us  [the longest x2 0.01 us: exchange(): got_a = lax.ppermute(side_a, AXIS, [(i, i ^ 1) for i in range(count)])]
    gather x2 -> x0, local copies, waits for them, and re-layouts: 16.1 us -> none  [section_rates(): chosen = column_blocks[position]]
    all_to_all x0 -> x2, starting transfers between devices: none -> 10.9 us  [exchange(): got = lax.all_to_all(slots, AXIS, 0, 0)]
    all_to_all x0 -> x1, blocking collectives: none -> 9.94 us  [on_device(): totals = lax.all_to_all(parts, AXIS, 0, 0).sum(axis=0)]
    ppermute x12 -> x4, starting transfers between devices: 16.2 us -> 9.45 us  [the longest x2 8.75 us: exchange(): got_b = lax.ppermute(side_b, AXIS, pairs)]
  transfers between devices with their start and end apart: 12 -> 6, of which waited for: 8 -> 0; matrix products, arithmetic and copies ran while one was open for 5% -> 0% of each run, Pallas kernels for 0% -> 28%
where the time goes in v2:
time: 71.5 us; the launch traced here: 71 us
  Pallas kernels  37.1 us (52%)
  starting transfers between devices  20.4 us (29%)
  blocking collectives  9.94 us (14%)
  local copies, waits for them, and re-layouts  1.51 us (2%)
  other arithmetic  1.21 us (2%)
  between operations  0.79 us (1%)
    all_to_all x2, starting transfers between devices, exchange(): got = lax.all_to_all(slots, AXIS, 0, 0)  10.9 us
    pallas_call x1, Pallas kernels, on_device(): pl.pallas_call(second_local_kernel, out_shape=like(state, state, state, s...  10.2 us
    all_to_all x1, blocking collectives, on_device(): totals = lax.all_to_all(parts, AXIS, 0, 0).sum(axis=0)  9.94 us
    pallas_call x1, Pallas kernels, on_device(): pl.pallas_call(first_local_kernel, out_shape=like(state, state, edge_kind...  9.75 us
    ppermute x2, starting transfers between devices, exchange(): got_b = lax.ppermute(side_b, AXIS, pairs)  8.75 us
    pallas_call x1, Pallas kernels, on_device(): pl.pallas_call(middle_kernel, out_shape=like(state, x_kind, slots_kind, s...  7.1 us
    pallas_call x1, Pallas kernels, on_device(): pl.pallas_call(close_kernel, out_shape=like(state, ((devices, 2, cols), F...  6.52 us
    pallas_call x1, Pallas kernels, on_device(): pl.pallas_call(open_kernel, out_shape=like(x_kind, slots_kind, side_kind,...  3.52 us
  transfers between devices with their start and end apart: 6, of which 0 were waited for; matrix products, arithmetic and copies ran while one was open for 0% of the time, Pallas kernels for 28%

profile of v2, /device:TPU:0, one launch (start us, length us, event | category | flops | bytes accessed | tf_op | source)
XLA Modules:
  0.0 71.0 jit_solution(13717741615725871753)
XLA Ops:
  0.6 0.7 pad_add_fusion.me_ref
  1.3 3.5 %open.1 = (bf16[17,128,128]{2,1,0:T(8,128)(2,1)}, bf16[16,32,128]{2,1,0:T(8,128)(2,1)}, bf16[6,128,128]{2,1,0:T(8,128)(2,1)}, bf16[6,128,128]{2,1,0:T(8,128)(2,1)}) custom-call(s32[2]{0:T(128)} %pad_add_fusion.me_ref, f32[16,128,128]{2,1,0:T(8,128)} %bitcast.14, bf16[128,2048]{1,0:T(8,128)(2,1)} %bitcast.19), custom_call_target="tpu_custom_call" | custom-call | tf_op jit(solution)/shard_map/open/pallas_call | solution.py:493
  4.8 7.4 %all-to-all-start = ((bf16[16,32,128]{2,1,0:T(8,128)(2,1)}), bf16[16,32,128]{2,1,0:T(8,128)(2,1)S(1)}, u32[]{:S(2)}, u32[]{:S(2)}) async-start(bf16[16,32,128]{2,1,0:T(8,128)(2,1)} %get-tuple-element.25), calls=%async_computation | async-start | bytes 262144 | tf_op jit(solution)/shard_map/all_to_all | solution.py:446
  12.3 0.4 collective-permute-start
  12.7 4.3 %collective-permute-start.1 = (bf16[6,128,128]{2,1,0:T(8,128)(2,1)}, bf16[6,128,128]{2,1,0:T(8,128)(2,1)S(1)}, u32[]{:S(2)}, u32[]{:S(2)}) collective-permute-start(bf16[6,128,128]{2,1,0:T(8,128)(2,1)} %get-tuple-element.24), channel_id=1, source_target_pairs={{0,15},{1,2},{2,1},{3,4},{4,3},{5,6},{6,5},{7,8},{8,7},{9,10},{10,... | collective-permute-start | bytes 589832 | tf_op jit(solution)/shard_map/ppermute | solution.py:445
  17.0 9.8 %local_one.1 = (f32[16,128,128]{2,1,0:T(8,128)}, f32[16,128,128]{2,1,0:T(8,128)}, bf16[42,128,128]{2,1,0:T(8,128)(2,1)}, bf16[16,128,128]{2,1,0:T(8,128)(2,1)}) custom-call(s32[2]{0:T(128)} %pad_add_fusion.me_ref, s32[16,12]{1,0:T(8,128)} %columns.3, bf16[17,128,128]{2,1,0:T(8,128)(2,1)} %get-tuple-element.26.x_in, bf16[16,12,128,128]{3,2,1,0:T(8,128)(2,1)} %near_in.3, ...), custom_call_target="tpu_custom_call" | custom-call | flops 805306368 | bytes 6291456 | tf_op jit(solution)/shard_map/local_one/pallas_call | solution.py:504
  26.8 0.0 collective-permute-done.a_in
  26.8 0.0 copy-start.4
  26.8 0.0 collective-permute-done.1.b_in
  26.8 0.0 copy-start.5
  26.8 0.0 all-to-all-done.got_in
  26.8 0.0 copy-start.1
  26.8 0.6 copy-done.4
  27.5 0.1 copy-done.5
  27.5 0.0 copy-done.1
  27.6 7.1 %middle.1 = (f32[16,128,128]{2,1,0:T(8,128)}, bf16[17,128,128]{2,1,0:T(8,128)(2,1)}, bf16[16,32,128]{2,1,0:T(8,128)(2,1)}, bf16[6,128,128]{2,1,0:T(8,128)(2,1)}, bf16[6,128,128]{2,1,0:T(8,128)(2,1)}) custom-call(s32[2]{0:T(128)} %pad_add_fusion.me_ref, bf16[6,128,128]{2,1,0:T(8,128)(2,1)} %copy-done.4, bf16[6,128,128]{2,1,0:T(8,128)(2,1)} %copy-done.5, ...), custom_call_target="tpu_custom_call" | custom-call | tf_op jit(solution)/shard_map/middle/pallas_call | solution.py:517
  34.7 3.5 %all-to-all-start.1 = ((bf16[16,32,128]{2,1,0:T(8,128)(2,1)}), bf16[16,32,128]{2,1,0:T(8,128)(2,1)S(1)}, u32[]{:S(2)}, u32[]{:S(2)}) async-start(bf16[16,32,128]{2,1,0:T(8,128)(2,1)} %get-tuple-element.33), calls=%async_computation.1 | async-start | bytes 262144 | tf_op jit(solution)/shard_map/all_to_all | solution.py:446
  38.2 0.3 collective-permute-start.2
  38.5 4.4 %collective-permute-start.3 = (bf16[6,128,128]{2,1,0:T(8,128)(2,1)}, bf16[6,128,128]{2,1,0:T(8,128)(2,1)S(1)}, u32[]{:S(2)}, u32[]{:S(2)}) collective-permute-start(bf16[6,128,128]{2,1,0:T(8,128)(2,1)} %get-tuple-element.32), channel_id=1, source_target_pairs={{0,15},{1,2},{2,1},{3,4},{4,3},{5,6},{6,5},{7,8},{8,7},{9,10},{10,... | collective-permute-start | bytes 589832 | tf_op jit(solution)/shard_map/ppermute | solution.py:445
  42.9 10.2 %local_two.1 = (f32[16,128,128]{2,1,0:T(8,128)}, f32[16,128,128]{2,1,0:T(8,128)}, f32[16,128,128]{2,1,0:T(8,128)}, f32[16,128,128]{2,1,0:T(8,128)}, f32[2,8,128]{2,1,0:T(8,128)}) custom-call(s32[2]{0:T(128)} %pad_add_fusion.me_ref, s32[16,12]{1,0:T(8,128)} %columns.3, bf16[17,128,128]{2,1,0:T(8,128)(2,1)} %get-tuple-element.34.x_in, ...), custom_call_target="tpu_custom_call" | custom-call | flops 805306368 | bytes 6291456 | tf_op jit(solution)/shard_map/local_two/pallas_call | solution.py:530
  53.1 0.0 collective-permute-done.2.a_in
  53.1 0.0 copy-start.2
  53.2 0.0 collective-permute-done.3.b_in
  53.2 0.0 copy-start.3
  53.2 0.0 all-to-all-done.1.got_in
  53.2 0.0 copy-start
  53.2 0.6 copy-done.2
  53.8 0.1 copy-done.3
  53.9 0.0 copy-done
  54.0 6.5 %close.1 = (f32[16,128,128]{2,1,0:T(8,128)}, f32[16,2,128]{2,1,0:T(2,128)}) custom-call(s32[2]{0:T(128)} %pad_add_fusion.me_ref, bf16[6,128,128]{2,1,0:T(8,128)(2,1)} %copy-done.2, bf16[6,128,128]{2,1,0:T(8,128)(2,1)} %copy-done.3, bf16[16,32,128]{2,1,0:T(8,128)(2,1)} %copy-done, bf16[42,128,128]{2,1,0:T(8,128)(2,1)} %get-tuple-element.27.edge_in, ...), custom_call_target="tpu_custom_call" | custom-call | tf_op jit(solution)/shard_map/close/pallas_call | solution.py:542
  60.5 9.9 %all_to_all.15 = f32[16,2,128]{2,1,0:T(2,128)S(1)} all-to-all(f32[16,2,128]{2,1,0:T(2,128)} %get-tuple-element.42), channel_id=1, replica_groups=mesh['member'=2,'patch'=16] {'patch'}, dimensions={0} | all-to-all | bytes 32768 | tf_op jit(solution)/shard_map/all_to_all | solution.py:553
  70.5 0.5 sqrt_bitcast_fusion
  (1 shorter events, 0.0 us)
Async XLA Ops:
  4.8 22.0 %all-to-all-start = ((bf16[16,32,128]{2,1,0:T(8,128)(2,1)}), bf16[16,32,128]{2,1,0:T(8,128)(2,1)S(1)}, u32[]{:S(2)}, u32[]{:S(2)}) async-start(bf16[16,32,128]{2,1,0:T(8,128)(2,1)} %get-tuple-element.25), calls=%async_computation | async-start | bytes 262144 | tf_op jit(solution)/shard_map/all_to_all | solution.py:446
  12.3 14.5 %collective-permute-start = (bf16[6,128,128]{2,1,0:T(8,128)(2,1)}, bf16[6,128,128]{2,1,0:T(8,128)(2,1)S(1)}, u32[]{:S(2)}, u32[]{:S(2)}) collective-permute-start(bf16[6,128,128]{2,1,0:T(8,128)(2,1)} %get-tuple-element.23), channel_id=1, source_target_pairs={{0,1},{1,0},{2,3},{3,2},{4,5},{5,4},{6,7},{7,6},{8,9},{9,8},{10,11... | collective-permute-start | bytes 589832 | tf_op jit(solution)/shard_map/ppermute | solution.py:443
  12.7 14.1 %collective-permute-start.1 = (bf16[6,128,128]{2,1,0:T(8,128)(2,1)}, bf16[6,128,128]{2,1,0:T(8,128)(2,1)S(1)}, u32[]{:S(2)}, u32[]{:S(2)}) collective-permute-start(bf16[6,128,128]{2,1,0:T(8,128)(2,1)} %get-tuple-element.24), channel_id=1, source_target_pairs={{0,15},{1,2},{2,1},{3,4},{4,3},{5,6},{6,5},{7,8},{8,7},{9,10},{10,... | collective-permute-start | bytes 589832 | tf_op jit(solution)/shard_map/ppermute | solution.py:445
  26.8 0.7 copy-start.4
  26.8 0.7 %copy-start.5 = (bf16[6,128,128]{2,1,0:T(8,128)(2,1)}, bf16[6,128,128]{2,1,0:T(8,128)(2,1)S(1)}, u32[]{:S(2)}) copy-start(bf16[6,128,128]{2,1,0:T(8,128)(2,1)S(1)} %collective-permute-done.1.b_in) | copy-start | bytes 589828
  26.8 0.7 %copy-start.1 = (bf16[16,32,128]{2,1,0:T(8,128)(2,1)}, bf16[16,32,128]{2,1,0:T(8,128)(2,1)S(1)}, u32[]{:S(2)}) copy-start(bf16[16,32,128]{2,1,0:T(8,128)(2,1)S(1)} %all-to-all-done.got_in) | copy-start | bytes 393220
  34.7 18.5 %all-to-all-start.1 = ((bf16[16,32,128]{2,1,0:T(8,128)(2,1)}), bf16[16,32,128]{2,1,0:T(8,128)(2,1)S(1)}, u32[]{:S(2)}, u32[]{:S(2)}) async-start(bf16[16,32,128]{2,1,0:T(8,128)(2,1)} %get-tuple-element.33), calls=%async_computation.1 | async-start | bytes 262144 | tf_op jit(solution)/shard_map/all_to_all | solution.py:446
  38.2 15.0 %collective-permute-start.2 = (bf16[6,128,128]{2,1,0:T(8,128)(2,1)}, bf16[6,128,128]{2,1,0:T(8,128)(2,1)S(1)}, u32[]{:S(2)}, u32[]{:S(2)}) collective-permute-start(bf16[6,128,128]{2,1,0:T(8,128)(2,1)} %get-tuple-element.31), channel_id=1, source_target_pairs={{0,1},{1,0},{2,3},{3,2},{4,5},{5,4},{6,7},{7,6},{8,9},{9,8},{10,11... | collective-permute-start | bytes 589832 | tf_op jit(solution)/shard_map/ppermute | solution.py:443
  38.5 14.7 %collective-permute-start.3 = (bf16[6,128,128]{2,1,0:T(8,128)(2,1)}, bf16[6,128,128]{2,1,0:T(8,128)(2,1)S(1)}, u32[]{:S(2)}, u32[]{:S(2)}) collective-permute-start(bf16[6,128,128]{2,1,0:T(8,128)(2,1)} %get-tuple-element.32), channel_id=1, source_target_pairs={{0,15},{1,2},{2,1},{3,4},{4,3},{5,6},{6,5},{7,8},{8,7},{9,10},{10,... | collective-permute-start | bytes 589832 | tf_op jit(solution)/shard_map/ppermute | solution.py:445
  53.1 0.7 copy-start.2
  53.2 0.8 %copy-start.3 = (bf16[6,128,128]{2,1,0:T(8,128)(2,1)}, bf16[6,128,128]{2,1,0:T(8,128)(2,1)S(1)}, u32[]{:S(2)}) copy-start(bf16[6,128,128]{2,1,0:T(8,128)(2,1)S(1)} %collective-permute-done.3.b_in) | copy-start | bytes 589828
  53.2 0.8 %copy-start = (bf16[16,32,128]{2,1,0:T(8,128)(2,1)}, bf16[16,32,128]{2,1,0:T(8,128)(2,1)S(1)}, u32[]{:S(2)}) copy-start(bf16[16,32,128]{2,1,0:T(8,128)(2,1)S(1)} %all-to-all-done.1.got_in) | copy-start | bytes 393220

commit v3 on v2

v3 whole, which is shorter than its diff:
```python
import jax
import jax.numpy as jnp
from jax import lax
from jax.experimental import pallas as pl
from jax.experimental.pallas import tpu as pltpu
from jax.sharding import PartitionSpec as P


REACH = 6

step_size = 0.1
damping = 0.5
error_scale = 0.01
half_step = 0.5 * step_size

AXIS = "patch"
F32 = jnp.float32
BF16 = jnp.bfloat16
PLAIN = pl.BlockSpec(memory_space=pltpu.HBM)
WHOLE = pl.BlockSpec(memory_space=pltpu.VMEM)
SCALARS = pl.BlockSpec(memory_space=pltpu.SMEM)
SEMS = pltpu.SemaphoreType.DMA


def cost(flops, moved, exps=0):
    return pl.CostEstimate(flops=flops, bytes_accessed=moved, transcendentals=exps)


def in_hbm(*shapes):
    return tuple(pltpu.HBM(shape, dtype) for shape, dtype in shapes)


def hbm(*arrays):
    return tuple(pltpu.with_memory_space_constraint(v, pltpu.HBM) for v in arrays)


def like(*shapes):
    return tuple(jax.ShapeDtypeStruct(shape, dtype) for shape, dtype in shapes)


def part(src, dst, sems, c, group):
    at = pl.ds(c * group, group)
    return pltpu.make_async_copy(src.at[at], dst.at[at], sems.at[c])


def edge_rows(row_blocks):
    left = [(r, r) for r in range(min(REACH, row_blocks))]
    right = [(r, r + REACH + 1 - row_blocks) for r in range(max(row_blocks - REACH, 0), row_blocks)]
    return left, right


def edge_list(row_blocks):
    left, right = edge_rows(row_blocks)
    return (
        [(r, t - REACH - r) for r, low in left for t in range(low, REACH)],
        [(r, row_blocks + t - r) for r, count in right for t in range(count)],
    )


def fill_slots(me, projected, slots):
    devices, rank, _ = slots.shape
    for m in range(devices):
        level = max(m.bit_length() - 1, 0)
        slots[me ^ m] = projected[level * rank : (level + 1) * rank].astype(slots.dtype)


def send_copies(me, x, slots, slots_out, a_out, b_out, sems):
    row_blocks = x.shape[0] - 1
    odd = lax.rem(me, 2)
    start_a = (1 - odd) * (row_blocks - REACH)
    start_b = odd * (row_blocks - REACH)
    return [
        pltpu.make_async_copy(slots, slots_out, sems.at[0]),
        pltpu.make_async_copy(x.at[pl.ds(start_a, REACH)], a_out, sems.at[1]),
        pltpu.make_async_copy(x.at[pl.ds(start_b, REACH)], b_out, sems.at[2]),
    ]


def open_kernel(
    p_in, basis_in, stiff, plate, direct, evolve, area,
    x_out, slots_out, a_out, b_out, columns_out,
    p, basis, x, slots, p_sems, x_sems, basis_sem, send_sems,
):
    row_blocks, size, cols = p.shape
    chunks = p_sems.shape[0]
    group = row_blocks // chunks
    me = lax.axis_index(AXIS)
    for c in range(chunks):
        part(p_in, p, p_sems, c, group).start()
        if c == 0:
            pltpu.make_async_copy(basis_in, basis, basis_sem).start()
    vectors = (stiff, plate, direct, evolve, area, area, area, area)
    for r in range(row_blocks):
        columns_out[r] = jnp.concatenate([v[r : r + 1] for v in vectors], axis=0)
    projected = jnp.zeros((basis.shape[0], cols), F32)
    for c in range(chunks):
        part(p_in, p, p_sems, c, group).wait()
        rows = slice(c * group, (c + 1) * group)
        rates = jnp.exp(p[rows]).astype(BF16)
        x[rows] = rates
        if c == 0:
            pltpu.make_async_copy(basis_in, basis, basis_sem).wait()
        projected += jnp.dot(
            basis[:, c * group * size : (c + 1) * group * size],
            rates.reshape(group * size, cols),
            preferred_element_type=F32,
        )
    x[row_blocks] = jnp.zeros((size, cols), BF16)
    fill_slots(me, projected, slots)
    copies = send_copies(me, x, slots, slots_out, a_out, b_out, send_sems)
    copies.append(pltpu.make_async_copy(x, x_out, x_sems))
    for copy in copies:
        copy.start()
    for copy in copies:
        copy.wait()


def find_columns(columns, picked, r, row_blocks, total, first, place=None):
    for k in range(columns.shape[1]):
        offset = columns[r, k] - first - r
        offset = jnp.where(offset > REACH, offset - total, offset)
        offset = jnp.where(offset < -REACH, offset + total, offset)
        if place is not None:
            place[r, offset + REACH] = k
        index = r + offset
        inside = jnp.logical_and(index >= 0, index < row_blocks)
        picked[k] = jnp.where(inside, index, row_blocks)


def near_product(near, x, picked, r):
    near_count = near.shape[1]
    left = jnp.concatenate([near[r, k] for k in range(near_count)], axis=1)
    right = jnp.concatenate([x[picked[k]] for k in range(near_count)], axis=0)
    return jnp.dot(left, right, preferred_element_type=F32)


def two_stage(row_blocks, find, wait_near, wait_rest, product, finish, even, odd, even_at, odd_at, carry):
    def body(i, carry):
        r = 2 * i
        wait_near(r + 1)
        wait_near(r + 2)
        wait_rest(r)
        wait_rest(r + 1)
        odd[...] = product(r + 1, odd_at)
        find(r + 2, even_at)
        carry = finish(r, even[...], carry)
        even[...] = product(r + 2, even_at)
        find(jnp.minimum(r + 3, row_blocks - 1), odd_at)
        return finish(r + 1, odd[...], carry)

    wait_near(0)
    find(0, even_at)
    find(1, odd_at)
    even[...] = product(0, even_at)
    carry = lax.fori_loop(0, row_blocks // 2 - 1, body, carry)
    last = row_blocks - 2
    wait_near(last + 1)
    wait_rest(last)
    wait_rest(last + 1)
    odd[...] = product(last + 1, odd_at)
    carry = finish(last, even[...], carry)
    return finish(last + 1, odd[...], carry)


def known_rates(velocity, state, near_term, rows):
    stiff, plate, direct, evolve = (rows[:, q : q + 1] for q in range(4))
    factor = 1.0 / (direct + damping * velocity)
    return (stiff * (plate - velocity) - near_term - evolve * state) * factor, factor


def first_local_kernel(
    columns, x_in, near_in, p_in, s_in, coupling, vectors,
    known_out, factor_out, edge_out, coupling_t_out,
    x, near, p, s, known, factor, edge, coupling_t, even, odd, even_at, odd_at, place,
    x_sem, near_sems, p_sems, s_sems, known_sems, factor_sems, edge_sems, ct_sem,
):
    row_blocks, _, size, _ = near.shape
    total = row_blocks * lax.axis_size(AXIS)
    first = row_blocks * lax.axis_index(AXIS)
    load_x = pltpu.make_async_copy(x_in, x, x_sem)
    load_x.start()

    def rest(r):
        return [part(p_in, p, p_sems, r, 1), part(s_in, s, s_sems, r, 1)]

    def stores(r):
        return [part(known, known_out, known_sems, r, 1), part(factor, factor_out, factor_sems, r, 1)]

    def start_loads(r, carry):
        for copy in [part(near_in, near, near_sems, r, 1)] + rest(r):
            copy.start()
        return carry

    lax.fori_loop(0, row_blocks, start_loads, 0)
    for r in range(row_blocks):
        for o in range(2 * REACH + 1):
            place[r, o] = -1
    for r in range(row_blocks):
        coupling_t[r] = coupling[:, r * size : (r + 1) * size].T
    store_ct = pltpu.make_async_copy(coupling_t, coupling_t_out, ct_sem)
    store_ct.start()
    load_x.wait()

    def finish(r, product, carry):
        now = p[r]
        velocity = jnp.exp(now)
        state = jnp.exp(-s[r]) - velocity
        rate, scale = known_rates(velocity, state, product, vectors[r].T)
        known[r] = now + step_size * rate
        factor[r] = step_size * scale
        for copy in stores(r):
            copy.start()
        return carry

    two_stage(
        row_blocks,
        lambda r, at: find_columns(columns, at, r, row_blocks, total, first, place),
        lambda r: part(near_in, near, near_sems, r, 1).wait(),
        lambda r: [copy.wait() for copy in rest(r)],
        lambda r, at: near_product(near, x, at, r),
        finish, even, odd, even_at, odd_at, 0,
    )
    n = 0
    store_edges = []
    for side, blocks in enumerate(edge_list(row_blocks)):
        begin = n
        for r, offset in blocks:
            k = place[r, offset + REACH]
            block = near[r, jnp.maximum(k, 0)]
            edge[n] = jnp.where(k >= 0, block, jnp.zeros_like(block))
            n += 1
        at = pl.ds(begin, n - begin)
        store_edges.append(pltpu.make_async_copy(edge.at[at], edge_out.at[at], edge_sems.at[side]))
        store_edges[-1].start()

    def wait_stores(r, carry):
        for copy in stores(r):
            copy.wait()
        return carry

    lax.fori_loop(0, row_blocks, wait_stores, 0)
    for copy in store_edges + [store_ct]:
        copy.wait()


def second_local_kernel(
    columns, x_in, near_in, p_in, s_in, p2_in, vectors,
    change_out, factor_out, new_s_out, parts,
    x, near, p, s, p2, change, factor, new_s, even, odd, even_at, odd_at,
    x_sem, near_sems, p_sems, s_sems, p2_sems, change_sems, factor_sems, new_s_sems,
):
    row_blocks, _, size, cols = near.shape
    total = row_blocks * lax.axis_size(AXIS)
    first = row_blocks * lax.axis_index(AXIS)
    load_x = pltpu.make_async_copy(x_in, x, x_sem)
    load_x.start()

    def rest(r):
        return [part(p_in, p, p_sems, r, 1), part(s_in, s, s_sems, r, 1), part(p2_in, p2, p2_sems, r, 1)]

    def stores(r):
        return [
            part(change, change_out, change_sems, r, 1),
            part(factor, factor_out, factor_sems, r, 1),
            part(new_s, new_s_out, new_s_sems, r, 1),
        ]

    def start_loads(r, carry):
        for copy in [part(near_in, near, near_sems, r, 1)] + rest(r):
            copy.start()
        return carry

    lax.fori_loop(0, row_blocks, start_loads, 0)
    load_x.wait()

    def finish(r, product, carry):
        errors, areas = carry
        before, now, start = p[r], p2[r], s[r]
        rows = vectors[r].T
        state_a = jnp.exp(-start) - jnp.exp(before)
        velocity = jnp.exp(now)
        state_b = jnp.exp(-(start + step_size * state_a)) - velocity
        rate, scale = known_rates(velocity, state_b, product, rows)
        change[r] = half_step * rate - (half_step / step_size) * (now - before)
        factor[r] = half_step * scale
        new_s[r] = start + half_step * (state_a + state_b)
        state_error = (half_step / error_scale) * (state_b - state_a)
        weight = jnp.broadcast_to(rows[:, 4:5], (size, cols))
        weighted = weight * (state_error * state_error)
        errors += jnp.sum(weighted.reshape(size // 8, 8, cols), axis=0)
        areas += jnp.sum(weight.reshape(size // 8, 8, cols), axis=0)
        for copy in stores(r):
            copy.start()
        return errors, areas

    zero = jnp.zeros((8, cols), F32)
    errors, areas = two_stage(
        row_blocks,
        lambda r, at: find_columns(columns, at, r, row_blocks, total, first),
        lambda r: part(near_in, near, near_sems, r, 1).wait(),
        lambda r: [copy.wait() for copy in rest(r)],
        lambda r, at: near_product(near, x, at, r),
        finish, even, odd, even_at, odd_at, (zero, zero),
    )
    parts[0] = errors
    parts[1] = areas

    def wait_stores(r, carry):
        for copy in stores(r):
            copy.wait()
        return carry

    lax.fori_loop(0, row_blocks, wait_stores, 0)


def couple(me, got, levels):
    devices = got.shape[0]
    sums = []
    for level in range(levels):
        total = got[me ^ (1 << level)].astype(F32)
        for m in range((1 << level) + 1, min(2 << level, devices)):
            total += got[me ^ m].astype(F32)
        sums.append(total.astype(BF16))
    return jnp.concatenate(sums, axis=0)


def row_order(row_blocks, chunks):
    group = row_blocks // chunks
    inner = [
        c for c in range(chunks) if c * group >= REACH and (c + 1) * group <= row_blocks - REACH
    ]
    return inner + [c for c in range(chunks) if c not in inner]


def outer_terms(coupled, coupling_t, halo, edge, r):
    row_blocks, _, _ = coupling_t.shape
    left, right = edge_rows(row_blocks)
    lhs, rhs = [coupling_t[r]], [coupled]
    n = 0
    for row, low in left:
        for t in range(low, REACH):
            if row == r:
                lhs.append(edge[n])
                rhs.append(halo[t])
            n += 1
    for row, count in right:
        for t in range(count):
            if row == r:
                lhs.append(edge[n])
                rhs.append(halo[REACH + t])
            n += 1
    return jnp.dot(
        jnp.concatenate(lhs, axis=1), jnp.concatenate(rhs, axis=0), preferred_element_type=F32
    )


def place_halo(me, got_a, got_b, halo):
    odd = lax.rem(me, 2)
    at_a = (1 - odd) * REACH
    at_b = odd * REACH
    for t in range(REACH):
        halo[at_a + t] = got_a[t]
        halo[at_b + t] = got_b[t]


def run_rows(order, loads, outer, row, done, start):
    ahead = 4
    for copy in outer[:1]:
        copy.start()
    for c in order[:ahead]:
        for copy in loads(c):
            copy.start()
        if c == order[0]:
            for copy in outer[1:]:
                copy.start()
    start()
    for n, c in enumerate(order):
        if n == 0:
            outer[0].wait()
        if n == 2:
            for copy in outer[1:]:
                copy.wait()
        for copy in loads(c):
            copy.wait()
        if n + ahead < len(order):
            for copy in loads(order[n + ahead]):
                copy.start()
        row(c)
        done(c)


def middle_kernel(
    got_a, got_b, got, edge_in, ct_in, basis_in, known_in, factor_in,
    p2_out, x_out, slots_out, a_out, b_out,
    halo, edge, coupling_t, basis, known, factor, p2, x, slots, coupled,
    outer_sems, known_sems, factor_sems, p2_sems, x_sem, send_sems,
):
    row_blocks, size, cols = known.shape
    chunks = known_sems.shape[0]
    group = row_blocks // chunks
    me = lax.axis_index(AXIS)
    order = row_order(row_blocks, chunks)
    outer = [
        pltpu.make_async_copy(ct_in, coupling_t, outer_sems.at[0]),
        pltpu.make_async_copy(edge_in, edge, outer_sems.at[1]),
        pltpu.make_async_copy(basis_in, basis, outer_sems.at[2]),
    ]

    def loads(c):
        return [part(known_in, known, known_sems, c, group), part(factor_in, factor, factor_sems, c, group)]

    def start():
        coupled[...] = couple(me, got, basis.shape[0] // got.shape[1])
        place_halo(me, got_a, got_b, halo)
        x[row_blocks] = jnp.zeros((size, cols), BF16)

    def row(c):
        for r in range(c * group, (c + 1) * group):
            value = known[r] - factor[r] * outer_terms(coupled[...], coupling_t, halo, edge, r)
            p2[r] = value
            x[r] = jnp.exp(value).astype(BF16)

    def done(c):
        part(p2, p2_out, p2_sems, c, group).start()

    run_rows(order, loads, outer, row, done, start)
    send = send_copies(me, x, slots, slots_out, a_out, b_out, send_sems)
    send.append(pltpu.make_async_copy(x, x_out, x_sem))
    for copy in send[1:]:
        copy.start()
    total = jnp.dot(
        basis[...], x[:row_blocks].reshape(row_blocks * size, cols), preferred_element_type=F32
    )
    fill_slots(me, total, slots)
    send[0].start()
    for copy in send + [part(p2, p2_out, p2_sems, c, group) for c in range(chunks)]:
        copy.wait()


def close_kernel(
    got_a, got_b, got, edge_in, ct_in, p2_in, change_in, factor_in, vectors, parts_in,
    new_p_out, parts_out,
    halo, edge, coupling_t, p2, change, factor, new_p, coupled,
    outer_sems, p2_sems, change_sems, factor_sems, new_p_sems,
):
    row_blocks, size, cols = change.shape
    chunks = change_sems.shape[0]
    group = row_blocks // chunks
    me = lax.axis_index(AXIS)
    order = row_order(row_blocks, chunks)
    outer = [
        pltpu.make_async_copy(ct_in, coupling_t, outer_sems.at[0]),
        pltpu.make_async_copy(edge_in, edge, outer_sems.at[1]),
    ]

    def loads(c):
        return [
            part(change_in, change, change_sems, c, group),
            part(factor_in, factor, factor_sems, c, group),
            part(p2_in, p2, p2_sems, c, group),
        ]

    def start():
        coupled[...] = couple(me, got, coupling_t.shape[2] // got.shape[1])
        place_halo(me, got_a, got_b, halo)

    errors = [parts_in[0]]

    def row(c):
        for r in range(c * group, (c + 1) * group):
            move = change[r] - factor[r] * outer_terms(coupled[...], coupling_t, halo, edge, r)
            new_p[r] = p2[r] + move
            rate_error = (1.0 / error_scale) * move
            weighted = vectors[r].T[:, 4:5] * (rate_error * rate_error)
            errors[0] += jnp.sum(weighted.reshape(size // 8, 8, cols), axis=0)

    def done(c):
        part(new_p, new_p_out, new_p_sems, c, group).start()

    run_rows(order, loads, outer, row, done, start)
    both = jnp.concatenate(
        [jnp.sum(errors[0], axis=0, keepdims=True), jnp.sum(parts_in[1], axis=0, keepdims=True)], axis=0
    )
    for j in range(parts_out.shape[0]):
        parts_out[j] = both
    for c in range(chunks):
        part(new_p, new_p_out, new_p_sems, c, group).wait()


def exchange(side_a, side_b, slots):
    count = lax.axis_size(AXIS)
    got_a = lax.ppermute(side_a, AXIS, [(i, i ^ 1) for i in range(count)])
    pairs = [(i, (i - 1) % count if i % 2 == 0 else (i + 1) % count) for i in range(count)]
    got_b = lax.ppermute(side_b, AXIS, pairs)
    got = lax.all_to_all(slots, AXIS, 0, 0)
    return got_a, got_b, got


def on_device(
    log_rate,
    log_state,
    near_blocks,
    near_columns,
    far_basis,
    far_coupling,
    self_stiffness,
    plate_rate,
    direct_effect,
    evolution_effect,
    triangle_area,
):
    rows, cols = log_rate.shape
    row_blocks, near_count, size, _ = near_blocks.shape
    levels, rank, _ = far_basis.shape
    devices = lax.axis_size(AXIS)
    p = log_rate.reshape(row_blocks, size, cols)
    s = log_state.reshape(row_blocks, size, cols)
    basis = far_basis.reshape(levels * rank, rows)
    coupling = far_coupling.reshape(levels * rank, rows)
    stiff, plate, direct, evolve, area = (
        v.reshape(row_blocks, size)
        for v in (self_stiffness, plate_rate, direct_effect, evolution_effect, triangle_area)
    )
    edges = sum(len(blocks) for blocks in edge_list(row_blocks))
    state = ((row_blocks, size, cols), F32)
    x_kind = ((row_blocks + 1, size, cols), BF16)
    slots_kind = ((devices, rank, cols), BF16)
    side_kind = ((REACH, size, cols), BF16)
    edge_kind = ((edges, size, size), BF16)
    ct_kind = ((row_blocks, size, levels * rank), BF16)
    basis_kind = ((levels * rank, rows), BF16)
    near_kind = (near_blocks.shape, BF16)
    halo_kind = ((2 * REACH, size, cols), BF16)
    chunks = 8 if row_blocks % 8 == 0 else row_blocks
    loads = 4 if row_blocks % 4 == 0 else row_blocks
    near_flops = 2 * rows * near_count * size * cols

    def vmem(*kinds):
        return [pltpu.VMEM(shape, dtype) for shape, dtype in kinds]

    small = pltpu.CompilerParams(vmem_limit_bytes=40 * 1024 * 1024)
    tiles_kind = ((row_blocks, 8, size), F32)
    coupled_kind = ((levels * rank, cols), BF16)
    product_kind = ((size, cols), F32)
    picked = [pltpu.SMEM((near_count,), jnp.int32)] * 2

    x, slots, side_a, side_b, vectors = pl.pallas_call(
        open_kernel,
        out_shape=in_hbm(x_kind, slots_kind, side_kind, side_kind) + like(tiles_kind),
        in_specs=[PLAIN, PLAIN] + [WHOLE] * 5,
        out_specs=(PLAIN,) * 4 + (WHOLE,),
        scratch_shapes=vmem(state, basis_kind, x_kind, slots_kind)
        + [SEMS((loads,)), SEMS(()), SEMS(()), SEMS((3,))],
        name="open",
    )(*hbm(p, basis), stiff, plate, direct, evolve, area)

    got_a, got_b, got = exchange(side_a, side_b, slots)
    known, factor, edge, coupling_t = pl.pallas_call(
        first_local_kernel,
        out_shape=in_hbm(state, state, edge_kind, ct_kind),
        in_specs=[SCALARS] + [PLAIN] * 4 + [WHOLE] * 2,
        out_specs=(PLAIN,) * 4,
        scratch_shapes=vmem(
            x_kind, near_kind, state, state, state, state, edge_kind, ct_kind, product_kind, product_kind
        )
        + picked
        + [pltpu.SMEM((row_blocks, 2 * REACH + 1), jnp.int32), SEMS(())]
        + [SEMS((row_blocks,))] * 5
        + [SEMS((2,)), SEMS(())],
        cost_estimate=cost(near_flops, near_blocks.size * 2),
        name="local_one",
    )(near_columns, *hbm(x, near_blocks, p, s), coupling, vectors)

    p2, x, slots, side_a, side_b = pl.pallas_call(
        middle_kernel,
        out_shape=in_hbm(state, x_kind, slots_kind, side_kind, side_kind),
        in_specs=[WHOLE] * 3 + [PLAIN] * 5,
        out_specs=(PLAIN,) * 5,
        scratch_shapes=vmem(
            halo_kind, edge_kind, ct_kind, basis_kind, state, state, state, x_kind, slots_kind, coupled_kind
        )
        + [SEMS((3,)), SEMS((chunks,)), SEMS((chunks,)), SEMS((chunks,)), SEMS(()), SEMS((3,))],
        compiler_params=small,
        name="middle",
    )(got_a, got_b, got, *hbm(edge, coupling_t, basis, known, factor))

    got_a, got_b, got = exchange(side_a, side_b, slots)
    change, factor, new_s, parts = pl.pallas_call(
        second_local_kernel,
        out_shape=in_hbm(state, state, state) + like(((2, 8, cols), F32)),
        in_specs=[SCALARS] + [PLAIN] * 5 + [WHOLE],
        out_specs=(PLAIN,) * 3 + (WHOLE,),
        scratch_shapes=vmem(
            x_kind, near_kind, state, state, state, state, state, state, product_kind, product_kind
        )
        + picked
        + [SEMS(())]
        + [SEMS((row_blocks,))] * 7,
        cost_estimate=cost(near_flops, near_blocks.size * 2),
        name="local_two",
    )(near_columns, *hbm(x, near_blocks, p, s, p2), vectors)

    new_p, parts = pl.pallas_call(
        close_kernel,
        out_shape=in_hbm(state) + like(((devices, 2, cols), F32)),
        in_specs=[WHOLE] * 3 + [PLAIN] * 5 + [WHOLE] * 2,
        out_specs=(PLAIN, WHOLE),
        scratch_shapes=vmem(halo_kind, edge_kind, ct_kind, state, state, state, state, coupled_kind)
        + [SEMS((2,))]
        + [SEMS((chunks,))] * 4,
        compiler_params=small,
        name="close",
    )(got_a, got_b, got, *hbm(edge, coupling_t, p2, change, factor), vectors, parts)

    totals = lax.all_to_all(parts, AXIS, 0, 0).sum(axis=0)
    error_norm = jnp.sqrt(totals[0] / totals[1] + 1e-06)
    return new_p.reshape(rows, cols), new_s.reshape(rows, cols), error_norm


def solution(mesh):
    split = P(("member", "patch"))
    in_specs = (
        P(("member", "patch"), None),
        P(("member", "patch"), None),
        P(("member", "patch"), None, None, None),
        P(("member", "patch"), None),
        P("member", None, "patch"),
        P("member", None, "patch"),
        split,
        split,
        split,
        split,
        split,
    )
    out_specs = (P(("member", "patch"), None), P(("member", "patch"), None), P("member"))
    return jax.shard_map(
        on_device, mesh=mesh, in_specs=in_specs, out_specs=out_specs, check_vma=False
    )
```

time: 71.5 us -> 62.7 us (0.88)
  Pallas kernels: 37.1 us -> 30.5 us
  blocking collectives: 9.94 us -> 9.07 us
  local copies, waits for them, and re-layouts: 1.51 us -> 0.7 us
    pallas_call x5, Pallas kernels: 37.1 us -> 30.5 us  [the longest x1 8.6 us: on_device(): pl.pallas_call(second_local_kernel, out_shape=in_hbm(state, state, state)...]
    all_to_all x1, blocking collectives: 9.94 us -> 9.07 us  [on_device(): totals = lax.all_to_all(parts, AXIS, 0, 0).sum(axis=0)]
    unnamed x12 -> x4, local copies, waits for them, and re-layouts: 1.51 us -> 0.7 us
  transfers between devices with their start and end apart: 6 -> 6, of which waited for: 0 -> 0; matrix products, arithmetic and copies ran while one was open for 0% -> 0% of each run, Pallas kernels for 28% -> 27%
where the time goes in v3:
time: 62.7 us; the launch traced here: 62.1 us
  Pallas kernels  30.5 us (49%)
  starting transfers between devices  20.5 us (33%)
  blocking collectives  9.07 us (14%)
  between operations  0.76 us (1%)
  local copies, waits for them, and re-layouts  0.7 us (1%)
    all_to_all x2, starting transfers between devices, exchange(): got = lax.all_to_all(slots, AXIS, 0, 0)  11.1 us
    all_to_all x1, blocking collectives, on_device(): totals = lax.all_to_all(parts, AXIS, 0, 0).sum(axis=0)  9.07 us
    ppermute x2, starting transfers between devices, exchange(): got_b = lax.ppermute(side_b, AXIS, pairs)  8.75 us
    pallas_call x1, Pallas kernels, on_device(): pl.pallas_call(second_local_kernel, out_shape=in_hbm(state, state, state)...  8.6 us
    pallas_call x1, Pallas kernels, on_device(): pl.pallas_call(first_local_kernel, out_shape=in_hbm(state, state, edge_ki...  8.12 us
    pallas_call x1, Pallas kernels, on_device(): pl.pallas_call(middle_kernel, out_shape=in_hbm(state, x_kind, slots_kind,...  4.86 us
    pallas_call x1, Pallas kernels, on_device(): pl.pallas_call(close_kernel, out_shape=in_hbm(state) + like(((devices, 2,...  4.65 us
    pallas_call x1, Pallas kernels, on_device(): pl.pallas_call(open_kernel, out_shape=in_hbm(x_kind, slots_kind, side_kin...  4.23 us
  transfers between devices with their start and end apart: 6, of which 0 were waited for; matrix products, arithmetic and copies ran while one was open for 0% of the time, Pallas kernels for 27%

profile of v3, /device:TPU:0, one launch (start us, length us, event | category | flops | bytes accessed | tf_op | source)
XLA Modules:
  0.0 62.1 jit_solution(2792354105855409848)
XLA Ops:
  0.6 4.2 %open.1 = (bf16[17,128,128]{2,1,0:T(8,128)(2,1)}, bf16[16,32,128]{2,1,0:T(8,128)(2,1)}, bf16[6,128,128]{2,1,0:T(8,128)(2,1)}, bf16[6,128,128]{2,1,0:T(8,128)(2,1)}, f32[16,8,128]{2,1,0:T(8,128)}) custom-call(f32[16,128,128]{2,1,0:T(8,128)} %bitcast.13, bf16[128,2048]{1,0:T(8,128)(2,1)} %bitcast.18, f32[16,128]{1,0:T(8,128)} %bitcast.21, f32[16,128]{1,0:T(8,128)} %bitcast.22, ...), custom_call_target="tpu_custom_call" | custom-call | tf_op jit(solution)/shard_map/open/pallas_call | solution.py:547
  4.9 7.4 %all-to-all-start = ((bf16[16,32,128]{2,1,0:T(8,128)(2,1)}), bf16[16,32,128]{2,1,0:T(8,128)(2,1)S(1)}, u32[]{:S(2)}, u32[]{:S(2)}) async-start(bf16[16,32,128]{2,1,0:T(8,128)(2,1)} %get-tuple-element.25), calls=%async_computation | async-start | bytes 262144 | tf_op jit(solution)/shard_map/all_to_all | solution.py:495
  12.3 0.4 collective-permute-start
  12.7 4.3 %collective-permute-start.1 = (bf16[6,128,128]{2,1,0:T(8,128)(2,1)}, bf16[6,128,128]{2,1,0:T(8,128)(2,1)S(1)}, u32[]{:S(2)}, u32[]{:S(2)}) collective-permute-start(bf16[6,128,128]{2,1,0:T(8,128)(2,1)} %get-tuple-element.24), channel_id=1, source_target_pairs={{0,15},{1,2},{2,1},{3,4},{4,3},{5,6},{6,5},{7,8},{8,7},{9,10},{10,... | collective-permute-start | bytes 589832 | tf_op jit(solution)/shard_map/ppermute | solution.py:494
  17.1 8.1 %local_one.1 = (f32[16,128,128]{2,1,0:T(8,128)}, f32[16,128,128]{2,1,0:T(8,128)}, bf16[42,128,128]{2,1,0:T(8,128)(2,1)}, bf16[16,128,128]{2,1,0:T(8,128)(2,1)}) custom-call(s32[16,12]{1,0:T(8,128)} %columns.3, bf16[17,128,128]{2,1,0:T(8,128)(2,1)} %get-tuple-element.26.x_in, bf16[16,12,128,128]{3,2,1,0:T(8,128)(2,1)} %near_in.3, f32[16,128,128]{2,1,0:T(8,128)} %bitcast.14, ...), custom_call_target="tpu_custom_call" | custom-call | flops 805306368 | bytes 6291456 | tf_op jit(solution)/shard_map/local_one/pallas_call | solution.py:558
  25.2 0.0 collective-permute-done.got_a
  25.2 0.0 collective-permute-done.1.got_b
  25.2 0.0 all-to-all-done.got
  25.2 4.9 %middle.1 = (f32[16,128,128]{2,1,0:T(8,128)}, bf16[17,128,128]{2,1,0:T(8,128)(2,1)}, bf16[16,32,128]{2,1,0:T(8,128)(2,1)}, bf16[6,128,128]{2,1,0:T(8,128)(2,1)}, bf16[6,128,128]{2,1,0:T(8,128)(2,1)}) custom-call(bf16[6,128,128]{2,1,0:T(8,128)(2,1)S(1)} %collective-permute-done.got_a, bf16[6,128,128]{2,1,0:T(8,128)(2,1)S(1)} %collective-permute-done.1.got_b, ...), custom_call_target="tpu_custom_call" | custom-call | tf_op jit(solution)/shard_map/middle/pallas_call | solution.py:574
  30.1 0.0 copy-start
  30.1 3.7 %all-to-all-start.1 = ((bf16[16,32,128]{2,1,0:T(8,128)(2,1)}), bf16[16,32,128]{2,1,0:T(8,128)(2,1)S(1)}, u32[]{:S(2)}, u32[]{:S(2)}) async-start(bf16[16,32,128]{2,1,0:T(8,128)(2,1)} %get-tuple-element.34), calls=%async_computation.1 | async-start | bytes 262144 | tf_op jit(solution)/shard_map/all_to_all | solution.py:495
  33.8 0.3 collective-permute-start.2
  34.0 4.4 %collective-permute-start.3 = (bf16[6,128,128]{2,1,0:T(8,128)(2,1)}, bf16[6,128,128]{2,1,0:T(8,128)(2,1)S(1)}, u32[]{:S(2)}, u32[]{:S(2)}) collective-permute-start(bf16[6,128,128]{2,1,0:T(8,128)(2,1)} %get-tuple-element.33), channel_id=1, source_target_pairs={{0,15},{1,2},{2,1},{3,4},{4,3},{5,6},{6,5},{7,8},{8,7},{9,10},{10,... | collective-permute-start | bytes 589832 | tf_op jit(solution)/shard_map/ppermute | solution.py:494
  38.5 8.6 %local_two.1 = (f32[16,128,128]{2,1,0:T(8,128)}, f32[16,128,128]{2,1,0:T(8,128)}, f32[16,128,128]{2,1,0:T(8,128)}, f32[2,8,128]{2,1,0:T(8,128)}) custom-call(s32[16,12]{1,0:T(8,128)} %columns.3, bf16[17,128,128]{2,1,0:T(8,128)(2,1)} %get-tuple-element.36.x_in, bf16[16,12,128,128]{3,2,1,0:T(8,128)(2,1)} %near_in.3, f32[16,128,128]{2,1,0:T(8,128)} %bitcast.15, ...), custom_call_target="tpu_custom_call" | custom-call | flops 805306368 | bytes 6291456 | tf_op jit(solution)/shard_map/local_two/pallas_call | solution.py:588
  47.1 0.0 collective-permute-done.2.got_a
  47.1 0.0 collective-permute-done.3.got_b
  47.1 0.0 all-to-all-done.1.got
  47.1 0.0 copy-done
  47.1 0.0 copy-start.1
  47.1 0.7 %copy-done.1 = f32[2,8,128]{2,1,0:T(8,128)S(1)} copy-done((f32[2,8,128]{2,1,0:T(8,128)S(1)}, f32[2,8,128]{2,1,0:T(8,128)}, u32[]{:S(2)}) %copy-start.1) | copy-done | bytes 8216
  47.8 4.7 %close.1 = (f32[16,128,128]{2,1,0:T(8,128)}, f32[16,2,128]{2,1,0:T(2,128)S(1)}) custom-call(bf16[6,128,128]{2,1,0:T(8,128)(2,1)S(1)} %collective-permute-done.2.got_a, bf16[6,128,128]{2,1,0:T(8,128)(2,1)S(1)} %collective-permute-done.3.got_b, bf16[16,32,128]{2,1,0:T(8,128)(2,1)S(1)} %all-to-all-done.1.got, bf16[42,128,128]{2,1,0:T(8,128)(2,1)} %get-tuple-element.28.edge_in, ...), custom_call_target="tpu_custom_call" | custom-call | tf_op jit(solution)/shard_map/close/pallas_call | solution.py:603
  52.5 9.1 %all_to_all.15 = f32[16,2,128]{2,1,0:T(2,128)S(1)} all-to-all(f32[16,2,128]{2,1,0:T(2,128)S(1)} %get-tuple-element.42), channel_id=1, replica_groups=mesh['member'=2,'patch'=16] {'patch'}, dimensions={0} | all-to-all | bytes 32768 | tf_op jit(solution)/shard_map/all_to_all | solution.py:615
  61.6 0.5 sqrt_bitcast_fusion
  (1 shorter events, 0.0 us)
Async XLA Ops:
  4.9 20.3 %all-to-all-start = ((bf16[16,32,128]{2,1,0:T(8,128)(2,1)}), bf16[16,32,128]{2,1,0:T(8,128)(2,1)S(1)}, u32[]{:S(2)}, u32[]{:S(2)}) async-start(bf16[16,32,128]{2,1,0:T(8,128)(2,1)} %get-tuple-element.25), calls=%async_computation | async-start | bytes 262144 | tf_op jit(solution)/shard_map/all_to_all | solution.py:495
  12.3 12.9 %collective-permute-start = (bf16[6,128,128]{2,1,0:T(8,128)(2,1)}, bf16[6,128,128]{2,1,0:T(8,128)(2,1)S(1)}, u32[]{:S(2)}, u32[]{:S(2)}) collective-permute-start(bf16[6,128,128]{2,1,0:T(8,128)(2,1)} %get-tuple-element.23), channel_id=1, source_target_pairs={{0,1},{1,0},{2,3},{3,2},{4,5},{5,4},{6,7},{7,6},{8,9},{9,8},{10,11... | collective-permute-start | bytes 589832 | tf_op jit(solution)/shard_map/ppermute | solution.py:492
  12.7 12.5 %collective-permute-start.1 = (bf16[6,128,128]{2,1,0:T(8,128)(2,1)}, bf16[6,128,128]{2,1,0:T(8,128)(2,1)S(1)}, u32[]{:S(2)}, u32[]{:S(2)}) collective-permute-start(bf16[6,128,128]{2,1,0:T(8,128)(2,1)} %get-tuple-element.24), channel_id=1, source_target_pairs={{0,15},{1,2},{2,1},{3,4},{4,3},{5,6},{6,5},{7,8},{8,7},{9,10},{10,... | collective-permute-start | bytes 589832 | tf_op jit(solution)/shard_map/ppermute | solution.py:494
  30.1 17.0 %copy-start = (f32[16,8,128]{2,1,0:T(8,128)S(1)}, f32[16,8,128]{2,1,0:T(8,128)}, u32[]{:S(2)}) copy-start(f32[16,8,128]{2,1,0:T(8,128)} %get-tuple-element.27.vectors) | copy-start | bytes 196612
  30.1 17.0 %all-to-all-start.1 = ((bf16[16,32,128]{2,1,0:T(8,128)(2,1)}), bf16[16,32,128]{2,1,0:T(8,128)(2,1)S(1)}, u32[]{:S(2)}, u32[]{:S(2)}) async-start(bf16[16,32,128]{2,1,0:T(8,128)(2,1)} %get-tuple-element.34), calls=%async_computation.1 | async-start | bytes 262144 | tf_op jit(solution)/shard_map/all_to_all | solution.py:495
  33.8 13.3 %collective-permute-start.2 = (bf16[6,128,128]{2,1,0:T(8,128)(2,1)}, bf16[6,128,128]{2,1,0:T(8,128)(2,1)S(1)}, u32[]{:S(2)}, u32[]{:S(2)}) collective-permute-start(bf16[6,128,128]{2,1,0:T(8,128)(2,1)} %get-tuple-element.32), channel_id=1, source_target_pairs={{0,1},{1,0},{2,3},{3,2},{4,5},{5,4},{6,7},{7,6},{8,9},{9,8},{10,11... | collective-permute-start | bytes 589832 | tf_op jit(solution)/shard_map/ppermute | solution.py:492
  34.0 13.0 %collective-permute-start.3 = (bf16[6,128,128]{2,1,0:T(8,128)(2,1)}, bf16[6,128,128]{2,1,0:T(8,128)(2,1)S(1)}, u32[]{:S(2)}, u32[]{:S(2)}) collective-permute-start(bf16[6,128,128]{2,1,0:T(8,128)(2,1)} %get-tuple-element.33), channel_id=1, source_target_pairs={{0,15},{1,2},{2,1},{3,4},{4,3},{5,6},{6,5},{7,8},{8,7},{9,10},{10,... | collective-permute-start | bytes 589832 | tf_op jit(solution)/shard_map/ppermute | solution.py:494
  47.1 0.7 %copy-start.1 = (f32[2,8,128]{2,1,0:T(8,128)S(1)}, f32[2,8,128]{2,1,0:T(8,128)}, u32[]{:S(2)}) copy-start(f32[2,8,128]{2,1,0:T(8,128)} %get-tuple-element.39.parts_in) | copy-start | bytes 24580

commit v4 on v3

v4 whole, which is shorter than its diff:
```python
import jax
import jax.numpy as jnp
from jax import lax
from jax.experimental import pallas as pl
from jax.experimental.pallas import tpu as pltpu
from jax.sharding import PartitionSpec as P


REACH = 6

step_size = 0.1
damping = 0.5
error_scale = 0.01
half_step = 0.5 * step_size

AXIS = "patch"
F32 = jnp.float32
BF16 = jnp.bfloat16
PLAIN = pl.BlockSpec(memory_space=pltpu.HBM)
WHOLE = pl.BlockSpec(memory_space=pltpu.VMEM)
SCALARS = pl.BlockSpec(memory_space=pltpu.SMEM)
SEMS = pltpu.SemaphoreType.DMA


def cost(flops, moved, exps=0):
    return pl.CostEstimate(flops=flops, bytes_accessed=moved, transcendentals=exps)


def in_hbm(*shapes):
    return tuple(pltpu.HBM(shape, dtype) for shape, dtype in shapes)


def hbm(*arrays):
    return tuple(pltpu.with_memory_space_constraint(v, pltpu.HBM) for v in arrays)


def like(*shapes):
    return tuple(jax.ShapeDtypeStruct(shape, dtype) for shape, dtype in shapes)


def part(src, dst, sems, c, group):
    at = pl.ds(c * group, group)
    return pltpu.make_async_copy(src.at[at], dst.at[at], sems.at[c])


def pair_columns(row_blocks, pair):
    reached = range((2 * pair - REACH) // 2, (2 * pair + 1 + REACH) // 2 + 1)
    count = row_blocks // 2
    return (
        [c for c in reached if c < 0],
        [c for c in reached if 0 <= c < count],
        [c for c in reached if c >= count],
    )


def edge_tiles(row_blocks):
    tiles = []
    for pair in range(row_blocks // 2):
        left, _, right = pair_columns(row_blocks, pair)
        tiles += [(pair, c) for c in left + right]
    return tiles


def project(basis, x):
    row_blocks, size, cols = x.shape
    return jnp.dot(basis[...], x[...].reshape(row_blocks * size, cols), preferred_element_type=F32)


def fill_slots(me, projected, slots):
    devices, rank, _ = slots.shape
    for m in range(devices):
        level = max(m.bit_length() - 1, 0)
        slots[me ^ m] = projected[level * rank : (level + 1) * rank].astype(slots.dtype)


def send_copies(me, x, slots, slots_out, a_out, b_out, sems):
    row_blocks = x.shape[0]
    odd = lax.rem(me, 2)
    start_a = (1 - odd) * (row_blocks - REACH)
    start_b = odd * (row_blocks - REACH)
    return [
        pltpu.make_async_copy(slots, slots_out, sems.at[0]),
        pltpu.make_async_copy(x.at[pl.ds(start_a, REACH)], a_out, sems.at[1]),
        pltpu.make_async_copy(x.at[pl.ds(start_b, REACH)], b_out, sems.at[2]),
    ]


def open_kernel(
    p_in, basis_in, x_out, slots_out, a_out, b_out,
    p, basis, x, slots, p_sems, x_sem, basis_sem, send_sems,
):
    row_blocks, _, _ = p.shape
    chunks = p_sems.shape[0]
    group = row_blocks // chunks
    me = lax.axis_index(AXIS)
    load_basis = pltpu.make_async_copy(basis_in, basis, basis_sem)
    for c in range(chunks):
        part(p_in, p, p_sems, c, group).start()
    load_basis.start()
    for c in range(chunks):
        part(p_in, p, p_sems, c, group).wait()
        rows = slice(c * group, (c + 1) * group)
        x[rows] = jnp.exp(p[rows]).astype(BF16)
    send = send_copies(me, x, slots, slots_out, a_out, b_out, send_sems)
    send.append(pltpu.make_async_copy(x, x_out, x_sem))
    for copy in send[1:]:
        copy.start()
    load_basis.wait()
    fill_slots(me, project(basis, x), slots)
    send[0].start()
    for copy in send:
        copy.wait()


def find_blocks(columns, where):
    row_blocks, near_count = columns.shape
    total = row_blocks * lax.axis_size(AXIS)
    first = row_blocks * lax.axis_index(AXIS)

    def row(r, carry):
        for o in range(2 * REACH + 1):
            where[r, o] = row_blocks * near_count
        for k in range(near_count):
            offset = columns[r, k] - first - r
            offset = jnp.where(offset > REACH, offset - total, offset)
            offset = jnp.where(offset < -REACH, offset + total, offset)
            where[r, offset + REACH] = r * near_count + k
        return carry

    lax.fori_loop(0, row_blocks, row, 0)


def near_block(near, where, r, c):
    if abs(c - r) > REACH:
        return jnp.zeros(near.shape[1:], near.dtype)
    return near[where[r, c - r + REACH]]


def near_product(near, x, where, pair):
    row_blocks, _, cols = x.shape
    own = pair_columns(row_blocks, pair)[1]
    lhs = [
        jnp.concatenate([near_block(near, where, r, c) for c in range(2 * own[0], 2 * own[-1] + 2)], axis=1)
        for r in (2 * pair, 2 * pair + 1)
    ]
    rhs = x[2 * own[0] : 2 * own[-1] + 2].reshape(-1, cols)
    return jnp.dot(jnp.concatenate(lhs, axis=0), rhs, preferred_element_type=F32)


def strips(size):
    step = 32 if size % 32 == 0 else size
    return [slice(i, i + step) for i in range(0, size, step)]


def columns_of(table, r, at):
    return [table[at, 8 * r + q : 8 * r + q + 1] for q in range(5)]


def known_rates(velocity, state, near_term, rows):
    stiff, plate, direct, evolve, _ = rows
    factor = 1.0 / (direct + damping * velocity)
    return (stiff * (plate - velocity) - near_term - evolve * state) * factor, factor


def in_pairs(pairs, wait, product, finish, store):
    wait(0)
    product(0)
    for pair in range(pairs):
        if pair + 1 < pairs:
            wait(pair + 1)
            product(pair + 1)
        finish(pair)
        store(pair)


def first_local_kernel(
    columns, x_in, near_in, p_in, s_in, coupling_in, stiff_in, plate_in, direct_in, evolve_in, area_in,
    known_out, factor_out, edge_out, coupling_t_out, table_out,
    x, near, p, s, coupling, stiff, plate, direct, evolve, area, known, factor, edge, coupling_t, table, products,
    where, x_sem, near_sems, p_sems, s_sems, coupling_sem, vector_sems, known_sems, factor_sems, rest_sems,
):
    row_blocks, size, _ = x.shape
    pairs = row_blocks // 2
    span = (near.shape[0] - 1) // pairs
    vectors = (stiff, plate, direct, evolve, area)
    load_x = pltpu.make_async_copy(x_in, x, x_sem)
    load_coupling = pltpu.make_async_copy(coupling_in, coupling, coupling_sem)
    load_vectors = [
        pltpu.make_async_copy(src, dst, vector_sems.at[q])
        for q, (src, dst) in enumerate(zip((stiff_in, plate_in, direct_in, evolve_in, area_in), vectors))
    ]

    def loads(c):
        return [part(near_in, near, near_sems, c, span), part(p_in, p, p_sems, c, 2), part(s_in, s, s_sems, c, 2)]

    def stores(c):
        return [part(known, known_out, known_sems, c, 2), part(factor, factor_out, factor_sems, c, 2)]

    for copy in load_vectors + [load_x] + loads(0) + [load_coupling]:
        copy.start()
    for c in range(1, pairs):
        for copy in loads(c):
            copy.start()
    near[near.shape[0] - 1] = jnp.zeros(near.shape[1:], near.dtype)
    find_blocks(columns, where)
    for copy in load_vectors:
        copy.wait()
    tiles = [
        jnp.concatenate([v[r : r + 1] for v in vectors + (area, area, area)], axis=0) for r in range(row_blocks)
    ]
    table[...] = jnp.concatenate(tiles, axis=0).T
    load_x.wait()

    def product(pair):
        products[pair] = near_product(near, x, where, pair)

    def finish(pair):
        for i in range(2):
            r = 2 * pair + i
            for at in strips(size):
                now = p[r, at]
                velocity = jnp.exp(now)
                state = jnp.exp(-s[r, at]) - velocity
                near_term = products[pair, i * size + at.start : i * size + at.stop]
                rate, scale = known_rates(velocity, state, near_term, columns_of(table, r, at))
                known[r, at] = now + step_size * rate
                factor[r, at] = step_size * scale

    in_pairs(
        pairs,
        lambda c: [copy.wait() for copy in loads(c)],
        product,
        finish,
        lambda c: [copy.start() for copy in stores(c)],
    )
    for n, (pair, c) in enumerate(edge_tiles(row_blocks)):
        for i in range(2):
            for j in range(2):
                edge[n, i * size : (i + 1) * size, j * size : (j + 1) * size] = near_block(
                    near, where, 2 * pair + i, 2 * c + j
                )
    load_coupling.wait()
    for r in range(row_blocks):
        coupling_t[r] = coupling[:, r * size : (r + 1) * size].T
    last = [
        pltpu.make_async_copy(edge, edge_out, rest_sems.at[0]),
        pltpu.make_async_copy(coupling_t, coupling_t_out, rest_sems.at[1]),
        pltpu.make_async_copy(table, table_out, rest_sems.at[2]),
    ]
    for copy in last:
        copy.start()
    for c in range(pairs):
        for copy in stores(c):
            copy.wait()
    for copy in last:
        copy.wait()


def second_local_kernel(
    columns, x_in, near_in, p_in, s_in, p2_in, table_in,
    change_out, factor_out, new_s_out, parts_out,
    x, near, p, s, p2, table, change, factor, new_s, parts, products,
    where, x_sem, near_sems, p_sems, s_sems, p2_sems, change_sems, factor_sems, new_s_sems, rest_sems,
):
    row_blocks, size, cols = x.shape
    pairs = row_blocks // 2
    span = (near.shape[0] - 1) // pairs
    load_x = pltpu.make_async_copy(x_in, x, x_sem)
    load_table = pltpu.make_async_copy(table_in, table, rest_sems.at[0])

    def loads(c):
        return [
            part(near_in, near, near_sems, c, span),
            part(p_in, p, p_sems, c, 2),
            part(s_in, s, s_sems, c, 2),
            part(p2_in, p2, p2_sems, c, 2),
        ]

    def stores(c):
        return [
            part(change, change_out, change_sems, c, 2),
            part(factor, factor_out, factor_sems, c, 2),
            part(new_s, new_s_out, new_s_sems, c, 2),
        ]

    load_x.start()
    load_table.start()
    for c in range(pairs):
        for copy in loads(c):
            copy.start()
    near[near.shape[0] - 1] = jnp.zeros(near.shape[1:], near.dtype)
    find_blocks(columns, where)
    load_x.wait()
    load_table.wait()
    errors = [jnp.zeros((8, cols), F32)]

    def product(pair):
        products[pair] = near_product(near, x, where, pair)

    def finish(pair):
        for i in range(2):
            r = 2 * pair + i
            for at in strips(size):
                rows = columns_of(table, r, at)
                before, now, start = p[r, at], p2[r, at], s[r, at]
                state_a = jnp.exp(-start) - jnp.exp(before)
                velocity = jnp.exp(now)
                state_b = jnp.exp(-(start + step_size * state_a)) - velocity
                near_term = products[pair, i * size + at.start : i * size + at.stop]
                rate, scale = known_rates(velocity, state_b, near_term, rows)
                change[r, at] = half_step * rate - (half_step / step_size) * (now - before)
                factor[r, at] = half_step * scale
                new_s[r, at] = start + half_step * (state_a + state_b)
                state_error = (half_step / error_scale) * (state_b - state_a)
                weighted = rows[4] * (state_error * state_error)
                errors[0] += jnp.sum(weighted.reshape(-1, 8, cols), axis=0)

    in_pairs(
        pairs,
        lambda c: [copy.wait() for copy in loads(c)],
        product,
        finish,
        lambda c: [copy.start() for copy in stores(c)],
    )
    parts[0] = errors[0]
    areas = jnp.zeros((size, 1), F32)
    for r in range(row_blocks):
        areas += table[:, 8 * r + 4 : 8 * r + 5]
    parts[1] = jnp.sum(jnp.broadcast_to(areas, (size, cols)).reshape(-1, 8, cols), axis=0)
    store_parts = pltpu.make_async_copy(parts, parts_out, rest_sems.at[1])
    store_parts.start()
    for c in range(pairs):
        for copy in stores(c):
            copy.wait()
    store_parts.wait()


def couple(me, got, levels):
    devices = got.shape[0]
    sums = []
    for level in range(levels):
        total = got[me ^ (1 << level)].astype(F32)
        for m in range((1 << level) + 1, min(2 << level, devices)):
            total += got[me ^ m].astype(F32)
        sums.append(total.astype(BF16))
    return jnp.concatenate(sums, axis=0)


def pair_order(row_blocks):
    edged = {pair for pair, _ in edge_tiles(row_blocks)}
    pairs = range(row_blocks // 2)
    return [c for c in pairs if c not in edged] + [c for c in pairs if c in edged]


def outer_terms(coupled, coupling_t, halo, edge, pair):
    row_blocks, size, rank = coupling_t.shape
    cols = halo.shape[2]
    lhs, rhs = [], []
    for n, (row_pair, c) in enumerate(edge_tiles(row_blocks)):
        if row_pair == pair:
            at = REACH + 2 * c if c < 0 else REACH + 2 * c - row_blocks
            lhs.append(edge[n])
            rhs.append(halo[at : at + 2].reshape(2 * size, cols))
    lhs.append(coupling_t[2 * pair : 2 * pair + 2].reshape(2 * size, rank))
    rhs.append(coupled)
    return jnp.dot(
        jnp.concatenate(lhs, axis=1), jnp.concatenate(rhs, axis=0), preferred_element_type=F32
    )


def place_halo(me, got_a, got_b, halo):
    odd = lax.rem(me, 2)
    at_a = (1 - odd) * REACH
    at_b = odd * REACH
    for t in range(REACH):
        halo[at_a + t] = got_a[t]
        halo[at_b + t] = got_b[t]


def run_rows(order, first_edged, loads, outer, row, done, start):
    ahead = 4
    for copy in outer[:1]:
        copy.start()
    for c in order[:ahead]:
        for copy in loads(c):
            copy.start()
        if c == order[0]:
            for copy in outer[1:]:
                copy.start()
    start()
    for n, c in enumerate(order):
        if n == 0:
            outer[0].wait()
        if n == first_edged:
            for copy in outer[1:]:
                copy.wait()
        for copy in loads(c):
            copy.wait()
        if n + ahead < len(order):
            for copy in loads(order[n + ahead]):
                copy.start()
        row(c)
        done(c)


def middle_kernel(
    got_a, got_b, got, edge_in, ct_in, basis_in, known_in, factor_in,
    p2_out, x_out, slots_out, a_out, b_out,
    halo, edge, coupling_t, basis, known, factor, p2, x, slots, coupled,
    outer_sems, known_sems, factor_sems, p2_sems, x_sem, send_sems,
):
    row_blocks, size, _ = known.shape
    chunks, group = row_blocks // 2, 2
    me = lax.axis_index(AXIS)
    order = pair_order(row_blocks)
    first_edged = order.index(0)
    outer = [
        pltpu.make_async_copy(ct_in, coupling_t, outer_sems.at[0]),
        pltpu.make_async_copy(edge_in, edge, outer_sems.at[1]),
        pltpu.make_async_copy(basis_in, basis, outer_sems.at[2]),
    ]

    def loads(c):
        return [part(known_in, known, known_sems, c, group), part(factor_in, factor, factor_sems, c, group)]

    def start():
        coupled[...] = couple(me, got, basis.shape[0] // got.shape[1])
        place_halo(me, got_a, got_b, halo)

    def row(c):
        terms = outer_terms(coupled[...], coupling_t, halo, edge, c)
        for i in range(2):
            r = 2 * c + i
            value = known[r] - factor[r] * terms[i * size : (i + 1) * size]
            p2[r] = value
            x[r] = jnp.exp(value).astype(BF16)

    def done(c):
        part(p2, p2_out, p2_sems, c, group).start()

    run_rows(order, first_edged, loads, outer, row, done, start)
    send = send_copies(me, x, slots, slots_out, a_out, b_out, send_sems)
    send.append(pltpu.make_async_copy(x, x_out, x_sem))
    for copy in send[1:]:
        copy.start()
    fill_slots(me, project(basis, x), slots)
    send[0].start()
    for copy in send + [part(p2, p2_out, p2_sems, c, group) for c in range(chunks)]:
        copy.wait()


def close_kernel(
    got_a, got_b, got, edge_in, ct_in, p2_in, change_in, factor_in, table_in, parts_in,
    new_p_out, parts_out,
    halo, edge, coupling_t, p2, change, factor, new_p, coupled, table, parts,
    outer_sems, p2_sems, change_sems, factor_sems, new_p_sems,
):
    row_blocks, size, cols = change.shape
    chunks, group = row_blocks // 2, 2
    me = lax.axis_index(AXIS)
    order = pair_order(row_blocks)
    first_edged = order.index(0)
    outer = [
        pltpu.make_async_copy(ct_in, coupling_t, outer_sems.at[0]),
        pltpu.make_async_copy(edge_in, edge, outer_sems.at[1]),
    ]
    small = [
        pltpu.make_async_copy(table_in, table, outer_sems.at[2]),
        pltpu.make_async_copy(parts_in, parts, outer_sems.at[3]),
    ]
    for copy in small:
        copy.start()

    def loads(c):
        return [
            part(change_in, change, change_sems, c, group),
            part(factor_in, factor, factor_sems, c, group),
            part(p2_in, p2, p2_sems, c, group),
        ]

    def start():
        coupled[...] = couple(me, got, coupling_t.shape[2] // got.shape[1])
        place_halo(me, got_a, got_b, halo)
        for copy in small:
            copy.wait()

    errors = [jnp.zeros((8, cols), F32)]

    def row(c):
        terms = outer_terms(coupled[...], coupling_t, halo, edge, c)
        for i in range(2):
            r = 2 * c + i
            move = change[r] - factor[r] * terms[i * size : (i + 1) * size]
            new_p[r] = p2[r] + move
            rate_error = (1.0 / error_scale) * move
            weighted = table[:, 8 * r + 4 : 8 * r + 5] * (rate_error * rate_error)
            errors[0] += jnp.sum(weighted.reshape(size // 8, 8, cols), axis=0)

    def done(c):
        part(new_p, new_p_out, new_p_sems, c, group).start()

    run_rows(order, first_edged, loads, outer, row, done, start)
    both = jnp.concatenate(
        [jnp.sum(errors[0] + parts[0], axis=0, keepdims=True), jnp.sum(parts[1], axis=0, keepdims=True)], axis=0
    )
    for j in range(parts_out.shape[0]):
        parts_out[j] = both
    for c in range(chunks):
        part(new_p, new_p_out, new_p_sems, c, group).wait()


def exchange(side_a, side_b, slots):
    count = lax.axis_size(AXIS)
    got_a = lax.ppermute(side_a, AXIS, [(i, i ^ 1) for i in range(count)])
    pairs = [(i, (i - 1) % count if i % 2 == 0 else (i + 1) % count) for i in range(count)]
    got_b = lax.ppermute(side_b, AXIS, pairs)
    got = lax.all_to_all(slots, AXIS, 0, 0)
    return got_a, got_b, got


def on_device(
    log_rate,
    log_state,
    near_blocks,
    near_columns,
    far_basis,
    far_coupling,
    self_stiffness,
    plate_rate,
    direct_effect,
    evolution_effect,
    triangle_area,
):
    rows, cols = log_rate.shape
    row_blocks, near_count, size, _ = near_blocks.shape
    levels, rank, _ = far_basis.shape
    devices = lax.axis_size(AXIS)
    p = log_rate.reshape(row_blocks, size, cols)
    s = log_state.reshape(row_blocks, size, cols)
    basis = far_basis.reshape(levels * rank, rows)
    coupling = far_coupling.reshape(levels * rank, rows)
    stiff, plate, direct, evolve, area = (
        v.reshape(row_blocks, size)
        for v in (self_stiffness, plate_rate, direct_effect, evolution_effect, triangle_area)
    )
    pairs = row_blocks // 2
    flat_near = near_blocks.reshape(row_blocks * near_count, size, size)
    state = ((row_blocks, size, cols), F32)
    x_kind = ((row_blocks, size, cols), BF16)
    slots_kind = ((devices, rank, cols), BF16)
    side_kind = ((REACH, size, cols), BF16)
    edge_kind = ((len(edge_tiles(row_blocks)), 2 * size, 2 * size), BF16)
    ct_kind = ((row_blocks, size, levels * rank), BF16)
    basis_kind = ((levels * rank, rows), BF16)
    near_kind = ((row_blocks * near_count + 1, size, size), BF16)
    halo_kind = ((2 * REACH, size, cols), BF16)
    vector_kind = ((row_blocks, size), F32)
    table_kind = ((size, 8 * row_blocks), F32)
    parts_kind = ((2, 8, cols), F32)
    products_kind = ((pairs, 2 * size, cols), F32)
    coupled_kind = ((levels * rank, cols), BF16)
    where_kind = pltpu.SMEM((row_blocks, 2 * REACH + 1), jnp.int32)
    loads = 4 if row_blocks % 4 == 0 else row_blocks
    near_flops = 2 * rows * near_count * size * cols

    def vmem(*kinds):
        return [pltpu.VMEM(shape, dtype) for shape, dtype in kinds]

    small = pltpu.CompilerParams(vmem_limit_bytes=40 * 1024 * 1024)
    x, slots, side_a, side_b = pl.pallas_call(
        open_kernel,
        out_shape=in_hbm(x_kind, slots_kind, side_kind, side_kind),
        in_specs=[PLAIN] * 2,
        out_specs=(PLAIN,) * 4,
        scratch_shapes=vmem(state, basis_kind, x_kind, slots_kind)
        + [SEMS((loads,)), SEMS(()), SEMS(()), SEMS((3,))],
        name="open",
    )(*hbm(p, basis))

    got_a, got_b, got = exchange(side_a, side_b, slots)
    known, factor, edge, coupling_t, table = pl.pallas_call(
        first_local_kernel,
        out_shape=in_hbm(state, state, edge_kind, ct_kind, table_kind),
        in_specs=[SCALARS] + [PLAIN] * 10,
        out_specs=(PLAIN,) * 5,
        scratch_shapes=vmem(
            x_kind, near_kind, state, state, basis_kind, *[vector_kind] * 5, state, state, edge_kind, ct_kind,
            table_kind, products_kind,
        )
        + [where_kind, SEMS(())]
        + [SEMS((pairs,))] * 3
        + [SEMS(()), SEMS((5,)), SEMS((pairs,)), SEMS((pairs,)), SEMS((3,))],
        cost_estimate=cost(near_flops, near_blocks.size * 2),
        name="local_one",
    )(near_columns, *hbm(x, flat_near, p, s, coupling, stiff, plate, direct, evolve, area))

    p2, x, slots, side_a, side_b = pl.pallas_call(
        middle_kernel,
        out_shape=in_hbm(state, x_kind, slots_kind, side_kind, side_kind),
        in_specs=[WHOLE] * 3 + [PLAIN] * 5,
        out_specs=(PLAIN,) * 5,
        scratch_shapes=vmem(
            halo_kind, edge_kind, ct_kind, basis_kind, state, state, state, x_kind, slots_kind, coupled_kind
        )
        + [SEMS((3,)), SEMS((pairs,)), SEMS((pairs,)), SEMS((pairs,)), SEMS(()), SEMS((3,))],
        compiler_params=small,
        name="middle",
    )(got_a, got_b, got, *hbm(edge, coupling_t, basis, known, factor))

    got_a, got_b, got = exchange(side_a, side_b, slots)
    change, factor, new_s, parts = pl.pallas_call(
        second_local_kernel,
        out_shape=in_hbm(state, state, state, parts_kind),
        in_specs=[SCALARS] + [PLAIN] * 6,
        out_specs=(PLAIN,) * 4,
        scratch_shapes=vmem(
            x_kind, near_kind, state, state, state, table_kind, state, state, state, parts_kind, products_kind
        )
        + [where_kind, SEMS(())]
        + [SEMS((pairs,))] * 7
        + [SEMS((2,))],
        cost_estimate=cost(near_flops, near_blocks.size * 2),
        name="local_two",
    )(near_columns, *hbm(x, flat_near, p, s, p2, table))

    new_p, parts = pl.pallas_call(
        close_kernel,
        out_shape=in_hbm(state) + like(((devices, 2, cols), F32)),
        in_specs=[WHOLE] * 3 + [PLAIN] * 7,
        out_specs=(PLAIN, WHOLE),
        scratch_shapes=vmem(
            halo_kind, edge_kind, ct_kind, state, state, state, state, coupled_kind, table_kind, parts_kind
        )
        + [SEMS((4,))]
        + [SEMS((pairs,))] * 4,
        compiler_params=small,
        name="close",
    )(got_a, got_b, got, *hbm(edge, coupling_t, p2, change, factor, table, parts))

    totals = lax.all_to_all(parts, AXIS, 0, 0).sum(axis=0)
    error_norm = jnp.sqrt(totals[0] / totals[1] + 1e-06)
    return new_p.reshape(rows, cols), new_s.reshape(rows, cols), error_norm


def solution(mesh):
    split = P(("member", "patch"))
    in_specs = (
        P(("member", "patch"), None),
        P(("member", "patch"), None),
        P(("member", "patch"), None, None, None),
        P(("member", "patch"), None),
        P("member", None, "patch"),
        P("member", None, "patch"),
        split,
        split,
        split,
        split,
        split,
    )
    out_specs = (P(("member", "patch"), None), P(("member", "patch"), None), P("member"))
    return jax.shard_map(
        on_device, mesh=mesh, in_specs=in_specs, out_specs=out_specs, check_vma=False
    )
```

time: 62.7 us -> 62 us (0.989)
  local copies, waits for them, and re-layouts: 0.7 us -> 0 us
    pallas_call x1, Pallas kernels: 4.23 us -> 2.4 us  [on_device(): pl.pallas_call(open_kernel, out_shape=in_hbm(x_kind, slots_kind, side_kin...]
    pallas_call x1, Pallas kernels: 8.12 us -> 9.37 us  [on_device(): pl.pallas_call(first_local_kernel, out_shape=in_hbm(state, state, edge_ki...]
    unnamed x4 -> x0, local copies, waits for them, and re-layouts: 0.7 us -> none
  transfers between devices with their start and end apart: 6 -> 6, of which waited for: 0 -> 0; matrix products, arithmetic and copies ran while one was open for 0% -> 0% of each run, Pallas kernels for 27% -> 30%
where the time goes in v4:
time: 62 us; the launch traced here: 61.5 us
  Pallas kernels  30.7 us (50%)
  starting transfers between devices  20.4 us (33%)
  blocking collectives  9.07 us (15%)
  between operations  0.74 us (1%)
    all_to_all x2, starting transfers between devices, exchange(): got = lax.all_to_all(slots, AXIS, 0, 0)  10.9 us
    pallas_call x1, Pallas kernels, on_device(): pl.pallas_call(first_local_kernel, out_shape=in_hbm(state, state, edge_ki...  9.37 us
    pallas_call x1, Pallas kernels, on_device(): pl.pallas_call(second_local_kernel, out_shape=in_hbm(state, state, state,...  9.19 us
    all_to_all x1, blocking collectives, on_device(): totals = lax.all_to_all(parts, AXIS, 0, 0).sum(axis=0)  9.07 us
    ppermute x2, starting transfers between devices, exchange(): got_b = lax.ppermute(side_b, AXIS, pairs)  8.75 us
    pallas_call x1, Pallas kernels, on_device(): pl.pallas_call(middle_kernel, out_shape=in_hbm(state, x_kind, slots_kind,...  4.96 us
    pallas_call x1, Pallas kernels, on_device(): pl.pallas_call(close_kernel, out_shape=in_hbm(state) + like(((devices, 2,...  4.77 us
    pallas_call x1, Pallas kernels, on_device(): pl.pallas_call(open_kernel, out_shape=in_hbm(x_kind, slots_kind, side_kin...  2.4 us
  transfers between devices with their start and end apart: 6, of which 0 were waited for; matrix products, arithmetic and copies ran while one was open for 0% of the time, Pallas kernels for 30%

profile of v4, /device:TPU:0, one launch (start us, length us, event | category | flops | bytes accessed | tf_op | source)
XLA Modules:
  0.0 61.5 jit_solution(451111369795732466)
XLA Ops:
  0.6 2.4 %open.1 = (bf16[16,128,128]{2,1,0:T(8,128)(2,1)}, bf16[16,32,128]{2,1,0:T(8,128)(2,1)}, bf16[6,128,128]{2,1,0:T(8,128)(2,1)}, bf16[6,128,128]{2,1,0:T(8,128)(2,1)}) custom-call(f32[16,128,128]{2,1,0:T(8,128)} %bitcast.16, bf16[128,2048]{1,0:T(8,128)(2,1)} %bitcast.21), custom_call_target="tpu_custom_call" | custom-call | tf_op jit(solution)/shard_map/open/pallas_call | solution.py:570
  3.0 7.4 %all-to-all-start = ((bf16[16,32,128]{2,1,0:T(8,128)(2,1)}), bf16[16,32,128]{2,1,0:T(8,128)(2,1)S(1)}, u32[]{:S(2)}, u32[]{:S(2)}) async-start(bf16[16,32,128]{2,1,0:T(8,128)(2,1)} %get-tuple-element.25), calls=%async_computation | async-start | bytes 262144 | tf_op jit(solution)/shard_map/all_to_all | solution.py:517
  10.5 0.4 collective-permute-start
  10.9 4.3 %collective-permute-start.1 = (bf16[6,128,128]{2,1,0:T(8,128)(2,1)}, bf16[6,128,128]{2,1,0:T(8,128)(2,1)S(1)}, u32[]{:S(2)}, u32[]{:S(2)}) collective-permute-start(bf16[6,128,128]{2,1,0:T(8,128)(2,1)} %get-tuple-element.24), channel_id=1, source_target_pairs={{0,15},{1,2},{2,1},{3,4},{4,3},{5,6},{6,5},{7,8},{8,7},{9,10},{10,... | collective-permute-start | bytes 589832 | tf_op jit(solution)/shard_map/ppermute | solution.py:516
  15.2 9.4 %local_one.1 = (f32[16,128,128]{2,1,0:T(8,128)}, f32[16,128,128]{2,1,0:T(8,128)}, bf16[12,256,256]{2,1,0:T(8,128)(2,1)}, bf16[16,128,128]{2,1,0:T(8,128)(2,1)}, f32[128,128]{1,0:T(8,128)}) custom-call(s32[16,12]{1,0:T(8,128)} %columns.3, bf16[16,128,128]{2,1,0:T(8,128)(2,1)} %get-tuple-element.26.x_in, bf16[192,128,128]{2,1,0:T(8,128)(2,1)} %bitcast.14, ...), custom_call_target="tpu_custom_call" | custom-call | flops 805306368 | bytes 6291456 | tf_op jit(solution)/shard_map/local_one/pallas_call | solution.py:581
  24.6 0.0 collective-permute-done.got_a
  24.6 0.0 collective-permute-done.1.got_b
  24.6 0.0 all-to-all-done.got
  24.6 5.0 %middle.1 = (f32[16,128,128]{2,1,0:T(8,128)}, bf16[16,128,128]{2,1,0:T(8,128)(2,1)}, bf16[16,32,128]{2,1,0:T(8,128)(2,1)}, bf16[6,128,128]{2,1,0:T(8,128)(2,1)}, bf16[6,128,128]{2,1,0:T(8,128)(2,1)}) custom-call(bf16[6,128,128]{2,1,0:T(8,128)(2,1)S(1)} %collective-permute-done.got_a, bf16[6,128,128]{2,1,0:T(8,128)(2,1)S(1)} %collective-permute-done.1.got_b, ...), custom_call_target="tpu_custom_call" | custom-call | tf_op jit(solution)/shard_map/middle/pallas_call | solution.py:597
  29.6 3.5 %all-to-all-start.1 = ((bf16[16,32,128]{2,1,0:T(8,128)(2,1)}), bf16[16,32,128]{2,1,0:T(8,128)(2,1)S(1)}, u32[]{:S(2)}, u32[]{:S(2)}) async-start(bf16[16,32,128]{2,1,0:T(8,128)(2,1)} %get-tuple-element.33), calls=%async_computation.1 | async-start | bytes 262144 | tf_op jit(solution)/shard_map/all_to_all | solution.py:517
  33.1 0.3 collective-permute-start.2
  33.4 4.4 %collective-permute-start.3 = (bf16[6,128,128]{2,1,0:T(8,128)(2,1)}, bf16[6,128,128]{2,1,0:T(8,128)(2,1)S(1)}, u32[]{:S(2)}, u32[]{:S(2)}) collective-permute-start(bf16[6,128,128]{2,1,0:T(8,128)(2,1)} %get-tuple-element.32), channel_id=1, source_target_pairs={{0,15},{1,2},{2,1},{3,4},{4,3},{5,6},{6,5},{7,8},{8,7},{9,10},{10,... | collective-permute-start | bytes 589832 | tf_op jit(solution)/shard_map/ppermute | solution.py:516
  37.8 9.2 %local_two.1 = (f32[16,128,128]{2,1,0:T(8,128)}, f32[16,128,128]{2,1,0:T(8,128)}, f32[16,128,128]{2,1,0:T(8,128)}, f32[2,8,128]{2,1,0:T(8,128)}) custom-call(s32[16,12]{1,0:T(8,128)} %columns.3, bf16[16,128,128]{2,1,0:T(8,128)(2,1)} %get-tuple-element.35.x_in, bf16[192,128,128]{2,1,0:T(8,128)(2,1)} %bitcast.15, f32[16,128,128]{2,1,0:T(8,128)} %bitcast.18, ...), custom_call_target="tpu_custom_call" | custom-call | flops 805306368 | bytes 6291456 | tf_op jit(solution)/shard_map/local_two/pallas_call | solution.py:611
  47.0 0.0 collective-permute-done.2.got_a
  47.0 0.0 collective-permute-done.3.got_b
  47.0 0.0 all-to-all-done.1.got
  47.1 4.8 %close.1 = (f32[16,128,128]{2,1,0:T(8,128)}, f32[16,2,128]{2,1,0:T(2,128)S(1)}) custom-call(bf16[6,128,128]{2,1,0:T(8,128)(2,1)S(1)} %collective-permute-done.2.got_a, bf16[6,128,128]{2,1,0:T(8,128)(2,1)S(1)} %collective-permute-done.3.got_b, bf16[16,32,128]{2,1,0:T(8,128)(2,1)S(1)} %all-to-all-done.1.got, bf16[12,256,256]{2,1,0:T(8,128)(2,1)} %get-tuple-element.27.edge_in, ...), custom_call_target="tpu_custom_call" | custom-call | tf_op jit(solution)/shard_map/close/pallas_call | solution.py:626
  51.8 9.1 %all_to_all.15 = f32[16,2,128]{2,1,0:T(2,128)S(1)} all-to-all(f32[16,2,128]{2,1,0:T(2,128)S(1)} %get-tuple-element.42), channel_id=1, replica_groups=mesh['member'=2,'patch'=16] {'patch'}, dimensions={0} | all-to-all | bytes 32768 | tf_op jit(solution)/shard_map/all_to_all | solution.py:640
  60.9 0.5 sqrt_bitcast_fusion
  (1 shorter events, 0.0 us)
Async XLA Ops:
  3.0 21.6 %all-to-all-start = ((bf16[16,32,128]{2,1,0:T(8,128)(2,1)}), bf16[16,32,128]{2,1,0:T(8,128)(2,1)S(1)}, u32[]{:S(2)}, u32[]{:S(2)}) async-start(bf16[16,32,128]{2,1,0:T(8,128)(2,1)} %get-tuple-element.25), calls=%async_computation | async-start | bytes 262144 | tf_op jit(solution)/shard_map/all_to_all | solution.py:517
  10.5 14.1 %collective-permute-start = (bf16[6,128,128]{2,1,0:T(8,128)(2,1)}, bf16[6,128,128]{2,1,0:T(8,128)(2,1)S(1)}, u32[]{:S(2)}, u32[]{:S(2)}) collective-permute-start(bf16[6,128,128]{2,1,0:T(8,128)(2,1)} %get-tuple-element.23), channel_id=1, source_target_pairs={{0,1},{1,0},{2,3},{3,2},{4,5},{5,4},{6,7},{7,6},{8,9},{9,8},{10,11... | collective-permute-start | bytes 589832 | tf_op jit(solution)/shard_map/ppermute | solution.py:514
  10.9 13.7 %collective-permute-start.1 = (bf16[6,128,128]{2,1,0:T(8,128)(2,1)}, bf16[6,128,128]{2,1,0:T(8,128)(2,1)S(1)}, u32[]{:S(2)}, u32[]{:S(2)}) collective-permute-start(bf16[6,128,128]{2,1,0:T(8,128)(2,1)} %get-tuple-element.24), channel_id=1, source_target_pairs={{0,15},{1,2},{2,1},{3,4},{4,3},{5,6},{6,5},{7,8},{8,7},{9,10},{10,... | collective-permute-start | bytes 589832 | tf_op jit(solution)/shard_map/ppermute | solution.py:516
  29.6 17.5 %all-to-all-start.1 = ((bf16[16,32,128]{2,1,0:T(8,128)(2,1)}), bf16[16,32,128]{2,1,0:T(8,128)(2,1)S(1)}, u32[]{:S(2)}, u32[]{:S(2)}) async-start(bf16[16,32,128]{2,1,0:T(8,128)(2,1)} %get-tuple-element.33), calls=%async_computation.1 | async-start | bytes 262144 | tf_op jit(solution)/shard_map/all_to_all | solution.py:517
  33.1 13.9 %collective-permute-start.2 = (bf16[6,128,128]{2,1,0:T(8,128)(2,1)}, bf16[6,128,128]{2,1,0:T(8,128)(2,1)S(1)}, u32[]{:S(2)}, u32[]{:S(2)}) collective-permute-start(bf16[6,128,128]{2,1,0:T(8,128)(2,1)} %get-tuple-element.31), channel_id=1, source_target_pairs={{0,1},{1,0},{2,3},{3,2},{4,5},{5,4},{6,7},{7,6},{8,9},{9,8},{10,11... | collective-permute-start | bytes 589832 | tf_op jit(solution)/shard_map/ppermute | solution.py:514
  33.4 13.6 %collective-permute-start.3 = (bf16[6,128,128]{2,1,0:T(8,128)(2,1)}, bf16[6,128,128]{2,1,0:T(8,128)(2,1)S(1)}, u32[]{:S(2)}, u32[]{:S(2)}) collective-permute-start(bf16[6,128,128]{2,1,0:T(8,128)(2,1)} %get-tuple-element.32), channel_id=1, source_target_pairs={{0,15},{1,2},{2,1},{3,4},{4,3},{5,6},{6,5},{7,8},{8,7},{9,10},{10,... | collective-permute-start | bytes 589832 | tf_op jit(solution)/shard_map/ppermute | solution.py:516

commit v5 on v4

v5 whole, which is shorter than its diff:
```python
import jax
import jax.numpy as jnp
from jax import lax
from jax.experimental import pallas as pl
from jax.experimental.pallas import tpu as pltpu
from jax.sharding import PartitionSpec as P


REACH = 6
PAD = REACH + REACH % 2

step_size = 0.1
damping = 0.5
error_scale = 0.01
half_step = 0.5 * step_size

AXIS = "patch"
F32 = jnp.float32
BF16 = jnp.bfloat16
PLAIN = pl.BlockSpec(memory_space=pltpu.HBM)
WHOLE = pl.BlockSpec(memory_space=pltpu.VMEM)
SCALARS = pl.BlockSpec(memory_space=pltpu.SMEM)
SEMS = pltpu.SemaphoreType.DMA


def cost(flops, moved, exps=0):
    return pl.CostEstimate(flops=flops, bytes_accessed=moved, transcendentals=exps)


def in_hbm(*shapes):
    return tuple(pltpu.HBM(shape, dtype) for shape, dtype in shapes)


def hbm(*arrays):
    return tuple(pltpu.with_memory_space_constraint(v, pltpu.HBM) for v in arrays)


def like(*shapes):
    return tuple(jax.ShapeDtypeStruct(shape, dtype) for shape, dtype in shapes)


def part(src, dst, sems, c, group):
    at = pl.ds(c * group, group)
    return pltpu.make_async_copy(src.at[at], dst.at[at], sems.at[c])


def edged_pairs(row_blocks):
    count = (REACH + 1) // 2
    pairs = row_blocks // 2
    return list(range(count)), list(range(pairs - count, pairs))


def pick(n, values):
    result = jnp.int32(values[0])
    for i, value in enumerate(values[1:], 1):
        result = jnp.where(n == i, jnp.int32(value), result)
    return result


def project(basis, x):
    row_blocks, size, cols = x.shape
    return jnp.dot(basis[...], x[...].reshape(row_blocks * size, cols), preferred_element_type=F32)


def fill_slots(me, projected, slots):
    devices, rank, _ = slots.shape
    for m in range(devices):
        level = max(m.bit_length() - 1, 0)
        slots[me ^ m] = projected[level * rank : (level + 1) * rank].astype(slots.dtype)


def send_copies(me, x, slots, slots_out, a_out, b_out, sems):
    row_blocks = x.shape[0]
    odd = lax.rem(me, 2)
    start_a = (1 - odd) * (row_blocks - REACH)
    start_b = odd * (row_blocks - REACH)
    return [
        pltpu.make_async_copy(slots, slots_out, sems.at[0]),
        pltpu.make_async_copy(x.at[pl.ds(start_a, REACH)], a_out, sems.at[1]),
        pltpu.make_async_copy(x.at[pl.ds(start_b, REACH)], b_out, sems.at[2]),
    ]


def open_kernel(
    p_in, basis_in, x_out, slots_out, a_out, b_out,
    p, basis, x, slots, p_sems, x_sem, basis_sem, send_sems,
):
    row_blocks, _, _ = p.shape
    chunks = p_sems.shape[0]
    group = row_blocks // chunks
    me = lax.axis_index(AXIS)
    load_basis = pltpu.make_async_copy(basis_in, basis, basis_sem)
    for c in range(chunks):
        part(p_in, p, p_sems, c, group).start()
    load_basis.start()
    for c in range(chunks):
        part(p_in, p, p_sems, c, group).wait()
        rows = slice(c * group, (c + 1) * group)
        x[rows] = jnp.exp(p[rows]).astype(BF16)
    send = send_copies(me, x, slots, slots_out, a_out, b_out, send_sems)
    send.append(pltpu.make_async_copy(x, x_out, x_sem))
    for copy in send[1:]:
        copy.start()
    load_basis.wait()
    fill_slots(me, project(basis, x), slots)
    send[0].start()
    for copy in send:
        copy.wait()


def find_blocks(columns, where):
    row_blocks, near_count = columns.shape
    total = row_blocks * lax.axis_size(AXIS)
    first = row_blocks * lax.axis_index(AXIS)

    def row(r, carry):
        for o in range(2 * REACH + 1):
            where[r, o] = row_blocks * near_count
        for k in range(near_count):
            offset = columns[r, k] - first - r
            offset = jnp.where(offset > REACH, offset - total, offset)
            offset = jnp.where(offset < -REACH, offset + total, offset)
            where[r, offset + REACH] = r * near_count + k
        return carry

    lax.fori_loop(0, row_blocks, row, 0)


def near_product(near, x, where, pair):
    size, cols = x.shape[1:]
    width = 2 * PAD + 2
    lhs = []
    for i in range(2):
        offsets = [j - PAD - i for j in range(width)]
        lhs.append(
            jnp.concatenate(
                [
                    near[where[2 * pair + i, o + REACH]] if abs(o) <= REACH else jnp.zeros((size, size), near.dtype)
                    for o in offsets
                ],
                axis=1,
            )
        )
    rhs = x[pl.ds(2 * pair, width)].reshape(width * size, cols)
    return jnp.dot(jnp.concatenate(lhs, axis=0), rhs, preferred_element_type=F32)


def strips(size):
    step = 32 if size % 32 == 0 else size
    return [slice(i, i + step) for i in range(0, size, step)]


def columns_of(table, pair, i, at):
    lanes = table.shape[1]
    turned = pltpu.roll(table[at], lax.rem(lanes - 16 * pair, lanes), axis=1)
    return [turned[:, 8 * i + q : 8 * i + q + 1] for q in range(5)]


def known_rates(velocity, state, near_term, rows):
    stiff, plate, direct, evolve, _ = rows
    factor = 1.0 / (direct + damping * velocity)
    return (stiff * (plate - velocity) - near_term - evolve * state) * factor, factor


def in_pairs(order, wait_product, wait_finish, product, finish, store, terms, carry):
    count = len(order)
    plain = order == list(range(count))

    def at(n):
        return n if plain else pick(n, order)

    def body(n, carry):
        now, before = at(jnp.minimum(n, count - 1)), at(jnp.maximum(n - 1, 0))
        pl.when(n < count)(lambda: wait_product(n, now))
        pl.when(n != 1)(lambda: wait_finish(before))
        new = product(now)
        carry = finish(before, n > 0, n <= 1, carry)
        terms[...] = new
        pl.when(n > 0)(lambda: store(before))
        return carry

    return lax.fori_loop(0, count + 1, body, carry)


def each(count, action):
    def body(n, carry):
        action(n)
        return carry

    lax.fori_loop(0, count, body, 0)


def start_all(copies):
    for copy in copies:
        copy.start()


def wait_all(copies):
    for copy in copies:
        copy.wait()


def inner(x, size_blocks):
    return x.at[pl.ds(PAD, size_blocks)]


def clear_pads(x, row_blocks):
    zeros = jnp.zeros((PAD,) + x.shape[1:], x.dtype)
    x[:PAD] = zeros
    x[PAD + row_blocks :] = zeros


def first_local_kernel(
    columns, x_in, near_in, p_in, s_in, coupling_in, stiff_in, plate_in, direct_in, evolve_in, area_in,
    known_out, factor_out, edge_out, coupling_t_out, table_out,
    x, near, p, s, coupling, stiff, plate, direct, evolve, area, known, factor, edge, coupling_t, table, terms,
    where, x_sem, near_sems, p_sems, s_sems, coupling_sem, vector_sems, known_sems, factor_sems, rest_sems,
):
    row_blocks, size, _ = p.shape
    pairs = row_blocks // 2
    span = (near.shape[0] - 1) // pairs
    vectors = (stiff, plate, direct, evolve, area)
    load_x = pltpu.make_async_copy(x_in, inner(x, row_blocks), x_sem)
    load_coupling = pltpu.make_async_copy(coupling_in, coupling, coupling_sem)
    load_vectors = [
        pltpu.make_async_copy(src, dst, vector_sems.at[q])
        for q, (src, dst) in enumerate(zip((stiff_in, plate_in, direct_in, evolve_in, area_in), vectors))
    ]

    def near_load(c):
        return part(near_in, near, near_sems, c, span)

    def loads(c):
        return [part(p_in, p, p_sems, c, 2), part(s_in, s, s_sems, c, 2)]

    def stores(c):
        return [part(known, known_out, known_sems, c, 2), part(factor, factor_out, factor_sems, c, 2)]

    start_all(load_vectors + [load_x])
    each(pairs, lambda c: start_all([near_load(c)] + loads(c)))
    load_coupling.start()
    near[near.shape[0] - 1] = jnp.zeros(near.shape[1:], near.dtype)
    clear_pads(x, row_blocks)
    find_blocks(columns, where)
    wait_all(load_vectors)
    tiles = [
        jnp.concatenate([v[r : r + 1] for v in vectors + (area, area, area)], axis=0) for r in range(row_blocks)
    ]
    table[...] = jnp.concatenate(tiles, axis=0).T
    load_x.wait()

    def finish(pair, counts, fresh, carry):
        for i in range(2):
            r = 2 * pair + i
            for at in strips(size):
                now = p[r, at]
                velocity = jnp.exp(now)
                state = jnp.exp(-s[r, at]) - velocity
                near_term = terms[i * size + at.start : i * size + at.stop]
                rate, scale = known_rates(velocity, state, near_term, columns_of(table, pair, i, at))
                known[r, at] = now + step_size * rate
                factor[r, at] = step_size * scale
        return carry

    in_pairs(
        list(range(pairs)),
        lambda n, c: near_load(c).wait(),
        lambda c: wait_all(loads(c)),
        lambda c: near_product(near, x, where, c),
        finish,
        lambda c: start_all(stores(c)),
        terms,
        0,
    )
    left, right = edged_pairs(row_blocks)
    width = edge.shape[2] // size
    for side, first in ((left, -width), (right, row_blocks)):

        def edge_pair(n, side=side, first=first):
            pair = side[0] + n
            slot = n if first < 0 else n + len(left)
            for i in range(2):
                for j in range(width):
                    offset = first + j - 2 * pair - i
                    inside = jnp.abs(offset) <= REACH
                    block = near[
                        jnp.where(inside, where[2 * pair + i, jnp.where(inside, offset, 0) + REACH], near.shape[0] - 1)
                    ]
                    edge[slot, i * size : (i + 1) * size, j * size : (j + 1) * size] = block

        each(len(side), edge_pair)
    store_edge = pltpu.make_async_copy(edge, edge_out, rest_sems.at[0])
    store_edge.start()
    load_coupling.wait()

    def turn(r):
        coupling_t[r] = coupling[:, pl.ds(pl.multiple_of(r * size, size), size)].T

    each(row_blocks, turn)
    last = [
        pltpu.make_async_copy(coupling_t, coupling_t_out, rest_sems.at[1]),
        pltpu.make_async_copy(table, table_out, rest_sems.at[2]),
    ]
    start_all(last)
    each(pairs, lambda c: wait_all(stores(c)))
    wait_all(last + [store_edge])


def second_local_kernel(
    columns, x_in, near_in, p_in, s_in, p2_in, table_in,
    change_out, factor_out, new_s_out, parts_out,
    x, near, p, s, p2, table, change, factor, new_s, parts, terms,
    where, x_sem, near_sems, p_sems, s_sems, p2_sems, change_sems, factor_sems, new_s_sems, rest_sems,
):
    row_blocks, size, cols = p.shape
    pairs = row_blocks // 2
    span = (near.shape[0] - 1) // pairs
    load_x = pltpu.make_async_copy(x_in, inner(x, row_blocks), x_sem)
    load_table = pltpu.make_async_copy(table_in, table, rest_sems.at[0])

    def near_load(c):
        return part(near_in, near, near_sems, c, span)

    def loads(c):
        return [part(p_in, p, p_sems, c, 2), part(s_in, s, s_sems, c, 2), part(p2_in, p2, p2_sems, c, 2)]

    def stores(c):
        return [
            part(change, change_out, change_sems, c, 2),
            part(factor, factor_out, factor_sems, c, 2),
            part(new_s, new_s_out, new_s_sems, c, 2),
        ]

    start_all([load_x, load_table])
    each(pairs, lambda c: start_all([near_load(c)] + loads(c)))
    near[near.shape[0] - 1] = jnp.zeros(near.shape[1:], near.dtype)
    clear_pads(x, row_blocks)
    find_blocks(columns, where)
    load_x.wait()
    load_table.wait()

    def finish(pair, counts, fresh, errors):
        more = jnp.zeros((8, cols), F32)
        for i in range(2):
            r = 2 * pair + i
            for at in strips(size):
                rows = columns_of(table, pair, i, at)
                before, now, start = p[r, at], p2[r, at], s[r, at]
                state_a = jnp.exp(-start) - jnp.exp(before)
                velocity = jnp.exp(now)
                state_b = jnp.exp(-(start + step_size * state_a)) - velocity
                near_term = terms[i * size + at.start : i * size + at.stop]
                rate, scale = known_rates(velocity, state_b, near_term, rows)
                change[r, at] = half_step * rate - (half_step / step_size) * (now - before)
                factor[r, at] = half_step * scale
                new_s[r, at] = start + half_step * (state_a + state_b)
                state_error = (half_step / error_scale) * (state_b - state_a)
                weighted = rows[4] * (state_error * state_error)
                more += jnp.sum(weighted.reshape(-1, 8, cols), axis=0)
        return errors + jnp.where(counts, more, jnp.zeros_like(more))

    parts[0] = in_pairs(
        list(range(pairs)),
        lambda n, c: near_load(c).wait(),
        lambda c: wait_all(loads(c)),
        lambda c: near_product(near, x, where, c),
        finish,
        lambda c: start_all(stores(c)),
        terms,
        jnp.zeros((8, cols), F32),
    )
    lane = lax.broadcasted_iota(jnp.int32, table.shape, 1)
    areas = jnp.where(lane % 8 == 4, table[...], jnp.zeros(table.shape, F32))
    areas = jnp.sum(areas.reshape(-1, 8, table.shape[1]), axis=0)
    parts[1] = jnp.broadcast_to(jnp.sum(areas, axis=1, keepdims=True), (8, cols))
    store_parts = pltpu.make_async_copy(parts, parts_out, rest_sems.at[1])
    store_parts.start()
    each(pairs, lambda c: wait_all(stores(c)))
    store_parts.wait()


def couple(me, got, levels):
    devices = got.shape[0]
    sums = []
    for level in range(levels):
        total = got[me ^ (1 << level)].astype(F32)
        for m in range((1 << level) + 1, min(2 << level, devices)):
            total += got[me ^ m].astype(F32)
        sums.append(total.astype(BF16))
    return jnp.concatenate(sums, axis=0)


def pair_order(row_blocks):
    edged = sum(edged_pairs(row_blocks), [])
    free = [c for c in range(row_blocks // 2) if c not in edged]
    return free + edged, len(free)


def outer_terms(coupled, coupling_t, halo, edge, pair):
    row_blocks, size, rank = coupling_t.shape
    cols = halo.shape[2]
    width = edge.shape[2] // size
    left, right = edged_pairs(row_blocks)
    in_left, in_right = pair <= left[-1], pair >= right[0]
    slot = jnp.where(in_left, pair, jnp.where(in_right, pair - right[0] + len(left), 0))
    at = jnp.where(in_left, 0, jnp.where(in_right, width, 2 * width))
    lhs = jnp.concatenate([edge[slot], coupling_t[pl.ds(2 * pair, 2)].reshape(2 * size, rank)], axis=1)
    rhs = jnp.concatenate([halo[pl.ds(at, width)].reshape(width * size, cols), coupled[...]], axis=0)
    return jnp.dot(lhs, rhs, preferred_element_type=F32)


def place_halo(me, got_a, got_b, halo):
    odd = lax.rem(me, 2)
    halo[pl.ds((1 - odd) * REACH, REACH)] = got_a[...]
    halo[pl.ds(odd * REACH, REACH)] = got_b[...]
    halo[2 * REACH :] = jnp.zeros(got_a.shape, got_a.dtype)


def middle_kernel(
    got_a, got_b, got, edge_in, ct_in, basis_in, known_in, factor_in,
    p2_out, x_out, slots_out, a_out, b_out,
    halo, edge, coupling_t, basis, known, factor, p2, x, slots, coupled, projected, terms,
    outer_sems, known_sems, factor_sems, p2_sems, x_sem, send_sems,
):
    row_blocks, size, cols = known.shape
    pairs = row_blocks // 2
    me = lax.axis_index(AXIS)
    order, _ = pair_order(row_blocks)
    load_ct = pltpu.make_async_copy(ct_in, coupling_t, outer_sems.at[0])
    load_edge = pltpu.make_async_copy(edge_in, edge, outer_sems.at[1])
    load_basis = pltpu.make_async_copy(basis_in, basis, outer_sems.at[2])

    def loads(c):
        return [part(known_in, known, known_sems, c, 2), part(factor_in, factor, factor_sems, c, 2)]

    def store(c):
        return part(p2, p2_out, p2_sems, c, 2)

    load_ct.start()
    for n, c in enumerate(order):
        start_all(loads(c))
        if n == 0:
            load_edge.start()
            load_basis.start()
    coupled[...] = couple(me, got, basis.shape[0] // got.shape[1])
    place_halo(me, got_a, got_b, halo)
    load_ct.wait()
    load_edge.wait()
    load_basis.wait()

    def finish(pair, counts, fresh, carry):
        for i in range(2):
            r = 2 * pair + i
            for at in strips(size):
                value = known[r, at] - factor[r, at] * terms[i * size + at.start : i * size + at.stop]
                p2[r, at] = value
                x[r, at] = jnp.exp(value).astype(BF16)
        more = jnp.dot(
            basis[:, pl.ds(pl.multiple_of(2 * pair * size, 2 * size), 2 * size)],
            x[pl.ds(2 * pair, 2)].reshape(2 * size, cols),
            preferred_element_type=F32,
        )
        projected[...] = more + jnp.where(fresh, jnp.zeros_like(more), projected[...])
        return carry

    in_pairs(
        order,
        lambda n, c: None,
        lambda c: wait_all(loads(c)),
        lambda c: outer_terms(coupled, coupling_t, halo, edge, c),
        finish,
        lambda c: store(c).start(),
        terms,
        0,
    )
    send = send_copies(me, x, slots, slots_out, a_out, b_out, send_sems)
    send.append(pltpu.make_async_copy(x, x_out, x_sem))
    start_all(send[1:])
    fill_slots(me, projected, slots)
    send[0].start()
    wait_all(send)
    each(pairs, lambda c: store(c).wait())


def close_kernel(
    got_a, got_b, got, edge_in, ct_in, p2_in, change_in, factor_in, table_in, parts_in,
    new_p_out, parts_out,
    halo, edge, coupling_t, p2, change, factor, new_p, coupled, table, parts, terms,
    outer_sems, p2_sems, change_sems, factor_sems, new_p_sems,
):
    row_blocks, size, cols = change.shape
    pairs = row_blocks // 2
    me = lax.axis_index(AXIS)
    order, _ = pair_order(row_blocks)
    load_ct = pltpu.make_async_copy(ct_in, coupling_t, outer_sems.at[0])
    load_edge = pltpu.make_async_copy(edge_in, edge, outer_sems.at[1])
    small = [
        pltpu.make_async_copy(table_in, table, outer_sems.at[2]),
        pltpu.make_async_copy(parts_in, parts, outer_sems.at[3]),
    ]

    def loads(c):
        return [
            part(change_in, change, change_sems, c, 2),
            part(factor_in, factor, factor_sems, c, 2),
            part(p2_in, p2, p2_sems, c, 2),
        ]

    def store(c):
        return part(new_p, new_p_out, new_p_sems, c, 2)

    start_all(small + [load_ct])
    for n, c in enumerate(order):
        start_all(loads(c))
        if n == 0:
            load_edge.start()
    coupled[...] = couple(me, got, coupling_t.shape[2] // got.shape[1])
    place_halo(me, got_a, got_b, halo)
    wait_all(small + [load_ct, load_edge])

    def finish(pair, counts, fresh, errors):
        more = jnp.zeros((8, cols), F32)
        for i in range(2):
            r = 2 * pair + i
            for at in strips(size):
                move = change[r, at] - factor[r, at] * terms[i * size + at.start : i * size + at.stop]
                new_p[r, at] = p2[r, at] + move
                rate_error = (1.0 / error_scale) * move
                weighted = columns_of(table, pair, i, at)[4] * (rate_error * rate_error)
                more += jnp.sum(weighted.reshape(-1, 8, cols), axis=0)
        return errors + jnp.where(counts, more, jnp.zeros_like(more))

    errors = in_pairs(
        order,
        lambda n, c: None,
        lambda c: wait_all(loads(c)),
        lambda c: outer_terms(coupled, coupling_t, halo, edge, c),
        finish,
        lambda c: store(c).start(),
        terms,
        parts[0],
    )
    both = jnp.concatenate(
        [jnp.sum(errors, axis=0, keepdims=True), jnp.sum(parts[1], axis=0, keepdims=True)], axis=0
    )
    for j in range(parts_out.shape[0]):
        parts_out[j] = both
    each(pairs, lambda c: store(c).wait())


def exchange(side_a, side_b, slots):
    count = lax.axis_size(AXIS)
    got_a = lax.ppermute(side_a, AXIS, [(i, i ^ 1) for i in range(count)])
    pairs = [(i, (i - 1) % count if i % 2 == 0 else (i + 1) % count) for i in range(count)]
    got_b = lax.ppermute(side_b, AXIS, pairs)
    got = lax.all_to_all(slots, AXIS, 0, 0)
    return got_a, got_b, got


def on_device(
    log_rate,
    log_state,
    near_blocks,
    near_columns,
    far_basis,
    far_coupling,
    self_stiffness,
    plate_rate,
    direct_effect,
    evolution_effect,
    triangle_area,
):
    rows, cols = log_rate.shape
    row_blocks, near_count, size, _ = near_blocks.shape
    levels, rank, _ = far_basis.shape
    devices = lax.axis_size(AXIS)
    p = log_rate.reshape(row_blocks, size, cols)
    s = log_state.reshape(row_blocks, size, cols)
    basis = far_basis.reshape(levels * rank, rows)
    coupling = far_coupling.reshape(levels * rank, rows)
    stiff, plate, direct, evolve, area = (
        v.reshape(row_blocks, size)
        for v in (self_stiffness, plate_rate, direct_effect, evolution_effect, triangle_area)
    )
    pairs = row_blocks // 2
    flat_near = near_blocks.reshape(row_blocks * near_count, size, size)
    state = ((row_blocks, size, cols), F32)
    x_kind = ((row_blocks, size, cols), BF16)
    slots_kind = ((devices, rank, cols), BF16)
    side_kind = ((REACH, size, cols), BF16)
    edge_kind = ((sum(map(len, edged_pairs(row_blocks))), 2 * size, REACH * size), BF16)
    ct_kind = ((row_blocks, size, levels * rank), BF16)
    basis_kind = ((levels * rank, rows), BF16)
    near_kind = ((row_blocks * near_count + 1, size, size), BF16)
    halo_kind = ((3 * REACH, size, cols), BF16)
    padded_kind = ((row_blocks + 2 * PAD, size, cols), BF16)
    vector_kind = ((row_blocks, size), F32)
    table_kind = ((size, 8 * row_blocks), F32)
    parts_kind = ((2, 8, cols), F32)
    terms_kind = ((2 * size, cols), F32)
    projected_kind = ((levels * rank, cols), F32)
    coupled_kind = ((levels * rank, cols), BF16)
    where_kind = pltpu.SMEM((row_blocks, 2 * REACH + 1), jnp.int32)
    loads = 4 if row_blocks % 4 == 0 else row_blocks
    near_flops = 2 * rows * near_count * size * cols

    def vmem(*kinds):
        return [pltpu.VMEM(shape, dtype) for shape, dtype in kinds]

    small = pltpu.CompilerParams(vmem_limit_bytes=40 * 1024 * 1024)
    x, slots, side_a, side_b = pl.pallas_call(
        open_kernel,
        out_shape=in_hbm(x_kind, slots_kind, side_kind, side_kind),
        in_specs=[PLAIN] * 2,
        out_specs=(PLAIN,) * 4,
        scratch_shapes=vmem(state, basis_kind, x_kind, slots_kind)
        + [SEMS((loads,)), SEMS(()), SEMS(()), SEMS((3,))],
        name="open",
    )(*hbm(p, basis))

    got_a, got_b, got = exchange(side_a, side_b, slots)
    known, factor, edge, coupling_t, table = pl.pallas_call(
        first_local_kernel,
        out_shape=in_hbm(state, state, edge_kind, ct_kind, table_kind),
        in_specs=[SCALARS] + [PLAIN] * 10,
        out_specs=(PLAIN,) * 5,
        scratch_shapes=vmem(
            padded_kind, near_kind, state, state, basis_kind, *[vector_kind] * 5, state, state, edge_kind, ct_kind,
            table_kind, terms_kind,
        )
        + [where_kind, SEMS(())]
        + [SEMS((pairs,))] * 3
        + [SEMS(()), SEMS((5,)), SEMS((pairs,)), SEMS((pairs,)), SEMS((3,))],
        cost_estimate=cost(near_flops, near_blocks.size * 2),
        name="local_one",
    )(near_columns, *hbm(x, flat_near, p, s, coupling, stiff, plate, direct, evolve, area))

    p2, x, slots, side_a, side_b = pl.pallas_call(
        middle_kernel,
        out_shape=in_hbm(state, x_kind, slots_kind, side_kind, side_kind),
        in_specs=[WHOLE] * 3 + [PLAIN] * 5,
        out_specs=(PLAIN,) * 5,
        scratch_shapes=vmem(
            halo_kind, edge_kind, ct_kind, basis_kind, state, state, state, x_kind, slots_kind, coupled_kind,
            projected_kind, terms_kind,
        )
        + [SEMS((3,)), SEMS((pairs,)), SEMS((pairs,)), SEMS((pairs,)), SEMS(()), SEMS((3,))],
        compiler_params=small,
        name="middle",
    )(got_a, got_b, got, *hbm(edge, coupling_t, basis, known, factor))

    got_a, got_b, got = exchange(side_a, side_b, slots)
    change, factor, new_s, parts = pl.pallas_call(
        second_local_kernel,
        out_shape=in_hbm(state, state, state, parts_kind),
        in_specs=[SCALARS] + [PLAIN] * 6,
        out_specs=(PLAIN,) * 4,
        scratch_shapes=vmem(
            padded_kind, near_kind, state, state, state, table_kind, state, state, state, parts_kind, terms_kind
        )
        + [where_kind, SEMS(())]
        + [SEMS((pairs,))] * 7
        + [SEMS((2,))],
        cost_estimate=cost(near_flops, near_blocks.size * 2),
        name="local_two",
    )(near_columns, *hbm(x, flat_near, p, s, p2, table))

    new_p, parts = pl.pallas_call(
        close_kernel,
        out_shape=in_hbm(state) + like(((devices, 2, cols), F32)),
        in_specs=[WHOLE] * 3 + [PLAIN] * 7,
        out_specs=(PLAIN, WHOLE),
        scratch_shapes=vmem(
            halo_kind, edge_kind, ct_kind, state, state, state, state, coupled_kind, table_kind, parts_kind,
            terms_kind,
        )
        + [SEMS((4,))]
        + [SEMS((pairs,))] * 4,
        compiler_params=small,
        name="close",
    )(got_a, got_b, got, *hbm(edge, coupling_t, p2, change, factor, table, parts))

    totals = lax.all_to_all(parts, AXIS, 0, 0).sum(axis=0)
    error_norm = jnp.sqrt(totals[0] / totals[1] + 1e-06)
    return new_p.reshape(rows, cols), new_s.reshape(rows, cols), error_norm


def solution(mesh):
    split = P(("member", "patch"))
    in_specs = (
        P(("member", "patch"), None),
        P(("member", "patch"), None),
        P(("member", "patch"), None, None, None),
        P(("member", "patch"), None),
        P("member", None, "patch"),
        P("member", None, "patch"),
        split,
        split,
        split,
        split,
        split,
    )
    out_specs = (P(("member", "patch"), None), P(("member", "patch"), None), P("member"))
    return jax.shard_map(
        on_device, mesh=mesh, in_specs=in_specs, out_specs=out_specs, check_vma=False
    )
```

time: 62 us -> 67.6 us (1.090)
  Pallas kernels: 30.7 us -> 36.4 us
    pallas_call x1, Pallas kernels: 9.37 us -> 11 us  [on_device(): pl.pallas_call(first_local_kernel, out_shape=in_hbm(state, state, edge_ki...]
    pallas_call x1, Pallas kernels: 4.96 us -> 6.59 us  [on_device(): pl.pallas_call(middle_kernel, out_shape=in_hbm(state, x_kind, slots_kind,...]
    pallas_call x1, Pallas kernels: 4.77 us -> 6.23 us  [on_device(): pl.pallas_call(close_kernel, out_shape=in_hbm(state) + like(((devices, 2,...]
    pallas_call x1, Pallas kernels: 9.19 us -> 10.1 us  [on_device(): pl.pallas_call(second_local_kernel, out_shape=in_hbm(state, state, state,...]
  transfers between devices with their start and end apart: 6 -> 6, of which waited for: 0 -> 0; matrix products, arithmetic and copies ran while one was open for 0% -> 0% of each run, Pallas kernels for 30% -> 31%
where the time goes in v5:
time: 67.6 us; the launch traced here: 67.1 us
  Pallas kernels  36.4 us (54%)
  starting transfers between devices  20.4 us (30%)
  blocking collectives  9.07 us (13%)
  between operations  0.74 us (1%)
    pallas_call x1, Pallas kernels, on_device(): pl.pallas_call(first_local_kernel, out_shape=in_hbm(state, state, edge_ki...  11 us
    all_to_all x2, starting transfers between devices, exchange(): got = lax.all_to_all(slots, AXIS, 0, 0)  10.9 us
    pallas_call x1, Pallas kernels, on_device(): pl.pallas_call(second_local_kernel, out_shape=in_hbm(state, state, state,...  10.1 us
    all_to_all x1, blocking collectives, on_device(): totals = lax.all_to_all(parts, AXIS, 0, 0).sum(axis=0)  9.07 us
    ppermute x2, starting transfers between devices, exchange(): got_b = lax.ppermute(side_b, AXIS, pairs)  8.75 us
    pallas_call x1, Pallas kernels, on_device(): pl.pallas_call(middle_kernel, out_shape=in_hbm(state, x_kind, slots_kind,...  6.59 us
    pallas_call x1, Pallas kernels, on_device(): pl.pallas_call(close_kernel, out_shape=in_hbm(state) + like(((devices, 2,...  6.23 us
    pallas_call x1, Pallas kernels, on_device(): pl.pallas_call(open_kernel, out_shape=in_hbm(x_kind, slots_kind, side_kin...  2.4 us
  transfers between devices with their start and end apart: 6, of which 0 were waited for; matrix products, arithmetic and copies ran while one was open for 0% of the time, Pallas kernels for 31%

profile of v5, /device:TPU:0, one launch (start us, length us, event | category | flops | bytes accessed | tf_op | source)
XLA Modules:
  0.0 67.1 jit_solution(14010562536428616759)
XLA Ops:
  0.6 2.4 %open.1 = (bf16[16,128,128]{2,1,0:T(8,128)(2,1)}, bf16[16,32,128]{2,1,0:T(8,128)(2,1)}, bf16[6,128,128]{2,1,0:T(8,128)(2,1)}, bf16[6,128,128]{2,1,0:T(8,128)(2,1)}) custom-call(f32[16,128,128]{2,1,0:T(8,128)} %bitcast.16, bf16[128,2048]{1,0:T(8,128)(2,1)} %bitcast.21), custom_call_target="tpu_custom_call" | custom-call | tf_op jit(solution)/shard_map/open/pallas_call | solution.py:611
  3.0 7.4 %all-to-all-start = ((bf16[16,32,128]{2,1,0:T(8,128)(2,1)}), bf16[16,32,128]{2,1,0:T(8,128)(2,1)S(1)}, u32[]{:S(2)}, u32[]{:S(2)}) async-start(bf16[16,32,128]{2,1,0:T(8,128)(2,1)} %get-tuple-element.25), calls=%async_computation | async-start | bytes 262144 | tf_op jit(solution)/shard_map/all_to_all | solution.py:556
  10.5 0.4 collective-permute-start
  10.9 4.3 %collective-permute-start.1 = (bf16[6,128,128]{2,1,0:T(8,128)(2,1)}, bf16[6,128,128]{2,1,0:T(8,128)(2,1)S(1)}, u32[]{:S(2)}, u32[]{:S(2)}) collective-permute-start(bf16[6,128,128]{2,1,0:T(8,128)(2,1)} %get-tuple-element.24), channel_id=1, source_target_pairs={{0,15},{1,2},{2,1},{3,4},{4,3},{5,6},{6,5},{7,8},{8,7},{9,10},{10,... | collective-permute-start | bytes 589832 | tf_op jit(solution)/shard_map/ppermute | solution.py:555
  15.2 11.0 %local_one.1 = (f32[16,128,128]{2,1,0:T(8,128)}, f32[16,128,128]{2,1,0:T(8,128)}, bf16[6,256,768]{2,1,0:T(8,128)(2,1)}, bf16[16,128,128]{2,1,0:T(8,128)(2,1)}, f32[128,128]{1,0:T(8,128)}) custom-call(s32[16,12]{1,0:T(8,128)} %columns.3, bf16[16,128,128]{2,1,0:T(8,128)(2,1)} %get-tuple-element.26.x_in, bf16[192,128,128]{2,1,0:T(8,128)(2,1)} %bitcast.14, ...), custom_call_target="tpu_custom_call" | custom-call | flops 805306368 | bytes 6291456 | tf_op jit(solution)/shard_map/local_one/pallas_call | solution.py:622
  26.3 0.0 collective-permute-done.got_a
  26.3 0.0 collective-permute-done.1.got_b
  26.3 0.0 all-to-all-done.got
  26.3 6.6 %middle.1 = (f32[16,128,128]{2,1,0:T(8,128)}, bf16[16,128,128]{2,1,0:T(8,128)(2,1)}, bf16[16,32,128]{2,1,0:T(8,128)(2,1)}, bf16[6,128,128]{2,1,0:T(8,128)(2,1)}, bf16[6,128,128]{2,1,0:T(8,128)(2,1)}) custom-call(bf16[6,128,128]{2,1,0:T(8,128)(2,1)S(1)} %collective-permute-done.got_a, bf16[6,128,128]{2,1,0:T(8,128)(2,1)S(1)} %collective-permute-done.1.got_b, ...), custom_call_target="tpu_custom_call" | custom-call | tf_op jit(solution)/shard_map/middle/pallas_call | solution.py:638
  32.9 3.5 %all-to-all-start.1 = ((bf16[16,32,128]{2,1,0:T(8,128)(2,1)}), bf16[16,32,128]{2,1,0:T(8,128)(2,1)S(1)}, u32[]{:S(2)}, u32[]{:S(2)}) async-start(bf16[16,32,128]{2,1,0:T(8,128)(2,1)} %get-tuple-element.33), calls=%async_computation.1 | async-start | bytes 262144 | tf_op jit(solution)/shard_map/all_to_all | solution.py:556
  36.4 0.3 collective-permute-start.2
  36.7 4.4 %collective-permute-start.3 = (bf16[6,128,128]{2,1,0:T(8,128)(2,1)}, bf16[6,128,128]{2,1,0:T(8,128)(2,1)S(1)}, u32[]{:S(2)}, u32[]{:S(2)}) collective-permute-start(bf16[6,128,128]{2,1,0:T(8,128)(2,1)} %get-tuple-element.32), channel_id=1, source_target_pairs={{0,15},{1,2},{2,1},{3,4},{4,3},{5,6},{6,5},{7,8},{8,7},{9,10},{10,... | collective-permute-start | bytes 589832 | tf_op jit(solution)/shard_map/ppermute | solution.py:555
  41.1 10.1 %local_two.1 = (f32[16,128,128]{2,1,0:T(8,128)}, f32[16,128,128]{2,1,0:T(8,128)}, f32[16,128,128]{2,1,0:T(8,128)}, f32[2,8,128]{2,1,0:T(8,128)}) custom-call(s32[16,12]{1,0:T(8,128)} %columns.3, bf16[16,128,128]{2,1,0:T(8,128)(2,1)} %get-tuple-element.35.x_in, bf16[192,128,128]{2,1,0:T(8,128)(2,1)} %bitcast.15, f32[16,128,128]{2,1,0:T(8,128)} %bitcast.18, ...), custom_call_target="tpu_custom_call" | custom-call | flops 805306368 | bytes 6291456 | tf_op jit(solution)/shard_map/local_two/pallas_call | solution.py:653
  51.2 0.0 collective-permute-done.2.got_a
  51.2 0.0 collective-permute-done.3.got_b
  51.3 0.0 all-to-all-done.1.got
  51.3 6.2 %close.1 = (f32[16,128,128]{2,1,0:T(8,128)}, f32[16,2,128]{2,1,0:T(2,128)S(1)}) custom-call(bf16[6,128,128]{2,1,0:T(8,128)(2,1)S(1)} %collective-permute-done.2.got_a, bf16[6,128,128]{2,1,0:T(8,128)(2,1)S(1)} %collective-permute-done.3.got_b, bf16[16,32,128]{2,1,0:T(8,128)(2,1)S(1)} %all-to-all-done.1.got, bf16[6,256,768]{2,1,0:T(8,128)(2,1)} %get-tuple-element.27.edge_in, ...), custom_call_target="tpu_custom_call" | custom-call | tf_op jit(solution)/shard_map/close/pallas_call | solution.py:668
  57.5 9.1 %all_to_all.15 = f32[16,2,128]{2,1,0:T(2,128)S(1)} all-to-all(f32[16,2,128]{2,1,0:T(2,128)S(1)} %get-tuple-element.42), channel_id=1, replica_groups=mesh['member'=2,'patch'=16] {'patch'}, dimensions={0} | all-to-all | bytes 32768 | tf_op jit(solution)/shard_map/all_to_all | solution.py:683
  66.6 0.5 sqrt_bitcast_fusion
  (1 shorter events, 0.0 us)
Async XLA Ops:
  3.0 23.2 %all-to-all-start = ((bf16[16,32,128]{2,1,0:T(8,128)(2,1)}), bf16[16,32,128]{2,1,0:T(8,128)(2,1)S(1)}, u32[]{:S(2)}, u32[]{:S(2)}) async-start(bf16[16,32,128]{2,1,0:T(8,128)(2,1)} %get-tuple-element.25), calls=%async_computation | async-start | bytes 262144 | tf_op jit(solution)/shard_map/all_to_all | solution.py:556
  10.5 15.8 %collective-permute-start = (bf16[6,128,128]{2,1,0:T(8,128)(2,1)}, bf16[6,128,128]{2,1,0:T(8,128)(2,1)S(1)}, u32[]{:S(2)}, u32[]{:S(2)}) collective-permute-start(bf16[6,128,128]{2,1,0:T(8,128)(2,1)} %get-tuple-element.23), channel_id=1, source_target_pairs={{0,1},{1,0},{2,3},{3,2},{4,5},{5,4},{6,7},{7,6},{8,9},{9,8},{10,11... | collective-permute-start | bytes 589832 | tf_op jit(solution)/shard_map/ppermute | solution.py:553
  10.9 15.4 %collective-permute-start.1 = (bf16[6,128,128]{2,1,0:T(8,128)(2,1)}, bf16[6,128,128]{2,1,0:T(8,128)(2,1)S(1)}, u32[]{:S(2)}, u32[]{:S(2)}) collective-permute-start(bf16[6,128,128]{2,1,0:T(8,128)(2,1)} %get-tuple-element.24), channel_id=1, source_target_pairs={{0,15},{1,2},{2,1},{3,4},{4,3},{5,6},{6,5},{7,8},{8,7},{9,10},{10,... | collective-permute-start | bytes 589832 | tf_op jit(solution)/shard_map/ppermute | solution.py:555
  32.9 18.4 %all-to-all-start.1 = ((bf16[16,32,128]{2,1,0:T(8,128)(2,1)}), bf16[16,32,128]{2,1,0:T(8,128)(2,1)S(1)}, u32[]{:S(2)}, u32[]{:S(2)}) async-start(bf16[16,32,128]{2,1,0:T(8,128)(2,1)} %get-tuple-element.33), calls=%async_computation.1 | async-start | bytes 262144 | tf_op jit(solution)/shard_map/all_to_all | solution.py:556
  36.4 14.8 %collective-permute-start.2 = (bf16[6,128,128]{2,1,0:T(8,128)(2,1)}, bf16[6,128,128]{2,1,0:T(8,128)(2,1)S(1)}, u32[]{:S(2)}, u32[]{:S(2)}) collective-permute-start(bf16[6,128,128]{2,1,0:T(8,128)(2,1)} %get-tuple-element.31), channel_id=1, source_target_pairs={{0,1},{1,0},{2,3},{3,2},{4,5},{5,4},{6,7},{7,6},{8,9},{9,8},{10,11... | collective-permute-start | bytes 589832 | tf_op jit(solution)/shard_map/ppermute | solution.py:553
  36.7 14.5 %collective-permute-start.3 = (bf16[6,128,128]{2,1,0:T(8,128)(2,1)}, bf16[6,128,128]{2,1,0:T(8,128)(2,1)S(1)}, u32[]{:S(2)}, u32[]{:S(2)}) collective-permute-start(bf16[6,128,128]{2,1,0:T(8,128)(2,1)} %get-tuple-element.32), channel_id=1, source_target_pairs={{0,15},{1,2},{2,1},{3,4},{4,3},{5,6},{6,5},{7,8},{8,7},{9,10},{10,... | collective-permute-start | bytes 589832 | tf_op jit(solution)/shard_map/ppermute | solution.py:555

commit v6 on v4

v6 whole, which is shorter than its diff:
```python
import jax
import jax.numpy as jnp
from jax import lax
from jax.experimental import pallas as pl
from jax.experimental.pallas import tpu as pltpu
from jax.sharding import PartitionSpec as P


REACH = 6
STRIP = 32

step_size = 0.1
damping = 0.5
error_scale = 0.01
half_step = 0.5 * step_size

AXIS = "patch"
F32 = jnp.float32
BF16 = jnp.bfloat16
PLAIN = pl.BlockSpec(memory_space=pltpu.HBM)
WHOLE = pl.BlockSpec(memory_space=pltpu.VMEM)
SCALARS = pl.BlockSpec(memory_space=pltpu.SMEM)
SEMS = pltpu.SemaphoreType.DMA


def cost(flops, moved, exps=0):
    return pl.CostEstimate(flops=flops, bytes_accessed=moved, transcendentals=exps)


def in_hbm(*shapes):
    return tuple(pltpu.HBM(shape, dtype) for shape, dtype in shapes)


def hbm(*arrays):
    return tuple(pltpu.with_memory_space_constraint(v, pltpu.HBM) for v in arrays)


def like(*shapes):
    return tuple(jax.ShapeDtypeStruct(shape, dtype) for shape, dtype in shapes)


def part(src, dst, sems, c, group):
    at = pl.ds(c * group, group)
    return pltpu.make_async_copy(src.at[at], dst.at[at], sems.at[c])


def pair_columns(row_blocks, pair):
    reached = range((2 * pair - REACH) // 2, (2 * pair + 1 + REACH) // 2 + 1)
    count = row_blocks // 2
    return (
        [c for c in reached if c < 0],
        [c for c in reached if 0 <= c < count],
        [c for c in reached if c >= count],
    )


def edge_tiles(row_blocks):
    tiles = []
    for pair in range(row_blocks // 2):
        left, _, right = pair_columns(row_blocks, pair)
        tiles += [(pair, c) for c in left + right]
    return tiles


NT = (((1,), (1,)), ((), ()))


def side_by_side(blocks):
    return jnp.concatenate(blocks, axis=1)


def project(basis, x):
    rates = side_by_side([x[r] for r in range(x.shape[0])])
    return lax.dot_general(rates, basis[...], NT, preferred_element_type=F32).T


def fill_slots(me, projected, slots):
    devices, rank, _ = slots.shape
    for m in range(devices):
        level = max(m.bit_length() - 1, 0)
        slots[me ^ m] = projected[level * rank : (level + 1) * rank].astype(slots.dtype)


def send_copies(me, x, slots, slots_out, a_out, b_out, sems):
    row_blocks = x.shape[0]
    odd = lax.rem(me, 2)
    start_a = (1 - odd) * (row_blocks - REACH)
    start_b = odd * (row_blocks - REACH)
    return [
        pltpu.make_async_copy(slots, slots_out, sems.at[0]),
        pltpu.make_async_copy(x.at[pl.ds(start_a, REACH)], a_out, sems.at[1]),
        pltpu.make_async_copy(x.at[pl.ds(start_b, REACH)], b_out, sems.at[2]),
    ]


def open_kernel(
    p_in, basis_in, x_out, slots_out, a_out, b_out,
    p, basis, x, slots, p_sems, x_sem, basis_sem, send_sems,
):
    row_blocks, _, _ = p.shape
    chunks = p_sems.shape[0]
    group = row_blocks // chunks
    me = lax.axis_index(AXIS)
    load_basis = pltpu.make_async_copy(basis_in, basis, basis_sem)
    for c in range(chunks):
        part(p_in, p, p_sems, c, group).start()
    load_basis.start()
    for c in range(chunks):
        part(p_in, p, p_sems, c, group).wait()
        for r in range(c * group, (c + 1) * group):
            x[r] = jnp.exp(p[r]).astype(BF16).T
    send = send_copies(me, x, slots, slots_out, a_out, b_out, send_sems)
    send.append(pltpu.make_async_copy(x, x_out, x_sem))
    for copy in send[1:]:
        copy.start()
    load_basis.wait()
    fill_slots(me, project(basis, x), slots)
    send[0].start()
    for copy in send:
        copy.wait()


def find_blocks(columns, where):
    row_blocks, near_count = columns.shape
    total = row_blocks * lax.axis_size(AXIS)
    first = row_blocks * lax.axis_index(AXIS)

    def row(r, carry):
        for o in range(2 * REACH + 1):
            where[r, o] = row_blocks * near_count
        for k in range(near_count):
            offset = columns[r, k] - first - r
            offset = jnp.where(offset > REACH, offset - total, offset)
            offset = jnp.where(offset < -REACH, offset + total, offset)
            where[r, offset + REACH] = r * near_count + k
        return carry

    lax.fori_loop(0, row_blocks, row, 0)


def near_block(near, where, r, c):
    if abs(c - r) > REACH:
        return jnp.zeros(near.shape[1:], near.dtype)
    return near[where[r, c - r + REACH]]


def near_product(near, x, where, pair):
    own = pair_columns(x.shape[0], pair)[1]
    reached = range(2 * own[0], 2 * own[-1] + 2)
    tiles = [side_by_side([near_block(near, where, r, c) for c in reached]) for r in (2 * pair, 2 * pair + 1)]
    rates = side_by_side([x[c] for c in reached])
    return lax.dot_general(rates, jnp.concatenate(tiles, axis=0), NT, preferred_element_type=F32)


def strips(size):
    step = STRIP if size % STRIP == 0 else size
    return [slice(i, i + step) for i in range(0, size, step)]


def known_rates(velocity, state, near_term, rows):
    stiff, plate, direct, evolve = rows
    factor = 1.0 / (direct + damping * velocity)
    return (stiff * (plate - velocity) - near_term - evolve * state) * factor, factor


def in_pairs(pairs, wait, product, finish, store):
    wait(0)
    product(0)
    for pair in range(pairs):
        if pair + 1 < pairs:
            wait(pair + 1)
            product(pair + 1)
        finish(pair)
        store(pair)


def vector_loads(sources, targets, sems):
    return [
        pltpu.make_async_copy(src, dst, sems.at[q]) for q, (src, dst) in enumerate(zip(sources, targets))
    ]


def start_all(copies):
    for copy in copies:
        copy.start()


def wait_all(copies):
    for copy in copies:
        copy.wait()


def first_local_kernel(
    columns, x_in, near_in, p_in, s_in, stiff_in, plate_in, direct_in, evolve_in,
    known_out, factor_out, edge_out,
    x, near, p, s, stiff, plate, direct, evolve, known, factor, edge, products, turned_p, turned_s,
    where, x_sem, near_sems, p_sems, s_sems, vector_sems, known_sems, factor_sems, rest_sems,
):
    row_blocks, size, _ = x.shape
    pairs = row_blocks // 2
    span = (near.shape[0] - 1) // pairs
    vectors = (stiff, plate, direct, evolve)
    load_x = pltpu.make_async_copy(x_in, x, x_sem)
    load_vectors = vector_loads((stiff_in, plate_in, direct_in, evolve_in), vectors, vector_sems)

    def loads(c):
        return [part(near_in, near, near_sems, c, span), part(p_in, p, p_sems, c, 2), part(s_in, s, s_sems, c, 2)]

    def stores(c):
        return [part(known, known_out, known_sems, c, 2), part(factor, factor_out, factor_sems, c, 2)]

    start_all([load_x] + loads(0) + load_vectors)
    for c in range(1, pairs):
        start_all(loads(c))
    near[near.shape[0] - 1] = jnp.zeros(near.shape[1:], near.dtype)
    find_blocks(columns, where)
    wait_all(load_vectors + [load_x])

    def product(pair):
        products[pair] = near_product(near, x, where, pair)

    def finish(pair):
        for i in range(2):
            r = 2 * pair + i
            rows = [v[r : r + 1] for v in vectors]
            turned_p[i] = p[r].T
            turned_s[i] = s[r].T
            for at in strips(size):
                now = turned_p[i, at]
                velocity = jnp.exp(now)
                state = jnp.exp(-turned_s[i, at]) - velocity
                near_term = products[pair, at, i * size : (i + 1) * size]
                rate, scale = known_rates(velocity, state, near_term, rows)
                known[r, at] = now + step_size * rate
                factor[r, at] = step_size * scale

    in_pairs(
        pairs,
        lambda c: wait_all(loads(c)),
        product,
        finish,
        lambda c: start_all(stores(c)),
    )
    for n, (pair, c) in enumerate(edge_tiles(row_blocks)):
        for i in range(2):
            for j in range(2):
                edge[n, i * size : (i + 1) * size, j * size : (j + 1) * size] = near_block(
                    near, where, 2 * pair + i, 2 * c + j
                )
    store_edge = pltpu.make_async_copy(edge, edge_out, rest_sems.at[0])
    store_edge.start()
    for c in range(pairs):
        wait_all(stores(c))
    store_edge.wait()


def second_local_kernel(
    columns, x_in, near_in, p_in, s_in, p2_in, stiff_in, plate_in, direct_in, evolve_in, area_in,
    change_out, factor_out, new_s_out, errors_out,
    x, near, p, s, p2, stiff, plate, direct, evolve, area, change, factor, new_s, errors, products,
    turned_p, turned_s, ended_s,
    where, x_sem, near_sems, p_sems, s_sems, p2_sems, vector_sems, change_sems, factor_sems, new_s_sems, rest_sems,
):
    row_blocks, size, _ = x.shape
    pairs = row_blocks // 2
    span = (near.shape[0] - 1) // pairs
    vectors = (stiff, plate, direct, evolve, area)
    load_x = pltpu.make_async_copy(x_in, x, x_sem)
    load_vectors = vector_loads((stiff_in, plate_in, direct_in, evolve_in, area_in), vectors, vector_sems)

    def loads(c):
        return [
            part(near_in, near, near_sems, c, span),
            part(p_in, p, p_sems, c, 2),
            part(s_in, s, s_sems, c, 2),
            part(p2_in, p2, p2_sems, c, 2),
        ]

    def stores(c):
        return [
            part(change, change_out, change_sems, c, 2),
            part(factor, factor_out, factor_sems, c, 2),
            part(new_s, new_s_out, new_s_sems, c, 2),
        ]

    start_all([load_x] + loads(0) + load_vectors)
    for c in range(1, pairs):
        start_all(loads(c))
    near[near.shape[0] - 1] = jnp.zeros(near.shape[1:], near.dtype)
    find_blocks(columns, where)
    wait_all(load_vectors + [load_x])

    def product(pair):
        products[pair] = near_product(near, x, where, pair)

    def finish(pair):
        for i in range(2):
            r = 2 * pair + i
            rows = [v[r : r + 1] for v in vectors]
            turned_p[i] = p[r].T
            turned_s[i] = s[r].T
            for at in strips(size):
                before, now, start = turned_p[i, at], p2[r, at], turned_s[i, at]
                state_a = jnp.exp(-start) - jnp.exp(before)
                velocity = jnp.exp(now)
                state_b = jnp.exp(-(start + step_size * state_a)) - velocity
                near_term = products[pair, at, i * size : (i + 1) * size]
                rate, scale = known_rates(velocity, state_b, near_term, rows[:4])
                change[r, at] = half_step * rate - (half_step / step_size) * (now - before)
                factor[r, at] = half_step * scale
                ended_s[i, at] = start + half_step * (state_a + state_b)
                state_error = (half_step / error_scale) * (state_b - state_a)
                weighted = rows[4] * (state_error * state_error)
                errors[at] = weighted + errors[at] if r else weighted
            new_s[r] = ended_s[i].T

    in_pairs(
        pairs,
        lambda c: wait_all(loads(c)),
        product,
        finish,
        lambda c: start_all(stores(c)),
    )
    store_errors = pltpu.make_async_copy(errors, errors_out, rest_sems.at[0])
    store_errors.start()
    for c in range(pairs):
        wait_all(stores(c))
    store_errors.wait()


def couple(me, got, levels):
    devices = got.shape[0]
    sums = []
    for level in range(levels):
        total = got[me ^ (1 << level)].astype(F32)
        for m in range((1 << level) + 1, min(2 << level, devices)):
            total += got[me ^ m].astype(F32)
        sums.append(total)
    return jnp.concatenate(sums, axis=0).T.astype(BF16)


def pair_order(row_blocks):
    edged = {pair for pair, _ in edge_tiles(row_blocks)}
    pairs = range(row_blocks // 2)
    return [c for c in pairs if c not in edged] + [c for c in pairs if c in edged]


def outer_terms(coupled, coupling, halo, edge, pair, row_blocks):
    size = halo.shape[2]
    terms = jnp.dot(
        coupled, coupling[:, 2 * pair * size : 2 * (pair + 1) * size], preferred_element_type=F32
    )
    rates, tiles = [], []
    for n, (row_pair, c) in enumerate(edge_tiles(row_blocks)):
        if row_pair == pair:
            at = REACH + 2 * c if c < 0 else REACH + 2 * c - row_blocks
            tiles.append(edge[n])
            rates += [halo[at], halo[at + 1]]
    if tiles:
        terms += lax.dot_general(side_by_side(rates), side_by_side(tiles), NT, preferred_element_type=F32)
    return terms


def place_halo(me, got_a, got_b, halo):
    odd = lax.rem(me, 2)
    at_a = (1 - odd) * REACH
    at_b = odd * REACH
    for t in range(REACH):
        halo[at_a + t] = got_a[t]
        halo[at_b + t] = got_b[t]


def run_rows(order, first_edged, loads, outer, row, done, start):
    ahead = 4
    for copy in outer[:1]:
        copy.start()
    for c in order[:ahead]:
        for copy in loads(c):
            copy.start()
        if c == order[0]:
            for copy in outer[1:]:
                copy.start()
    start()
    for n, c in enumerate(order):
        if n == 0:
            outer[0].wait()
        if n == first_edged:
            for copy in outer[1:]:
                copy.wait()
        for copy in loads(c):
            copy.wait()
        if n + ahead < len(order):
            for copy in loads(order[n + ahead]):
                copy.start()
        row(c)
        done(c)


def middle_kernel(
    got_a, got_b, got, edge_in, coupling_in, basis_in, known_in, factor_in,
    p2_out, x_out, slots_out, a_out, b_out,
    halo, edge, coupling, basis, known, factor, p2, x, slots, coupled,
    outer_sems, known_sems, factor_sems, p2_sems, x_sem, send_sems,
):
    row_blocks, size, _ = known.shape
    me = lax.axis_index(AXIS)
    order = pair_order(row_blocks)
    outer = [
        pltpu.make_async_copy(coupling_in, coupling, outer_sems.at[0]),
        pltpu.make_async_copy(edge_in, edge, outer_sems.at[1]),
        pltpu.make_async_copy(basis_in, basis, outer_sems.at[2]),
    ]

    def loads(c):
        return [part(known_in, known, known_sems, c, 2), part(factor_in, factor, factor_sems, c, 2)]

    def start():
        coupled[...] = couple(me, got, basis.shape[0] // got.shape[1])
        place_halo(me, got_a, got_b, halo)

    def row(c):
        terms = outer_terms(coupled[...], coupling, halo, edge, c, row_blocks)
        for i in range(2):
            r = 2 * c + i
            value = known[r] - factor[r] * terms[:, i * size : (i + 1) * size]
            p2[r] = value
            x[r] = jnp.exp(value).astype(BF16)

    def done(c):
        part(p2, p2_out, p2_sems, c, 2).start()

    run_rows(order, order.index(0), loads, outer, row, done, start)
    send = send_copies(me, x, slots, slots_out, a_out, b_out, send_sems)
    send.append(pltpu.make_async_copy(x, x_out, x_sem))
    start_all(send[1:])
    fill_slots(me, project(basis, x), slots)
    send[0].start()
    wait_all(send + [part(p2, p2_out, p2_sems, c, 2) for c in order])


def close_kernel(
    got_a, got_b, got, edge_in, coupling_in, p2_in, change_in, factor_in, area_in, errors_in,
    new_p_out, parts_out,
    halo, edge, coupling, p2, change, factor, new_p, coupled, area, errors,
    outer_sems, p2_sems, change_sems, factor_sems, new_p_sems,
):
    row_blocks, size, _ = change.shape
    me = lax.axis_index(AXIS)
    order = pair_order(row_blocks)
    outer = [
        pltpu.make_async_copy(coupling_in, coupling, outer_sems.at[0]),
        pltpu.make_async_copy(edge_in, edge, outer_sems.at[1]),
    ]
    extra = [
        pltpu.make_async_copy(area_in, area, outer_sems.at[2]),
        pltpu.make_async_copy(errors_in, errors, outer_sems.at[3]),
    ]

    def loads(c):
        return [
            part(change_in, change, change_sems, c, 2),
            part(factor_in, factor, factor_sems, c, 2),
            part(p2_in, p2, p2_sems, c, 2),
        ]

    def start():
        start_all(extra)
        coupled[...] = couple(me, got, coupling.shape[0] // got.shape[1])
        place_halo(me, got_a, got_b, halo)
        wait_all(extra)

    def row(c):
        terms = outer_terms(coupled[...], coupling, halo, edge, c, row_blocks)
        for i in range(2):
            r = 2 * c + i
            move = change[r] - factor[r] * terms[:, i * size : (i + 1) * size]
            new_p[r] = (p2[r] + move).T
            rate_error = (1.0 / error_scale) * move
            errors[...] += area[r : r + 1] * (rate_error * rate_error)

    def done(c):
        part(new_p, new_p_out, new_p_sems, c, 2).start()

    run_rows(order, order.index(0), loads, outer, row, done, start)
    total = jnp.sum(errors[...].T, axis=0, keepdims=True)
    areas = jnp.sum(jnp.sum(area[...], axis=0, keepdims=True), axis=1, keepdims=True)
    both = jnp.concatenate([total, jnp.broadcast_to(areas, total.shape)], axis=0)
    for j in range(parts_out.shape[0]):
        parts_out[j] = both
    wait_all([part(new_p, new_p_out, new_p_sems, c, 2) for c in order])


def exchange(side_a, side_b, slots):
    count = lax.axis_size(AXIS)
    got_a = lax.ppermute(side_a, AXIS, [(i, i ^ 1) for i in range(count)])
    pairs = [(i, (i - 1) % count if i % 2 == 0 else (i + 1) % count) for i in range(count)]
    got_b = lax.ppermute(side_b, AXIS, pairs)
    got = lax.all_to_all(slots, AXIS, 0, 0)
    return got_a, got_b, got


def on_device(
    log_rate,
    log_state,
    near_blocks,
    near_columns,
    far_basis,
    far_coupling,
    self_stiffness,
    plate_rate,
    direct_effect,
    evolution_effect,
    triangle_area,
):
    rows, cols = log_rate.shape
    row_blocks, near_count, size, _ = near_blocks.shape
    levels, rank, _ = far_basis.shape
    devices = lax.axis_size(AXIS)
    p = log_rate.reshape(row_blocks, size, cols)
    s = log_state.reshape(row_blocks, size, cols)
    basis = far_basis.reshape(levels * rank, rows)
    coupling = far_coupling.reshape(levels * rank, rows)
    stiff, plate, direct, evolve, area = (
        v.reshape(row_blocks, size)
        for v in (self_stiffness, plate_rate, direct_effect, evolution_effect, triangle_area)
    )
    pairs = row_blocks // 2
    flat_near = near_blocks.reshape(row_blocks * near_count, size, size)
    state = ((row_blocks, size, cols), F32)
    x_kind = ((row_blocks, size, cols), BF16)
    slots_kind = ((devices, rank, cols), BF16)
    side_kind = ((REACH, size, cols), BF16)
    edge_kind = ((len(edge_tiles(row_blocks)), 2 * size, 2 * size), BF16)
    basis_kind = ((levels * rank, rows), BF16)
    near_kind = ((row_blocks * near_count + 1, size, size), BF16)
    halo_kind = ((2 * REACH, size, cols), BF16)
    vector_kind = ((row_blocks, size), F32)
    errors_kind = ((cols, size), F32)
    products_kind = ((pairs, cols, 2 * size), F32)
    coupled_kind = ((cols, levels * rank), BF16)
    turned_kind = ((2, cols, size), F32)
    where_kind = pltpu.SMEM((row_blocks, 2 * REACH + 1), jnp.int32)
    loads = 4 if row_blocks % 4 == 0 else row_blocks
    near_flops = 2 * rows * near_count * size * cols

    def vmem(*kinds):
        return [pltpu.VMEM(shape, dtype) for shape, dtype in kinds]

    small = pltpu.CompilerParams(vmem_limit_bytes=40 * 1024 * 1024)
    x, slots, side_a, side_b = pl.pallas_call(
        open_kernel,
        out_shape=in_hbm(x_kind, slots_kind, side_kind, side_kind),
        in_specs=[PLAIN] * 2,
        out_specs=(PLAIN,) * 4,
        scratch_shapes=vmem(state, basis_kind, x_kind, slots_kind)
        + [SEMS((loads,)), SEMS(()), SEMS(()), SEMS((3,))],
        name="open",
    )(*hbm(p, basis))

    got_a, got_b, got = exchange(side_a, side_b, slots)
    known, factor, edge = pl.pallas_call(
        first_local_kernel,
        out_shape=in_hbm(state, state, edge_kind),
        in_specs=[SCALARS] + [PLAIN] * 8,
        out_specs=(PLAIN,) * 3,
        scratch_shapes=vmem(
            x_kind, near_kind, state, state, *[vector_kind] * 4, state, state, edge_kind, products_kind,
            turned_kind, turned_kind,
        )
        + [where_kind, SEMS(())]
        + [SEMS((pairs,))] * 3
        + [SEMS((4,)), SEMS((pairs,)), SEMS((pairs,)), SEMS((1,))],
        cost_estimate=cost(near_flops, near_blocks.size * 2),
        name="local_one",
    )(near_columns, *hbm(x, flat_near, p, s, stiff, plate, direct, evolve))

    p2, x, slots, side_a, side_b = pl.pallas_call(
        middle_kernel,
        out_shape=in_hbm(state, x_kind, slots_kind, side_kind, side_kind),
        in_specs=[WHOLE] * 3 + [PLAIN] * 5,
        out_specs=(PLAIN,) * 5,
        scratch_shapes=vmem(
            halo_kind, edge_kind, basis_kind, basis_kind, state, state, state, x_kind, slots_kind, coupled_kind
        )
        + [SEMS((3,)), SEMS((pairs,)), SEMS((pairs,)), SEMS((pairs,)), SEMS(()), SEMS((3,))],
        compiler_params=small,
        name="middle",
    )(got_a, got_b, got, *hbm(edge, coupling, basis, known, factor))

    got_a, got_b, got = exchange(side_a, side_b, slots)
    change, factor, new_s, errors = pl.pallas_call(
        second_local_kernel,
        out_shape=in_hbm(state, state, state, errors_kind),
        in_specs=[SCALARS] + [PLAIN] * 10,
        out_specs=(PLAIN,) * 4,
        scratch_shapes=vmem(
            x_kind, near_kind, state, state, state, *[vector_kind] * 5, state, state, state, errors_kind,
            products_kind, turned_kind, turned_kind, turned_kind,
        )
        + [where_kind, SEMS(())]
        + [SEMS((pairs,))] * 4
        + [SEMS((5,))]
        + [SEMS((pairs,))] * 3
        + [SEMS((1,))],
        cost_estimate=cost(near_flops, near_blocks.size * 2),
        name="local_two",
    )(near_columns, *hbm(x, flat_near, p, s, p2, stiff, plate, direct, evolve, area))

    new_p, parts = pl.pallas_call(
        close_kernel,
        out_shape=in_hbm(state) + like(((devices, 2, cols), F32)),
        in_specs=[WHOLE] * 3 + [PLAIN] * 7,
        out_specs=(PLAIN, WHOLE),
        scratch_shapes=vmem(
            halo_kind, edge_kind, basis_kind, state, state, state, state, coupled_kind, vector_kind, errors_kind
        )
        + [SEMS((4,))]
        + [SEMS((pairs,))] * 4,
        compiler_params=small,
        name="close",
    )(got_a, got_b, got, *hbm(edge, coupling, p2, change, factor, area, errors))

    totals = lax.all_to_all(parts, AXIS, 0, 0).sum(axis=0)
    error_norm = jnp.sqrt(totals[0] / totals[1] + 1e-06)
    return new_p.reshape(rows, cols), new_s.reshape(rows, cols), error_norm


def solution(mesh):
    split = P(("member", "patch"))
    in_specs = (
        P(("member", "patch"), None),
        P(("member", "patch"), None),
        P(("member", "patch"), None, None, None),
        P(("member", "patch"), None),
        P("member", None, "patch"),
        P("member", None, "patch"),
        split,
        split,
        split,
        split,
        split,
    )
    out_specs = (P(("member", "patch"), None), P(("member", "patch"), None), P("member"))
    return jax.shard_map(
        on_device, mesh=mesh, in_specs=in_specs, out_specs=out_specs, check_vma=False
    )
```

time: 62 us -> 65.3 us (1.053)
  Pallas kernels: 30.7 us -> 34 us
    pallas_call x1, Pallas kernels: 9.19 us -> 10.2 us  [on_device(): pl.pallas_call(second_local_kernel, out_shape=in_hbm(state, state, state,...]
    pallas_call x1, Pallas kernels: 4.77 us -> 5.75 us  [on_device(): pl.pallas_call(close_kernel, out_shape=in_hbm(state) + like(((devices, 2,...]
    pallas_call x1, Pallas kernels: 9.37 us -> 10.3 us  [on_device(): pl.pallas_call(first_local_kernel, out_shape=in_hbm(state, state, edge_ki...]
  transfers between devices with their start and end apart: 6 -> 6, of which waited for: 0 -> 0; matrix products, arithmetic and copies ran while one was open for 0% -> 0% of each run, Pallas kernels for 30% -> 32%
where the time goes in v6:
time: 65.3 us; the launch traced here: 64.8 us
  Pallas kernels  34 us (52%)
  starting transfers between devices  20.4 us (31%)
  blocking collectives  9.07 us (14%)
  between operations  0.74 us (1%)
    all_to_all x2, starting transfers between devices, exchange(): got = lax.all_to_all(slots, AXIS, 0, 0)  10.9 us
    pallas_call x1, Pallas kernels, on_device(): pl.pallas_call(first_local_kernel, out_shape=in_hbm(state, state, edge_ki...  10.3 us
    pallas_call x1, Pallas kernels, on_device(): pl.pallas_call(second_local_kernel, out_shape=in_hbm(state, state, state,...  10.2 us
    all_to_all x1, blocking collectives, on_device(): totals = lax.all_to_all(parts, AXIS, 0, 0).sum(axis=0)  9.07 us
    ppermute x2, starting transfers between devices, exchange(): got_b = lax.ppermute(side_b, AXIS, pairs)  8.75 us
    pallas_call x1, Pallas kernels, on_device(): pl.pallas_call(close_kernel, out_shape=in_hbm(state) + like(((devices, 2,...  5.75 us
    pallas_call x1, Pallas kernels, on_device(): pl.pallas_call(middle_kernel, out_shape=in_hbm(state, x_kind, slots_kind,...  5.3 us
    pallas_call x1, Pallas kernels, on_device(): pl.pallas_call(open_kernel, out_shape=in_hbm(x_kind, slots_kind, side_kin...  2.48 us
  transfers between devices with their start and end apart: 6, of which 0 were waited for; matrix products, arithmetic and copies ran while one was open for 0% of the time, Pallas kernels for 32%

profile of v6, /device:TPU:0, one launch (start us, length us, event | category | flops | bytes accessed | tf_op | source)
XLA Modules:
  0.0 64.8 jit_solution(2725261369818597359)
XLA Ops:
  0.6 2.5 %open.1 = (bf16[16,128,128]{2,1,0:T(8,128)(2,1)}, bf16[16,32,128]{2,1,0:T(8,128)(2,1)}, bf16[6,128,128]{2,1,0:T(8,128)(2,1)}, bf16[6,128,128]{2,1,0:T(8,128)(2,1)}) custom-call(f32[16,128,128]{2,1,0:T(8,128)} %bitcast.16, bf16[128,2048]{1,0:T(8,128)(2,1)} %bitcast.21), custom_call_target="tpu_custom_call" | custom-call | tf_op jit(solution)/shard_map/open/pallas_call | solution.py:550
  3.1 7.4 %all-to-all-start = ((bf16[16,32,128]{2,1,0:T(8,128)(2,1)}), bf16[16,32,128]{2,1,0:T(8,128)(2,1)S(1)}, u32[]{:S(2)}, u32[]{:S(2)}) async-start(bf16[16,32,128]{2,1,0:T(8,128)(2,1)} %get-tuple-element.23), calls=%async_computation | async-start | bytes 262144 | tf_op jit(solution)/shard_map/all_to_all | solution.py:498
  10.6 0.4 collective-permute-start
  11.0 4.3 %collective-permute-start.1 = (bf16[6,128,128]{2,1,0:T(8,128)(2,1)}, bf16[6,128,128]{2,1,0:T(8,128)(2,1)S(1)}, u32[]{:S(2)}, u32[]{:S(2)}) collective-permute-start(bf16[6,128,128]{2,1,0:T(8,128)(2,1)} %get-tuple-element.22), channel_id=1, source_target_pairs={{0,15},{1,2},{2,1},{3,4},{4,3},{5,6},{6,5},{7,8},{8,7},{9,10},{10,... | collective-permute-start | bytes 589832 | tf_op jit(solution)/shard_map/ppermute | solution.py:497
  15.3 10.3 %local_one.1 = (f32[16,128,128]{2,1,0:T(8,128)}, f32[16,128,128]{2,1,0:T(8,128)}, bf16[12,256,256]{2,1,0:T(8,128)(2,1)}) custom-call(s32[16,12]{1,0:T(8,128)} %columns.3, bf16[16,128,128]{2,1,0:T(8,128)(2,1)} %get-tuple-element.24.x_in, bf16[192,128,128]{2,1,0:T(8,128)(2,1)} %bitcast.14, f32[16,128,128]{2,1,0:T(8,128)} %bitcast.17, ...), custom_call_target="tpu_custom_call" | custom-call | flops 805306368 | bytes 6291456 | tf_op jit(solution)/shard_map/local_one/pallas_call | solution.py:561
  25.6 0.0 collective-permute-done.got_a
  25.6 0.0 collective-permute-done.1.got_b
  25.6 0.0 all-to-all-done.got
  25.6 5.3 %middle.1 = (f32[16,128,128]{2,1,0:T(8,128)}, bf16[16,128,128]{2,1,0:T(8,128)(2,1)}, bf16[16,32,128]{2,1,0:T(8,128)(2,1)}, bf16[6,128,128]{2,1,0:T(8,128)(2,1)}, bf16[6,128,128]{2,1,0:T(8,128)(2,1)}) custom-call(bf16[6,128,128]{2,1,0:T(8,128)(2,1)S(1)} %collective-permute-done.got_a, bf16[6,128,128]{2,1,0:T(8,128)(2,1)S(1)} %collective-permute-done.1.got_b, ...), custom_call_target="tpu_custom_call" | custom-call | tf_op jit(solution)/shard_map/middle/pallas_call | solution.py:577
  30.9 3.5 %all-to-all-start.1 = ((bf16[16,32,128]{2,1,0:T(8,128)(2,1)}), bf16[16,32,128]{2,1,0:T(8,128)(2,1)S(1)}, u32[]{:S(2)}, u32[]{:S(2)}) async-start(bf16[16,32,128]{2,1,0:T(8,128)(2,1)} %get-tuple-element.30), calls=%async_computation.1 | async-start | bytes 262144 | tf_op jit(solution)/shard_map/all_to_all | solution.py:498
  34.5 0.3 collective-permute-start.2
  34.8 4.4 %collective-permute-start.3 = (bf16[6,128,128]{2,1,0:T(8,128)(2,1)}, bf16[6,128,128]{2,1,0:T(8,128)(2,1)S(1)}, u32[]{:S(2)}, u32[]{:S(2)}) collective-permute-start(bf16[6,128,128]{2,1,0:T(8,128)(2,1)} %get-tuple-element.29), channel_id=1, source_target_pairs={{0,15},{1,2},{2,1},{3,4},{4,3},{5,6},{6,5},{7,8},{8,7},{9,10},{10,... | collective-permute-start | bytes 589832 | tf_op jit(solution)/shard_map/ppermute | solution.py:497
  39.2 10.2 %local_two.1 = (f32[16,128,128]{2,1,0:T(8,128)}, f32[16,128,128]{2,1,0:T(8,128)}, f32[16,128,128]{2,1,0:T(8,128)}, f32[128,128]{1,0:T(8,128)}) custom-call(s32[16,12]{1,0:T(8,128)} %columns.3, bf16[16,128,128]{2,1,0:T(8,128)(2,1)} %get-tuple-element.32.x_in, bf16[192,128,128]{2,1,0:T(8,128)(2,1)} %bitcast.15, f32[16,128,128]{2,1,0:T(8,128)} %bitcast.18, ...), custom_call_target="tpu_custom_call" | custom-call | flops 805306368 | bytes 6291456 | tf_op jit(solution)/shard_map/local_two/pallas_call | solution.py:591
  49.4 0.0 collective-permute-done.2.got_a
  49.4 0.0 collective-permute-done.3.got_b
  49.4 0.0 all-to-all-done.1.got
  49.4 5.8 %close.1 = (f32[16,128,128]{2,1,0:T(8,128)}, f32[16,2,128]{2,1,0:T(2,128)S(1)}) custom-call(bf16[6,128,128]{2,1,0:T(8,128)(2,1)S(1)} %collective-permute-done.2.got_a, bf16[6,128,128]{2,1,0:T(8,128)(2,1)S(1)} %collective-permute-done.3.got_b, bf16[16,32,128]{2,1,0:T(8,128)(2,1)S(1)} %all-to-all-done.1.got, bf16[12,256,256]{2,1,0:T(8,128)(2,1)} %get-tuple-element.25.edge_in, ...), custom_call_target="tpu_custom_call" | custom-call | tf_op jit(solution)/shard_map/close/pallas_call | solution.py:609
  55.2 9.1 %all_to_all.15 = f32[16,2,128]{2,1,0:T(2,128)S(1)} all-to-all(f32[16,2,128]{2,1,0:T(2,128)S(1)} %get-tuple-element.38), channel_id=1, replica_groups=mesh['member'=2,'patch'=16] {'patch'}, dimensions={0} | all-to-all | bytes 32768 | tf_op jit(solution)/shard_map/all_to_all | solution.py:623
  64.3 0.5 sqrt_bitcast_fusion
  (1 shorter events, 0.0 us)
Async XLA Ops:
  3.1 22.5 %all-to-all-start = ((bf16[16,32,128]{2,1,0:T(8,128)(2,1)}), bf16[16,32,128]{2,1,0:T(8,128)(2,1)S(1)}, u32[]{:S(2)}, u32[]{:S(2)}) async-start(bf16[16,32,128]{2,1,0:T(8,128)(2,1)} %get-tuple-element.23), calls=%async_computation | async-start | bytes 262144 | tf_op jit(solution)/shard_map/all_to_all | solution.py:498
  10.6 15.1 %collective-permute-start = (bf16[6,128,128]{2,1,0:T(8,128)(2,1)}, bf16[6,128,128]{2,1,0:T(8,128)(2,1)S(1)}, u32[]{:S(2)}, u32[]{:S(2)}) collective-permute-start(bf16[6,128,128]{2,1,0:T(8,128)(2,1)} %get-tuple-element.21), channel_id=1, source_target_pairs={{0,1},{1,0},{2,3},{3,2},{4,5},{5,4},{6,7},{7,6},{8,9},{9,8},{10,11... | collective-permute-start | bytes 589832 | tf_op jit(solution)/shard_map/ppermute | solution.py:495
  11.0 14.7 %collective-permute-start.1 = (bf16[6,128,128]{2,1,0:T(8,128)(2,1)}, bf16[6,128,128]{2,1,0:T(8,128)(2,1)S(1)}, u32[]{:S(2)}, u32[]{:S(2)}) collective-permute-start(bf16[6,128,128]{2,1,0:T(8,128)(2,1)} %get-tuple-element.22), channel_id=1, source_target_pairs={{0,15},{1,2},{2,1},{3,4},{4,3},{5,6},{6,5},{7,8},{8,7},{9,10},{10,... | collective-permute-start | bytes 589832 | tf_op jit(solution)/shard_map/ppermute | solution.py:497
  30.9 18.5 %all-to-all-start.1 = ((bf16[16,32,128]{2,1,0:T(8,128)(2,1)}), bf16[16,32,128]{2,1,0:T(8,128)(2,1)S(1)}, u32[]{:S(2)}, u32[]{:S(2)}) async-start(bf16[16,32,128]{2,1,0:T(8,128)(2,1)} %get-tuple-element.30), calls=%async_computation.1 | async-start | bytes 262144 | tf_op jit(solution)/shard_map/all_to_all | solution.py:498
  34.5 14.9 %collective-permute-start.2 = (bf16[6,128,128]{2,1,0:T(8,128)(2,1)}, bf16[6,128,128]{2,1,0:T(8,128)(2,1)S(1)}, u32[]{:S(2)}, u32[]{:S(2)}) collective-permute-start(bf16[6,128,128]{2,1,0:T(8,128)(2,1)} %get-tuple-element.28), channel_id=1, source_target_pairs={{0,1},{1,0},{2,3},{3,2},{4,5},{5,4},{6,7},{7,6},{8,9},{9,8},{10,11... | collective-permute-start | bytes 589832 | tf_op jit(solution)/shard_map/ppermute | solution.py:495
  34.8 14.6 %collective-permute-start.3 = (bf16[6,128,128]{2,1,0:T(8,128)(2,1)}, bf16[6,128,128]{2,1,0:T(8,128)(2,1)S(1)}, u32[]{:S(2)}, u32[]{:S(2)}) collective-permute-start(bf16[6,128,128]{2,1,0:T(8,128)(2,1)} %get-tuple-element.29), channel_id=1, source_target_pairs={{0,15},{1,2},{2,1},{3,4},{4,3},{5,6},{6,5},{7,8},{8,7},{9,10},{10,... | collective-permute-start | bytes 589832 | tf_op jit(solution)/shard_map/ppermute | solution.py:497

commit v7 on v6

--- a/solution.py
+++ b/solution.py
@@ -8,6 +8,8 @@
 
 REACH = 6
 STRIP = 32
+AHEAD = 3
+BUSY = 10**10
 
 step_size = 0.1
 damping = 0.5
@@ -33,6 +35,10 @@
 
 def hbm(*arrays):
     return tuple(pltpu.with_memory_space_constraint(v, pltpu.HBM) for v in arrays)
+
+
+def resident(*arrays):
+    return tuple(pltpu.with_memory_space_constraint(v, pltpu.VMEM) for v in arrays)
 
 
 def like(*shapes):
@@ -127,7 +133,7 @@
 
     def row(r, carry):
         for o in range(2 * REACH + 1):
-            where[r, o] = row_blocks * near_count
+            where[r, o] = -1
         for k in range(near_count):
             offset = columns[r, k] - first - r
             offset = jnp.where(offset > REACH, offset - total, offset)
@@ -139,9 +145,14 @@
 
 
 def near_block(near, where, r, c):
-    if abs(c - r) > REACH:
+    offset = c - r
+    if abs(offset) > REACH:
         return jnp.zeros(near.shape[1:], near.dtype)
-    return near[where[r, c - r + REACH]]
+    at = where[r, offset + REACH]
+    block = near[jnp.maximum(at, 0)]
+    if offset == 0 or abs(offset) == REACH:
+        return block
+    return jnp.where(at >= 0, block, jnp.zeros_like(block))
 
 
 def near_product(near, x, where, pair):
@@ -174,12 +185,6 @@
         store(pair)
 
 
-def vector_loads(sources, targets, sems):
-    return [
-        pltpu.make_async_copy(src, dst, sems.at[q]) for q, (src, dst) in enumerate(zip(sources, targets))
-    ]
-
-
 def start_all(copies):
     for copy in copies:
         copy.start()
@@ -191,32 +196,32 @@
 
 
 def first_local_kernel(
-    columns, x_in, near_in, p_in, s_in, stiff_in, plate_in, direct_in, evolve_in,
+    columns, x_in, near_in, p, s, stiff, plate, direct, evolve,
     known_out, factor_out, edge_out,
-    x, near, p, s, stiff, plate, direct, evolve, known, factor, edge, products, turned_p, turned_s,
-    where, x_sem, near_sems, p_sems, s_sems, vector_sems, known_sems, factor_sems, rest_sems,
+    x, near, known, factor, edge, products, turned_p, turned_s,
+    where, x_sem, near_sems, known_sems, factor_sems, rest_sems,
 ):
     row_blocks, size, _ = x.shape
     pairs = row_blocks // 2
-    span = (near.shape[0] - 1) // pairs
     vectors = (stiff, plate, direct, evolve)
+    span = near.shape[0] // pairs
     load_x = pltpu.make_async_copy(x_in, x, x_sem)
-    load_vectors = vector_loads((stiff_in, plate_in, direct_in, evolve_in), vectors, vector_sems)
 
     def loads(c):
-        return [part(near_in, near, near_sems, c, span), part(p_in, p, p_sems, c, 2), part(s_in, s, s_sems, c, 2)]
+        return [part(near_in, near, near_sems, c, span)]
 
     def stores(c):
         return [part(known, known_out, known_sems, c, 2), part(factor, factor_out, factor_sems, c, 2)]
 
-    start_all([load_x] + loads(0) + load_vectors)
-    for c in range(1, pairs):
+    load_x.start()
+    for c in range(AHEAD):
         start_all(loads(c))
-    near[near.shape[0] - 1] = jnp.zeros(near.shape[1:], near.dtype)
     find_blocks(columns, where)
-    wait_all(load_vectors + [load_x])
+    load_x.wait()
 
     def product(pair):
+        if pair + AHEAD < pairs:
+            start_all(loads(pair + AHEAD))
         products[pair] = near_product(near, x, where, pair)
 
     def finish(pair):
@@ -255,26 +260,20 @@
 
 
 def second_local_kernel(
-    columns, x_in, near_in, p_in, s_in, p2_in, stiff_in, plate_in, direct_in, evolve_in, area_in,
+    columns, x_in, near_in, p, s, p2_in, stiff, plate, direct, evolve, area,
     change_out, factor_out, new_s_out, errors_out,
-    x, near, p, s, p2, stiff, plate, direct, evolve, area, change, factor, new_s, errors, products,
+    x, near, p2, change, factor, new_s, errors, products,
     turned_p, turned_s, ended_s,
-    where, x_sem, near_sems, p_sems, s_sems, p2_sems, vector_sems, change_sems, factor_sems, new_s_sems, rest_sems,
+    where, x_sem, near_sems, p2_sems, change_sems, factor_sems, new_s_sems, rest_sems,
 ):
     row_blocks, size, _ = x.shape
     pairs = row_blocks // 2
-    span = (near.shape[0] - 1) // pairs
     vectors = (stiff, plate, direct, evolve, area)
+    span = near.shape[0] // pairs
     load_x = pltpu.make_async_copy(x_in, x, x_sem)
-    load_vectors = vector_loads((stiff_in, plate_in, direct_in, evolve_in, area_in), vectors, vector_sems)
 
     def loads(c):
-        return [
-            part(near_in, near, near_sems, c, span),
-            part(p_in, p, p_sems, c, 2),
-            part(s_in, s, s_sems, c, 2),
-            part(p2_in, p2, p2_sems, c, 2),
-        ]
+        return [part(near_in, near, near_sems, c, span), part(p2_in, p2, p2_sems, c, 2)]
 
     def stores(c):
         return [
@@ -283,14 +282,15 @@
             part(new_s, new_s_out, new_s_sems, c, 2),
         ]
 
-    start_all([load_x] + loads(0) + load_vectors)
-    for c in range(1, pairs):
+    load_x.start()
+    for c in range(AHEAD):
         start_all(loads(c))
-    near[near.shape[0] - 1] = jnp.zeros(near.shape[1:], near.dtype)
     find_blocks(columns, where)
-    wait_all(load_vectors + [load_x])
+    load_x.wait()
 
     def product(pair):
+        if pair + AHEAD < pairs:
+            start_all(loads(pair + AHEAD))
         products[pair] = near_product(near, x, where, pair)
 
     def finish(pair):
@@ -372,43 +372,33 @@
 
 def run_rows(order, first_edged, loads, outer, row, done, start):
     ahead = 4
-    for copy in outer[:1]:
-        copy.start()
     for c in order[:ahead]:
-        for copy in loads(c):
-            copy.start()
+        start_all(loads(c))
         if c == order[0]:
-            for copy in outer[1:]:
-                copy.start()
+            start_all(outer)
     start()
     for n, c in enumerate(order):
-        if n == 0:
-            outer[0].wait()
         if n == first_edged:
-            for copy in outer[1:]:
-                copy.wait()
-        for copy in loads(c):
-            copy.wait()
+            wait_all(outer)
+        wait_all(loads(c))
         if n + ahead < len(order):
-            for copy in loads(order[n + ahead]):
-                copy.start()
+            start_all(loads(order[n + ahead]))
         row(c)
         done(c)
 
 
 def middle_kernel(
-    got_a, got_b, got, edge_in, coupling_in, basis_in, known_in, factor_in,
+    got_a, got_b, got, edge_in, coupling, basis_in, known_in, factor_in,
     p2_out, x_out, slots_out, a_out, b_out,
-    halo, edge, coupling, basis, known, factor, p2, x, slots, coupled,
+    halo, edge, basis, known, factor, p2, x, slots, coupled,
     outer_sems, known_sems, factor_sems, p2_sems, x_sem, send_sems,
 ):
     row_blocks, size, _ = known.shape
     me = lax.axis_index(AXIS)
     order = pair_order(row_blocks)
     outer = [
-        pltpu.make_async_copy(coupling_in, coupling, outer_sems.at[0]),
-        pltpu.make_async_copy(edge_in, edge, outer_sems.at[1]),
-        pltpu.make_async_copy(basis_in, basis, outer_sems.at[2]),
+        pltpu.make_async_copy(edge_in, edge, outer_sems.at[0]),
+        pltpu.make_async_copy(basis_in, basis, outer_sems.at[1]),
     ]
 
     def loads(c):
@@ -439,21 +429,18 @@
 
 
 def close_kernel(
-    got_a, got_b, got, edge_in, coupling_in, p2_in, change_in, factor_in, area_in, errors_in,
+    got_a, got_b, got, edge_in, coupling, p2_in, change_in, factor_in, area_in, errors_in,
     new_p_out, parts_out,
-    halo, edge, coupling, p2, change, factor, new_p, coupled, area, errors,
+    halo, edge, p2, change, factor, new_p, coupled, area, errors,
     outer_sems, p2_sems, change_sems, factor_sems, new_p_sems,
 ):
     row_blocks, size, _ = change.shape
     me = lax.axis_index(AXIS)
     order = pair_order(row_blocks)
-    outer = [
-        pltpu.make_async_copy(coupling_in, coupling, outer_sems.at[0]),
-        pltpu.make_async_copy(edge_in, edge, outer_sems.at[1]),
-    ]
+    outer = [pltpu.make_async_copy(edge_in, edge, outer_sems.at[0])]
     extra = [
-        pltpu.make_async_copy(area_in, area, outer_sems.at[2]),
-        pltpu.make_async_copy(errors_in, errors, outer_sems.at[3]),
+        pltpu.make_async_copy(area_in, area, outer_sems.at[1]),
+        pltpu.make_async_copy(errors_in, errors, outer_sems.at[2]),
     ]
 
     def loads(c):
@@ -532,7 +519,7 @@
     side_kind = ((REACH, size, cols), BF16)
     edge_kind = ((len(edge_tiles(row_blocks)), 2 * size, 2 * size), BF16)
     basis_kind = ((levels * rank, rows), BF16)
-    near_kind = ((row_blocks * near_count + 1, size, size), BF16)
+    near_kind = ((row_blocks * near_count, size, size), BF16)
     halo_kind = ((2 * REACH, size, cols), BF16)
     vector_kind = ((row_blocks, size), F32)
     errors_kind = ((cols, size), F32)
@@ -541,12 +528,12 @@
     turned_kind = ((2, cols, size), F32)
     where_kind = pltpu.SMEM((row_blocks, 2 * REACH + 1), jnp.int32)
     loads = 4 if row_blocks % 4 == 0 else row_blocks
+    small = pltpu.CompilerParams(vmem_limit_bytes=32 * 1024 * 1024)
     near_flops = 2 * rows * near_count * size * cols
 
     def vmem(*kinds):
         return [pltpu.VMEM(shape, dtype) for shape, dtype in kinds]
 
-    small = pltpu.CompilerParams(vmem_limit_bytes=40 * 1024 * 1024)
     x, slots, side_a, side_b = pl.pallas_call(
         open_kernel,
         out_shape=in_hbm(x_kind, slots_kind, side_kind, side_kind),
@@ -554,6 +541,8 @@
         out_specs=(PLAIN,) * 4,
         scratch_shapes=vmem(state, basis_kind, x_kind, slots_kind)
         + [SEMS((loads,)), SEMS(()), SEMS(()), SEMS((3,))],
+        compiler_params=small,
+        cost_estimate=cost(BUSY, 0),
         name="open",
     )(*hbm(p, basis))
 
@@ -561,64 +550,58 @@
     known, factor, edge = pl.pallas_call(
         first_local_kernel,
         out_shape=in_hbm(state, state, edge_kind),
-        in_specs=[SCALARS] + [PLAIN] * 8,
+        in_specs=[SCALARS, PLAIN, PLAIN] + [WHOLE] * 6,
         out_specs=(PLAIN,) * 3,
-        scratch_shapes=vmem(
-            x_kind, near_kind, state, state, *[vector_kind] * 4, state, state, edge_kind, products_kind,
-            turned_kind, turned_kind,
-        )
-        + [where_kind, SEMS(())]
-        + [SEMS((pairs,))] * 3
-        + [SEMS((4,)), SEMS((pairs,)), SEMS((pairs,)), SEMS((1,))],
+        scratch_shapes=vmem(x_kind, near_kind, state, state, edge_kind, products_kind, turned_kind, turned_kind)
+        + [where_kind, SEMS(()), SEMS((pairs,)), SEMS((pairs,)), SEMS((pairs,)), SEMS((1,))],
+        compiler_params=small,
         cost_estimate=cost(near_flops, near_blocks.size * 2),
         name="local_one",
-    )(near_columns, *hbm(x, flat_near, p, s, stiff, plate, direct, evolve))
+    )(near_columns, *hbm(x, flat_near), *resident(p, s), stiff, plate, direct, evolve)
 
     p2, x, slots, side_a, side_b = pl.pallas_call(
         middle_kernel,
         out_shape=in_hbm(state, x_kind, slots_kind, side_kind, side_kind),
-        in_specs=[WHOLE] * 3 + [PLAIN] * 5,
+        in_specs=[WHOLE] * 3 + [PLAIN] + [WHOLE] + [PLAIN] * 3,
         out_specs=(PLAIN,) * 5,
-        scratch_shapes=vmem(
-            halo_kind, edge_kind, basis_kind, basis_kind, state, state, state, x_kind, slots_kind, coupled_kind
-        )
-        + [SEMS((3,)), SEMS((pairs,)), SEMS((pairs,)), SEMS((pairs,)), SEMS(()), SEMS((3,))],
+        scratch_shapes=vmem(halo_kind, edge_kind, basis_kind, state, state, state, x_kind, slots_kind, coupled_kind)
+        + [SEMS((2,)), SEMS((pairs,)), SEMS((pairs,)), SEMS((pairs,)), SEMS(()), SEMS((3,))],
         compiler_params=small,
+        cost_estimate=cost(BUSY, 0),
         name="middle",
-    )(got_a, got_b, got, *hbm(edge, coupling, basis, known, factor))
+    )(got_a, got_b, got, *hbm(edge), *resident(coupling), *hbm(basis, known, factor))
 
     got_a, got_b, got = exchange(side_a, side_b, slots)
     change, factor, new_s, errors = pl.pallas_call(
         second_local_kernel,
         out_shape=in_hbm(state, state, state, errors_kind),
-        in_specs=[SCALARS] + [PLAIN] * 10,
+        in_specs=[SCALARS, PLAIN, PLAIN] + [WHOLE] * 2 + [PLAIN] + [WHOLE] * 5,
         out_specs=(PLAIN,) * 4,
         scratch_shapes=vmem(
-            x_kind, near_kind, state, state, state, *[vector_kind] * 5, state, state, state, errors_kind,
-            products_kind, turned_kind, turned_kind, turned_kind,
+            x_kind, near_kind, state, state, state, state, errors_kind, products_kind, turned_kind, turned_kind,
+            turned_kind,
         )
         + [where_kind, SEMS(())]
-        + [SEMS((pairs,))] * 4
-        + [SEMS((5,))]
-        + [SEMS((pairs,))] * 3
+        + [SEMS((pairs,))] * 5
         + [SEMS((1,))],
+        compiler_params=small,
         cost_estimate=cost(near_flops, near_blocks.size * 2),
         name="local_two",
-    )(near_columns, *hbm(x, flat_near, p, s, p2, stiff, plate, direct, evolve, area))
+    )(near_columns, *hbm(x, flat_near), *resident(p, s), *hbm(p2), stiff, plate, direct, evolve, area)
 
     new_p, parts = pl.pallas_call(
         close_kernel,
         out_shape=in_hbm(state) + like(((devices, 2, cols), F32)),
-        in_specs=[WHOLE] * 3 + [PLAIN] * 7,
+        in_specs=[WHOLE] * 3 + [PLAIN] + [WHOLE] + [PLAIN] * 5,
         out_specs=(PLAIN, WHOLE),
         scratch_shapes=vmem(
-            halo_kind, edge_kind, basis_kind, state, state, state, state, coupled_kind, vector_kind, errors_kind
+            halo_kind, edge_kind, state, state, state, state, coupled_kind, vector_kind, errors_kind
         )
-        + [SEMS((4,))]
+        + [SEMS((3,))]
         + [SEMS((pairs,))] * 4,
         compiler_params=small,
         name="close",
-    )(got_a, got_b, got, *hbm(edge, coupling, p2, change, factor, area, errors))
+    )(got_a, got_b, got, *hbm(edge), *resident(coupling), *hbm(p2, change, factor, area, errors))
 
     totals = lax.all_to_all(parts, AXIS, 0, 0).sum(axis=0)
     error_norm = jnp.sqrt(totals[0] / totals[1] + 1e-06)

time: 65.3 us -> 60.9 us (0.933)
  Pallas kernels: 34 us -> 29.4 us
    pallas_call x1, Pallas kernels: 10.2 us -> 7.8 us  [on_device(): pl.pallas_call(second_local_kernel, out_shape=in_hbm(state, state, state,...]
    pallas_call x1, Pallas kernels: 10.3 us -> 8.21 us  [on_device(): pl.pallas_call(first_local_kernel, out_shape=in_hbm(state, state, edge_ki...]
  transfers between devices with their start and end apart: 6 -> 6, of which waited for: 0 -> 0; matrix products, arithmetic and copies ran while one was open for 0% -> 0% of each run, Pallas kernels for 32% -> 26%
where the time goes in v7:
time: 60.9 us; the launch traced here: 60.5 us
  Pallas kernels  29.4 us (48%)
  starting transfers between devices  20.5 us (34%)
  blocking collectives  9.07 us (15%)
  between operations  0.85 us (1%)
    all_to_all x2, starting transfers between devices, exchange(): got = lax.all_to_all(slots, AXIS, 0, 0)  11.1 us
    all_to_all x1, blocking collectives, on_device(): totals = lax.all_to_all(parts, AXIS, 0, 0).sum(axis=0)  9.07 us
    ppermute x2, starting transfers between devices, exchange(): got_b = lax.ppermute(side_b, AXIS, pairs)  8.75 us
    pallas_call x1, Pallas kernels, on_device(): pl.pallas_call(first_local_kernel, out_shape=in_hbm(state, state, edge_ki...  8.21 us
    pallas_call x1, Pallas kernels, on_device(): pl.pallas_call(second_local_kernel, out_shape=in_hbm(state, state, state,...  7.8 us
    pallas_call x1, Pallas kernels, on_device(): pl.pallas_call(close_kernel, out_shape=in_hbm(state) + like(((devices, 2,...  5.66 us
    pallas_call x1, Pallas kernels, on_device(): pl.pallas_call(middle_kernel, out_shape=in_hbm(state, x_kind, slots_kind,...  5.17 us
    pallas_call x1, Pallas kernels, on_device(): pl.pallas_call(open_kernel, out_shape=in_hbm(x_kind, slots_kind, side_kin...  2.6 us
  transfers between devices with their start and end apart: 6, of which 0 were waited for; matrix products, arithmetic and copies ran while one was open for 0% of the time, Pallas kernels for 26%

profile of v7, /device:TPU:0, one launch (start us, length us, event | category | flops | bytes accessed | tf_op | source)
XLA Modules:
  0.0 60.5 jit_solution(5490486800157182616)
XLA Ops:
  0.6 0.0 copy-start
  0.6 0.0 copy-start.1
  0.7 0.0 copy-start.3
  0.7 0.0 copy-start.4
  0.7 0.0 copy-start.5
  0.7 0.0 copy-start.6
  0.7 0.0 copy-start.7
  0.7 2.6 %open.1 = (bf16[16,128,128]{2,1,0:T(8,128)(2,1)}, bf16[16,32,128]{2,1,0:T(8,128)(2,1)}, bf16[6,128,128]{2,1,0:T(8,128)(2,1)}, bf16[6,128,128]{2,1,0:T(8,128)(2,1)}) custom-call(f32[16,128,128]{2,1,0:T(8,128)} %bitcast.14, bf16[128,2048]{1,0:T(8,128)(2,1)} %bitcast.35), custom_call_target="tpu_custom_call" | custom-call | flops 10000000000 | tf_op jit(solution)/shard_map/open/pallas_call | solution.py:537
  3.3 0.0 copy-start.2
  3.3 7.6 %all-to-all-start = ((bf16[16,32,128]{2,1,0:T(8,128)(2,1)}), bf16[16,32,128]{2,1,0:T(8,128)(2,1)S(1)}, u32[]{:S(2)}, u32[]{:S(2)}) async-start(bf16[16,32,128]{2,1,0:T(8,128)(2,1)} %get-tuple-element.23), calls=%async_computation | async-start | bytes 262144 | tf_op jit(solution)/shard_map/all_to_all | solution.py:485
  10.9 0.4 collective-permute-start
  11.3 4.3 %collective-permute-start.1 = (bf16[6,128,128]{2,1,0:T(8,128)(2,1)}, bf16[6,128,128]{2,1,0:T(8,128)(2,1)S(1)}, u32[]{:S(2)}, u32[]{:S(2)}) collective-permute-start(bf16[6,128,128]{2,1,0:T(8,128)(2,1)} %get-tuple-element.22), channel_id=1, source_target_pairs={{0,15},{1,2},{2,1},{3,4},{4,3},{5,6},{6,5},{7,8},{8,7},{9,10},{10,... | collective-permute-start | bytes 589832 | tf_op jit(solution)/shard_map/ppermute | solution.py:484
  15.6 0.0 copy-done.4
  15.7 0.0 copy-done.5
  15.7 0.0 copy-done.6
  15.7 0.0 copy-done.7
  15.7 8.2 %local_one.1 = (f32[16,128,128]{2,1,0:T(8,128)}, f32[16,128,128]{2,1,0:T(8,128)}, bf16[12,256,256]{2,1,0:T(8,128)(2,1)}) custom-call(s32[16,12]{1,0:T(8,128)S(1)} %copy-done.3, bf16[16,128,128]{2,1,0:T(8,128)(2,1)} %get-tuple-element.24.x_in, bf16[192,128,128]{2,1,0:T(8,128)(2,1)} %bitcast.31, f32[16,128,128]{2,1,0:T(8,128)S(1)} %bitcast.15, ...), custom_call_target="tpu_custom_call" | custom-call | flops 805306368 | bytes 6291456 | tf_op jit(solution)/shard_map/local_one/pallas_call | solution.py:550
  23.9 0.0 collective-permute-done.got_a
  23.9 0.0 collective-permute-done.1.got_b
  23.9 0.0 all-to-all-done.got
  23.9 0.0 copy-start.8
  23.9 5.2 %middle.1 = (f32[16,128,128]{2,1,0:T(8,128)}, bf16[16,128,128]{2,1,0:T(8,128)(2,1)}, bf16[16,32,128]{2,1,0:T(8,128)(2,1)}, bf16[6,128,128]{2,1,0:T(8,128)(2,1)}, bf16[6,128,128]{2,1,0:T(8,128)(2,1)}) custom-call(bf16[6,128,128]{2,1,0:T(8,128)(2,1)S(1)} %collective-permute-done.got_a, bf16[6,128,128]{2,1,0:T(8,128)(2,1)S(1)} %collective-permute-done.1.got_b, ...), custom_call_target="tpu_custom_call" | custom-call | flops 10000000000 | tf_op jit(solution)/shard_map/middle/pallas_call | solution.py:562
  29.1 3.5 %all-to-all-start.1 = ((bf16[16,32,128]{2,1,0:T(8,128)(2,1)}), bf16[16,32,128]{2,1,0:T(8,128)(2,1)S(1)}, u32[]{:S(2)}, u32[]{:S(2)}) async-start(bf16[16,32,128]{2,1,0:T(8,128)(2,1)} %get-tuple-element.30), calls=%async_computation.1 | async-start | bytes 262144 | tf_op jit(solution)/shard_map/all_to_all | solution.py:485
  32.7 0.3 collective-permute-start.2
  33.0 4.4 %collective-permute-start.3 = (bf16[6,128,128]{2,1,0:T(8,128)(2,1)}, bf16[6,128,128]{2,1,0:T(8,128)(2,1)S(1)}, u32[]{:S(2)}, u32[]{:S(2)}) collective-permute-start(bf16[6,128,128]{2,1,0:T(8,128)(2,1)} %get-tuple-element.29), channel_id=1, source_target_pairs={{0,15},{1,2},{2,1},{3,4},{4,3},{5,6},{6,5},{7,8},{8,7},{9,10},{10,... | collective-permute-start | bytes 589832 | tf_op jit(solution)/shard_map/ppermute | solution.py:484
  37.4 7.8 %local_two.1 = (f32[16,128,128]{2,1,0:T(8,128)}, f32[16,128,128]{2,1,0:T(8,128)}, f32[16,128,128]{2,1,0:T(8,128)}, f32[128,128]{1,0:T(8,128)}) custom-call(s32[16,12]{1,0:T(8,128)S(1)} %copy-done.3, bf16[16,128,128]{2,1,0:T(8,128)(2,1)} %get-tuple-element.32.x_in, bf16[192,128,128]{2,1,0:T(8,128)(2,1)} %bitcast.32, f32[16,128,128]{2,1,0:T(8,128)S(1)} %bitcast.16, ...), custom_call_target="tpu_custom_call" | custom-call | flops 805306368 | bytes 6291456 | tf_op jit(solution)/shard_map/local_two/pallas_call | solution.py:575
  45.2 0.0 collective-permute-done.2.got_a
  45.2 0.0 collective-permute-done.3.got_b
  45.2 0.0 all-to-all-done.1.got
  45.2 5.7 %close.1 = (f32[16,128,128]{2,1,0:T(8,128)}, f32[16,2,128]{2,1,0:T(2,128)S(1)}) custom-call(bf16[6,128,128]{2,1,0:T(8,128)(2,1)S(1)} %collective-permute-done.2.got_a, bf16[6,128,128]{2,1,0:T(8,128)(2,1)S(1)} %collective-permute-done.3.got_b, bf16[16,32,128]{2,1,0:T(8,128)(2,1)S(1)} %all-to-all-done.1.got, bf16[12,256,256]{2,1,0:T(8,128)(2,1)} %get-tuple-element.25.edge_in, ...), custom_call_target="tpu_custom_call" | custom-call | tf_op jit(solution)/shard_map/close/pallas_call | solution.py:592
  50.9 9.1 %all_to_all.15 = f32[16,2,128]{2,1,0:T(2,128)S(1)} all-to-all(f32[16,2,128]{2,1,0:T(2,128)S(1)} %get-tuple-element.38), channel_id=1, replica_groups=mesh['member'=2,'patch'=16] {'patch'}, dimensions={0} | all-to-all | bytes 32768 | tf_op jit(solution)/shard_map/all_to_all | solution.py:606
  60.0 0.5 sqrt_bitcast_fusion
  (6 shorter events, 0.0 us)
Async XLA Ops:
  0.6 15.0 %copy-start = (f32[2048,128]{1,0:T(8,128)S(1)}, f32[2048,128]{1,0:T(8,128)}, u32[]{:S(2)}) copy-start(f32[2048,128]{1,0:T(8,128)} %param.11) | copy-start | bytes 3145732
  0.6 15.0 %copy-start.1 = (f32[2048,128]{1,0:T(8,128)S(1)}, f32[2048,128]{1,0:T(8,128)}, u32[]{:S(2)}) copy-start(f32[2048,128]{1,0:T(8,128)} %param.12) | copy-start | bytes 3145732
  0.7 15.0 %copy-start.3 = (s32[16,12]{1,0:T(8,128)S(1)}, s32[16,12]{1,0:T(8,128)}, u32[]{:S(2)}) copy-start(s32[16,12]{1,0:T(8,128)} %columns.3) | copy-start | bytes 2308
  0.7 15.0 %copy-start.4 = (f32[2048]{0:T(1024)S(1)}, f32[2048]{0:T(1024)}, u32[]{:S(2)}) copy-start(f32[2048]{0:T(1024)} %param.17) | copy-start | bytes 24580
  0.7 15.0 %copy-start.5 = (f32[2048]{0:T(1024)S(1)}, f32[2048]{0:T(1024)}, u32[]{:S(2)}) copy-start(f32[2048]{0:T(1024)} %param.18) | copy-start | bytes 24580
  0.7 15.0 %copy-start.6 = (f32[2048]{0:T(1024)S(1)}, f32[2048]{0:T(1024)}, u32[]{:S(2)}) copy-start(f32[2048]{0:T(1024)} %param.19) | copy-start | bytes 24580
  0.7 15.0 %copy-start.7 = (f32[2048]{0:T(1024)S(1)}, f32[2048]{0:T(1024)}, u32[]{:S(2)}) copy-start(f32[2048]{0:T(1024)} %param.20) | copy-start | bytes 24580
  3.3 20.6 %copy-start.2 = (bf16[4,32,2048]{2,1,0:T(8,128)(2,1)S(1)}, bf16[4,32,2048]{2,1,0:T(8,128)(2,1)}, u32[]{:S(2)}) copy-start(bf16[4,32,2048]{2,1,0:T(8,128)(2,1)} %param.16) | copy-start | bytes 1572868
  3.3 20.6 %all-to-all-start = ((bf16[16,32,128]{2,1,0:T(8,128)(2,1)}), bf16[16,32,128]{2,1,0:T(8,128)(2,1)S(1)}, u32[]{:S(2)}, u32[]{:S(2)}) async-start(bf16[16,32,128]{2,1,0:T(8,128)(2,1)} %get-tuple-element.23), calls=%async_computation | async-start | bytes 262144 | tf_op jit(solution)/shard_map/all_to_all | solution.py:485
  10.9 13.0 %collective-permute-start = (bf16[6,128,128]{2,1,0:T(8,128)(2,1)}, bf16[6,128,128]{2,1,0:T(8,128)(2,1)S(1)}, u32[]{:S(2)}, u32[]{:S(2)}) collective-permute-start(bf16[6,128,128]{2,1,0:T(8,128)(2,1)} %get-tuple-element.21), channel_id=1, source_target_pairs={{0,1},{1,0},{2,3},{3,2},{4,5},{5,4},{6,7},{7,6},{8,9},{9,8},{10,11... | collective-permute-start | bytes 589832 | tf_op jit(solution)/shard_map/ppermute | solution.py:482
  11.3 12.6 %collective-permute-start.1 = (bf16[6,128,128]{2,1,0:T(8,128)(2,1)}, bf16[6,128,128]{2,1,0:T(8,128)(2,1)S(1)}, u32[]{:S(2)}, u32[]{:S(2)}) collective-permute-start(bf16[6,128,128]{2,1,0:T(8,128)(2,1)} %get-tuple-element.22), channel_id=1, source_target_pairs={{0,15},{1,2},{2,1},{3,4},{4,3},{5,6},{6,5},{7,8},{8,7},{9,10},{10,... | collective-permute-start | bytes 589832 | tf_op jit(solution)/shard_map/ppermute | solution.py:484
  23.9 13.4 %copy-start.8 = (f32[2048]{0:T(1024)S(1)}, f32[2048]{0:T(1024)}, u32[]{:S(2)}) copy-start(f32[2048]{0:T(1024)} %param.21) | copy-start | bytes 24580
  29.1 16.1 %all-to-all-start.1 = ((bf16[16,32,128]{2,1,0:T(8,128)(2,1)}), bf16[16,32,128]{2,1,0:T(8,128)(2,1)S(1)}, u32[]{:S(2)}, u32[]{:S(2)}) async-start(bf16[16,32,128]{2,1,0:T(8,128)(2,1)} %get-tuple-element.30), calls=%async_computation.1 | async-start | bytes 262144 | tf_op jit(solution)/shard_map/all_to_all | solution.py:485
  32.7 12.5 %collective-permute-start.2 = (bf16[6,128,128]{2,1,0:T(8,128)(2,1)}, bf16[6,128,128]{2,1,0:T(8,128)(2,1)S(1)}, u32[]{:S(2)}, u32[]{:S(2)}) collective-permute-start(bf16[6,128,128]{2,1,0:T(8,128)(2,1)} %get-tuple-element.28), channel_id=1, source_target_pairs={{0,1},{1,0},{2,3},{3,2},{4,5},{5,4},{6,7},{7,6},{8,9},{9,8},{10,11... | collective-permute-start | bytes 589832 | tf_op jit(solution)/shard_map/ppermute | solution.py:482
  33.0 12.2 %collective-permute-start.3 = (bf16[6,128,128]{2,1,0:T(8,128)(2,1)}, bf16[6,128,128]{2,1,0:T(8,128)(2,1)S(1)}, u32[]{:S(2)}, u32[]{:S(2)}) collective-permute-start(bf16[6,128,128]{2,1,0:T(8,128)(2,1)} %get-tuple-element.29), channel_id=1, source_target_pairs={{0,15},{1,2},{2,1},{3,4},{4,3},{5,6},{6,5},{7,8},{8,7},{9,10},{10,... | collective-permute-start | bytes 589832 | tf_op jit(solution)/shard_map/ppermute | solution.py:484

commit v8 on v7

--- a/solution.py
+++ b/solution.py
@@ -7,6 +7,7 @@
 
 
 REACH = 6
+PAD = REACH + REACH % 2
 STRIP = 32
 AHEAD = 3
 BUSY = 10**10
@@ -144,8 +145,7 @@
     lax.fori_loop(0, row_blocks, row, 0)
 
 
-def near_block(near, where, r, c):
-    offset = c - r
+def near_block(near, where, r, offset):
     if abs(offset) > REACH:
         return jnp.zeros(near.shape[1:], near.dtype)
     at = where[r, offset + REACH]
@@ -156,10 +156,9 @@
 
 
 def near_product(near, x, where, pair):
-    own = pair_columns(x.shape[0], pair)[1]
-    reached = range(2 * own[0], 2 * own[-1] + 2)
-    tiles = [side_by_side([near_block(near, where, r, c) for c in reached]) for r in (2 * pair, 2 * pair + 1)]
-    rates = side_by_side([x[c] for c in reached])
+    reached = range(2 * PAD + 2)
+    tiles = [side_by_side([near_block(near, where, 2 * pair + i, j - PAD - i) for j in reached]) for i in range(2)]
+    rates = side_by_side([x[2 * pair + j] for j in reached])
     return lax.dot_general(rates, jnp.concatenate(tiles, axis=0), NT, preferred_element_type=F32)
 
 
@@ -174,15 +173,22 @@
     return (stiff * (plate - velocity) - near_term - evolve * state) * factor, factor
 
 
-def in_pairs(pairs, wait, product, finish, store):
-    wait(0)
-    product(0)
-    for pair in range(pairs):
-        if pair + 1 < pairs:
-            wait(pair + 1)
-            product(pair + 1)
+def in_pairs(pairs, loads, product, finish, stores):
+    def body(pair, carry):
+        pl.when(pair + AHEAD < pairs)(lambda: start_all(loads(pair + AHEAD)))
+        wait_all(loads(pair))
+        product(pair)
         finish(pair)
-        store(pair)
+        start_all(stores(pair))
+        return carry
+
+    lax.fori_loop(0, pairs, body, 0)
+
+
+def clear_pads(x, row_blocks):
+    zeros = jnp.zeros((PAD,) + x.shape[1:], x.dtype)
+    x[:PAD] = zeros
+    x[PAD + row_blocks :] = zeros
 
 
 def start_all(copies):
@@ -201,11 +207,11 @@
     x, near, known, factor, edge, products, turned_p, turned_s,
     where, x_sem, near_sems, known_sems, factor_sems, rest_sems,
 ):
-    row_blocks, size, _ = x.shape
+    row_blocks, size, _ = p.shape
     pairs = row_blocks // 2
     vectors = (stiff, plate, direct, evolve)
     span = near.shape[0] // pairs
-    load_x = pltpu.make_async_copy(x_in, x, x_sem)
+    load_x = pltpu.make_async_copy(x_in, x.at[pl.ds(PAD, row_blocks)], x_sem)
 
     def loads(c):
         return [part(near_in, near, near_sems, c, span)]
@@ -216,41 +222,40 @@
     load_x.start()
     for c in range(AHEAD):
         start_all(loads(c))
+    clear_pads(x, row_blocks)
     find_blocks(columns, where)
     load_x.wait()
 
     def product(pair):
-        if pair + AHEAD < pairs:
-            start_all(loads(pair + AHEAD))
-        products[pair] = near_product(near, x, where, pair)
+        products[...] = near_product(near, x, where, pair)
 
     def finish(pair):
         for i in range(2):
             r = 2 * pair + i
-            rows = [v[r : r + 1] for v in vectors]
+            rows = [v[pl.ds(r, 1), :] for v in vectors]
             turned_p[i] = p[r].T
             turned_s[i] = s[r].T
             for at in strips(size):
                 now = turned_p[i, at]
                 velocity = jnp.exp(now)
                 state = jnp.exp(-turned_s[i, at]) - velocity
-                near_term = products[pair, at, i * size : (i + 1) * size]
+                near_term = products[at, i * size : (i + 1) * size]
                 rate, scale = known_rates(velocity, state, near_term, rows)
                 known[r, at] = now + step_size * rate
                 factor[r, at] = step_size * scale
 
     in_pairs(
         pairs,
-        lambda c: wait_all(loads(c)),
+        loads,
         product,
         finish,
-        lambda c: start_all(stores(c)),
+        stores,
     )
     for n, (pair, c) in enumerate(edge_tiles(row_blocks)):
         for i in range(2):
             for j in range(2):
                 edge[n, i * size : (i + 1) * size, j * size : (j + 1) * size] = near_block(
-                    near, where, 2 * pair + i, 2 * c + j
+                    near, where, 2 * pair + i, 2 * c + j - 2 * pair - i
                 )
     store_edge = pltpu.make_async_copy(edge, edge_out, rest_sems.at[0])
     store_edge.start()
@@ -266,11 +271,11 @@
     turned_p, turned_s, ended_s,
     where, x_sem, near_sems, p2_sems, change_sems, factor_sems, new_s_sems, rest_sems,
 ):
-    row_blocks, size, _ = x.shape
+    row_blocks, size, _ = p.shape
     pairs = row_blocks // 2
     vectors = (stiff, plate, direct, evolve, area)
     span = near.shape[0] // pairs
-    load_x = pltpu.make_async_copy(x_in, x, x_sem)
+    load_x = pltpu.make_async_copy(x_in, x.at[pl.ds(PAD, row_blocks)], x_sem)
 
     def loads(c):
         return [part(near_in, near, near_sems, c, span), part(p2_in, p2, p2_sems, c, 2)]
@@ -285,18 +290,18 @@
     load_x.start()
     for c in range(AHEAD):
         start_all(loads(c))
+    clear_pads(x, row_blocks)
+    errors[...] = jnp.zeros(errors.shape, F32)
     find_blocks(columns, where)
     load_x.wait()
 
     def product(pair):
-        if pair + AHEAD < pairs:
-            start_all(loads(pair + AHEAD))
-        products[pair] = near_product(near, x, where, pair)
+        products[...] = near_product(near, x, where, pair)
 
     def finish(pair):
         for i in range(2):
             r = 2 * pair + i
-            rows = [v[r : r + 1] for v in vectors]
+            rows = [v[pl.ds(r, 1), :] for v in vectors]
             turned_p[i] = p[r].T
             turned_s[i] = s[r].T
             for at in strips(size):
@@ -304,22 +309,22 @@
                 state_a = jnp.exp(-start) - jnp.exp(before)
                 velocity = jnp.exp(now)
                 state_b = jnp.exp(-(start + step_size * state_a)) - velocity
-                near_term = products[pair, at, i * size : (i + 1) * size]
+                near_term = products[at, i * size : (i + 1) * size]
                 rate, scale = known_rates(velocity, state_b, near_term, rows[:4])
                 change[r, at] = half_step * rate - (half_step / step_size) * (now - before)
                 factor[r, at] = half_step * scale
                 ended_s[i, at] = start + half_step * (state_a + state_b)
                 state_error = (half_step / error_scale) * (state_b - state_a)
                 weighted = rows[4] * (state_error * state_error)
-                errors[at] = weighted + errors[at] if r else weighted
+                errors[at] += weighted
             new_s[r] = ended_s[i].T
 
     in_pairs(
         pairs,
-        lambda c: wait_all(loads(c)),
+        loads,
         product,
         finish,
-        lambda c: start_all(stores(c)),
+        stores,
     )
     store_errors = pltpu.make_async_copy(errors, errors_out, rest_sems.at[0])
     store_errors.start()
@@ -523,7 +528,8 @@
     halo_kind = ((2 * REACH, size, cols), BF16)
     vector_kind = ((row_blocks, size), F32)
     errors_kind = ((cols, size), F32)
-    products_kind = ((pairs, cols, 2 * size), F32)
+    products_kind = ((cols, 2 * size), F32)
+    padded_kind = ((row_blocks + 2 * PAD, size, cols), BF16)
     coupled_kind = ((cols, levels * rank), BF16)
     turned_kind = ((2, cols, size), F32)
     where_kind = pltpu.SMEM((row_blocks, 2 * REACH + 1), jnp.int32)
@@ -552,7 +558,7 @@
         out_shape=in_hbm(state, state, edge_kind),
         in_specs=[SCALARS, PLAIN, PLAIN] + [WHOLE] * 6,
         out_specs=(PLAIN,) * 3,
-        scratch_shapes=vmem(x_kind, near_kind, state, state, edge_kind, products_kind, turned_kind, turned_kind)
+        scratch_shapes=vmem(padded_kind, near_kind, state, state, edge_kind, products_kind, turned_kind, turned_kind)
         + [where_kind, SEMS(()), SEMS((pairs,)), SEMS((pairs,)), SEMS((pairs,)), SEMS((1,))],
         compiler_params=small,
         cost_estimate=cost(near_flops, near_blocks.size * 2),
@@ -578,7 +584,7 @@
         in_specs=[SCALARS, PLAIN, PLAIN] + [WHOLE] * 2 + [PLAIN] + [WHOLE] * 5,
         out_specs=(PLAIN,) * 4,
         scratch_shapes=vmem(
-            x_kind, near_kind, state, state, state, state, errors_kind, products_kind, turned_kind, turned_kind,
+            padded_kind, near_kind, state, state, state, state, errors_kind, products_kind, turned_kind, turned_kind,
             turned_kind,
         )
         + [where_kind, SEMS(())]

time: 60.9 us -> 59.6 us (0.979)
  Pallas kernels: 29.4 us -> 28.2 us
    pallas_call x1, Pallas kernels: 7.8 us -> 7.13 us  [on_device(): pl.pallas_call(second_local_kernel, out_shape=in_hbm(state, state, state,...]
  transfers between devices with their start and end apart: 6 -> 6, of which waited for: 0 -> 0; matrix products, arithmetic and copies ran while one was open for 0% -> 0% of each run, Pallas kernels for 26% -> 25%
where the time goes in v8:
time: 59.6 us; the launch traced here: 59.3 us
  Pallas kernels  28.2 us (47%)
  starting transfers between devices  20.5 us (34%)
  blocking collectives  9.07 us (15%)
  between operations  0.85 us (1%)
    all_to_all x2, starting transfers between devices, exchange(): got = lax.all_to_all(slots, AXIS, 0, 0)  11.1 us
    all_to_all x1, blocking collectives, on_device(): totals = lax.all_to_all(parts, AXIS, 0, 0).sum(axis=0)  9.07 us
    ppermute x2, starting transfers between devices, exchange(): got_b = lax.ppermute(side_b, AXIS, pairs)  8.75 us
    pallas_call x1, Pallas kernels, on_device(): pl.pallas_call(first_local_kernel, out_shape=in_hbm(state, state, edge_ki...  7.63 us
    pallas_call x1, Pallas kernels, on_device(): pl.pallas_call(second_local_kernel, out_shape=in_hbm(state, state, state,...  7.13 us
    pallas_call x1, Pallas kernels, on_device(): pl.pallas_call(close_kernel, out_shape=in_hbm(state) + like(((devices, 2,...  5.65 us
    pallas_call x1, Pallas kernels, on_device(): pl.pallas_call(middle_kernel, out_shape=in_hbm(state, x_kind, slots_kind,...  5.17 us
    pallas_call x1, Pallas kernels, on_device(): pl.pallas_call(open_kernel, out_shape=in_hbm(x_kind, slots_kind, side_kin...  2.6 us
  transfers between devices with their start and end apart: 6, of which 0 were waited for; matrix products, arithmetic and copies ran while one was open for 0% of the time, Pallas kernels for 25%

profile of v8, /device:TPU:0, one launch (start us, length us, event | category | flops | bytes accessed | tf_op | source)
XLA Modules:
  0.0 59.3 jit_solution(13608813495585345334)
XLA Ops:
  0.6 0.0 copy-start
  0.6 0.0 copy-start.1
  0.7 0.0 copy-start.3
  0.7 0.0 copy-start.4
  0.7 0.0 copy-start.5
  0.7 0.0 copy-start.6
  0.7 0.0 copy-start.7
  0.7 2.6 %open.1 = (bf16[16,128,128]{2,1,0:T(8,128)(2,1)}, bf16[16,32,128]{2,1,0:T(8,128)(2,1)}, bf16[6,128,128]{2,1,0:T(8,128)(2,1)}, bf16[6,128,128]{2,1,0:T(8,128)(2,1)}) custom-call(f32[16,128,128]{2,1,0:T(8,128)} %bitcast.14, bf16[128,2048]{1,0:T(8,128)(2,1)} %bitcast.35), custom_call_target="tpu_custom_call" | custom-call | flops 10000000000 | tf_op jit(solution)/shard_map/open/pallas_call | solution.py:543
  3.3 0.0 copy-start.2
  3.3 7.6 %all-to-all-start = ((bf16[16,32,128]{2,1,0:T(8,128)(2,1)}), bf16[16,32,128]{2,1,0:T(8,128)(2,1)S(1)}, u32[]{:S(2)}, u32[]{:S(2)}) async-start(bf16[16,32,128]{2,1,0:T(8,128)(2,1)} %get-tuple-element.23), calls=%async_computation | async-start | bytes 262144 | tf_op jit(solution)/shard_map/all_to_all | solution.py:490
  10.9 0.4 collective-permute-start
  11.3 4.3 %collective-permute-start.1 = (bf16[6,128,128]{2,1,0:T(8,128)(2,1)}, bf16[6,128,128]{2,1,0:T(8,128)(2,1)S(1)}, u32[]{:S(2)}, u32[]{:S(2)}) collective-permute-start(bf16[6,128,128]{2,1,0:T(8,128)(2,1)} %get-tuple-element.22), channel_id=1, source_target_pairs={{0,15},{1,2},{2,1},{3,4},{4,3},{5,6},{6,5},{7,8},{8,7},{9,10},{10,... | collective-permute-start | bytes 589832 | tf_op jit(solution)/shard_map/ppermute | solution.py:489
  15.6 0.0 copy-done.4
  15.7 0.0 copy-done.5
  15.7 0.0 copy-done.6
  15.7 0.0 copy-done.7
  15.7 7.6 %local_one.1 = (f32[16,128,128]{2,1,0:T(8,128)}, f32[16,128,128]{2,1,0:T(8,128)}, bf16[12,256,256]{2,1,0:T(8,128)(2,1)}) custom-call(s32[16,12]{1,0:T(8,128)S(1)} %copy-done.3, bf16[16,128,128]{2,1,0:T(8,128)(2,1)} %get-tuple-element.24.x_in, bf16[192,128,128]{2,1,0:T(8,128)(2,1)} %bitcast.31, f32[16,128,128]{2,1,0:T(8,128)S(1)} %bitcast.15, ...), custom_call_target="tpu_custom_call" | custom-call | flops 805306368 | bytes 6291456 | tf_op jit(solution)/shard_map/local_one/pallas_call | solution.py:556
  23.3 0.0 collective-permute-done.got_a
  23.3 0.0 collective-permute-done.1.got_b
  23.3 0.0 all-to-all-done.got
  23.4 0.0 copy-start.8
  23.4 5.2 %middle.1 = (f32[16,128,128]{2,1,0:T(8,128)}, bf16[16,128,128]{2,1,0:T(8,128)(2,1)}, bf16[16,32,128]{2,1,0:T(8,128)(2,1)}, bf16[6,128,128]{2,1,0:T(8,128)(2,1)}, bf16[6,128,128]{2,1,0:T(8,128)(2,1)}) custom-call(bf16[6,128,128]{2,1,0:T(8,128)(2,1)S(1)} %collective-permute-done.got_a, bf16[6,128,128]{2,1,0:T(8,128)(2,1)S(1)} %collective-permute-done.1.got_b, ...), custom_call_target="tpu_custom_call" | custom-call | flops 10000000000 | tf_op jit(solution)/shard_map/middle/pallas_call | solution.py:568
  28.5 3.5 %all-to-all-start.1 = ((bf16[16,32,128]{2,1,0:T(8,128)(2,1)}), bf16[16,32,128]{2,1,0:T(8,128)(2,1)S(1)}, u32[]{:S(2)}, u32[]{:S(2)}) async-start(bf16[16,32,128]{2,1,0:T(8,128)(2,1)} %get-tuple-element.30), calls=%async_computation.1 | async-start | bytes 262144 | tf_op jit(solution)/shard_map/all_to_all | solution.py:490
  32.1 0.3 collective-permute-start.2
  32.4 4.4 %collective-permute-start.3 = (bf16[6,128,128]{2,1,0:T(8,128)(2,1)}, bf16[6,128,128]{2,1,0:T(8,128)(2,1)S(1)}, u32[]{:S(2)}, u32[]{:S(2)}) collective-permute-start(bf16[6,128,128]{2,1,0:T(8,128)(2,1)} %get-tuple-element.29), channel_id=1, source_target_pairs={{0,15},{1,2},{2,1},{3,4},{4,3},{5,6},{6,5},{7,8},{8,7},{9,10},{10,... | collective-permute-start | bytes 589832 | tf_op jit(solution)/shard_map/ppermute | solution.py:489
  36.8 7.1 %local_two.1 = (f32[16,128,128]{2,1,0:T(8,128)}, f32[16,128,128]{2,1,0:T(8,128)}, f32[16,128,128]{2,1,0:T(8,128)}, f32[128,128]{1,0:T(8,128)}) custom-call(s32[16,12]{1,0:T(8,128)S(1)} %copy-done.3, bf16[16,128,128]{2,1,0:T(8,128)(2,1)} %get-tuple-element.32.x_in, bf16[192,128,128]{2,1,0:T(8,128)(2,1)} %bitcast.32, f32[16,128,128]{2,1,0:T(8,128)S(1)} %bitcast.16, ...), custom_call_target="tpu_custom_call" | custom-call | flops 805306368 | bytes 6291456 | tf_op jit(solution)/shard_map/local_two/pallas_call | solution.py:581
  43.9 0.0 collective-permute-done.2.got_a
  43.9 0.0 collective-permute-done.3.got_b
  44.0 0.0 all-to-all-done.1.got
  44.0 5.7 %close.1 = (f32[16,128,128]{2,1,0:T(8,128)}, f32[16,2,128]{2,1,0:T(2,128)S(1)}) custom-call(bf16[6,128,128]{2,1,0:T(8,128)(2,1)S(1)} %collective-permute-done.2.got_a, bf16[6,128,128]{2,1,0:T(8,128)(2,1)S(1)} %collective-permute-done.3.got_b, bf16[16,32,128]{2,1,0:T(8,128)(2,1)S(1)} %all-to-all-done.1.got, bf16[12,256,256]{2,1,0:T(8,128)(2,1)} %get-tuple-element.25.edge_in, ...), custom_call_target="tpu_custom_call" | custom-call | tf_op jit(solution)/shard_map/close/pallas_call | solution.py:598
  49.6 9.1 %all_to_all.15 = f32[16,2,128]{2,1,0:T(2,128)S(1)} all-to-all(f32[16,2,128]{2,1,0:T(2,128)S(1)} %get-tuple-element.38), channel_id=1, replica_groups=mesh['member'=2,'patch'=16] {'patch'}, dimensions={0} | all-to-all | bytes 32768 | tf_op jit(solution)/shard_map/all_to_all | solution.py:612
  58.7 0.5 sqrt_bitcast_fusion
  (6 shorter events, 0.0 us)
Async XLA Ops:
  0.6 15.0 %copy-start = (f32[2048,128]{1,0:T(8,128)S(1)}, f32[2048,128]{1,0:T(8,128)}, u32[]{:S(2)}) copy-start(f32[2048,128]{1,0:T(8,128)} %param.11) | copy-start | bytes 3145732
  0.6 15.0 %copy-start.1 = (f32[2048,128]{1,0:T(8,128)S(1)}, f32[2048,128]{1,0:T(8,128)}, u32[]{:S(2)}) copy-start(f32[2048,128]{1,0:T(8,128)} %param.12) | copy-start | bytes 3145732
  0.7 15.0 %copy-start.3 = (s32[16,12]{1,0:T(8,128)S(1)}, s32[16,12]{1,0:T(8,128)}, u32[]{:S(2)}) copy-start(s32[16,12]{1,0:T(8,128)} %columns.3) | copy-start | bytes 2308
  0.7 15.0 %copy-start.4 = (f32[2048]{0:T(1024)S(1)}, f32[2048]{0:T(1024)}, u32[]{:S(2)}) copy-start(f32[2048]{0:T(1024)} %param.17) | copy-start | bytes 24580
  0.7 15.0 %copy-start.5 = (f32[2048]{0:T(1024)S(1)}, f32[2048]{0:T(1024)}, u32[]{:S(2)}) copy-start(f32[2048]{0:T(1024)} %param.18) | copy-start | bytes 24580
  0.7 15.0 %copy-start.6 = (f32[2048]{0:T(1024)S(1)}, f32[2048]{0:T(1024)}, u32[]{:S(2)}) copy-start(f32[2048]{0:T(1024)} %param.19) | copy-start | bytes 24580
  0.7 15.0 %copy-start.7 = (f32[2048]{0:T(1024)S(1)}, f32[2048]{0:T(1024)}, u32[]{:S(2)}) copy-start(f32[2048]{0:T(1024)} %param.20) | copy-start | bytes 24580
  3.3 20.0 %copy-start.2 = (bf16[4,32,2048]{2,1,0:T(8,128)(2,1)S(1)}, bf16[4,32,2048]{2,1,0:T(8,128)(2,1)}, u32[]{:S(2)}) copy-start(bf16[4,32,2048]{2,1,0:T(8,128)(2,1)} %param.16) | copy-start | bytes 1572868
  3.3 20.0 %all-to-all-start = ((bf16[16,32,128]{2,1,0:T(8,128)(2,1)}), bf16[16,32,128]{2,1,0:T(8,128)(2,1)S(1)}, u32[]{:S(2)}, u32[]{:S(2)}) async-start(bf16[16,32,128]{2,1,0:T(8,128)(2,1)} %get-tuple-element.23), calls=%async_computation | async-start | bytes 262144 | tf_op jit(solution)/shard_map/all_to_all | solution.py:490
  10.9 12.4 %collective-permute-start = (bf16[6,128,128]{2,1,0:T(8,128)(2,1)}, bf16[6,128,128]{2,1,0:T(8,128)(2,1)S(1)}, u32[]{:S(2)}, u32[]{:S(2)}) collective-permute-start(bf16[6,128,128]{2,1,0:T(8,128)(2,1)} %get-tuple-element.21), channel_id=1, source_target_pairs={{0,1},{1,0},{2,3},{3,2},{4,5},{5,4},{6,7},{7,6},{8,9},{9,8},{10,11... | collective-permute-start | bytes 589832 | tf_op jit(solution)/shard_map/ppermute | solution.py:487
  11.3 12.0 %collective-permute-start.1 = (bf16[6,128,128]{2,1,0:T(8,128)(2,1)}, bf16[6,128,128]{2,1,0:T(8,128)(2,1)S(1)}, u32[]{:S(2)}, u32[]{:S(2)}) collective-permute-start(bf16[6,128,128]{2,1,0:T(8,128)(2,1)} %get-tuple-element.22), channel_id=1, source_target_pairs={{0,15},{1,2},{2,1},{3,4},{4,3},{5,6},{6,5},{7,8},{8,7},{9,10},{10,... | collective-permute-start | bytes 589832 | tf_op jit(solution)/shard_map/ppermute | solution.py:489
  23.4 13.4 %copy-start.8 = (f32[2048]{0:T(1024)S(1)}, f32[2048]{0:T(1024)}, u32[]{:S(2)}) copy-start(f32[2048]{0:T(1024)} %param.21) | copy-start | bytes 24580
  28.5 15.4 %all-to-all-start.1 = ((bf16[16,32,128]{2,1,0:T(8,128)(2,1)}), bf16[16,32,128]{2,1,0:T(8,128)(2,1)S(1)}, u32[]{:S(2)}, u32[]{:S(2)}) async-start(bf16[16,32,128]{2,1,0:T(8,128)(2,1)} %get-tuple-element.30), calls=%async_computation.1 | async-start | bytes 262144 | tf_op jit(solution)/shard_map/all_to_all | solution.py:490
  32.1 11.9 %collective-permute-start.2 = (bf16[6,128,128]{2,1,0:T(8,128)(2,1)}, bf16[6,128,128]{2,1,0:T(8,128)(2,1)S(1)}, u32[]{:S(2)}, u32[]{:S(2)}) collective-permute-start(bf16[6,128,128]{2,1,0:T(8,128)(2,1)} %get-tuple-element.28), channel_id=1, source_target_pairs={{0,1},{1,0},{2,3},{3,2},{4,5},{5,4},{6,7},{7,6},{8,9},{9,8},{10,11... | collective-permute-start | bytes 589832 | tf_op jit(solution)/shard_map/ppermute | solution.py:487
  32.4 11.6 %collective-permute-start.3 = (bf16[6,128,128]{2,1,0:T(8,128)(2,1)}, bf16[6,128,128]{2,1,0:T(8,128)(2,1)S(1)}, u32[]{:S(2)}, u32[]{:S(2)}) collective-permute-start(bf16[6,128,128]{2,1,0:T(8,128)(2,1)} %get-tuple-element.29), channel_id=1, source_target_pairs={{0,15},{1,2},{2,1},{3,4},{4,3},{5,6},{6,5},{7,8},{8,7},{9,10},{10,... | collective-permute-start | bytes 589832 | tf_op jit(solution)/shard_map/ppermute | solution.py:489

commit v9 on v8

--- a/solution.py
+++ b/solution.py
@@ -251,17 +251,18 @@
         finish,
         stores,
     )
-    for n, (pair, c) in enumerate(edge_tiles(row_blocks)):
+    tiles = edge_tiles(row_blocks)
+    edge_stores = [part(edge, edge_out, rest_sems, n, 1) for n in range(len(tiles))]
+    for n, (pair, c) in enumerate(tiles):
         for i in range(2):
             for j in range(2):
                 edge[n, i * size : (i + 1) * size, j * size : (j + 1) * size] = near_block(
                     near, where, 2 * pair + i, 2 * c + j - 2 * pair - i
                 )
-    store_edge = pltpu.make_async_copy(edge, edge_out, rest_sems.at[0])
-    store_edge.start()
+        edge_stores[n].start()
     for c in range(pairs):
         wait_all(stores(c))
-    store_edge.wait()
+    wait_all(edge_stores)
 
 
 def second_local_kernel(
@@ -379,7 +380,7 @@
     ahead = 4
     for c in order[:ahead]:
         start_all(loads(c))
-        if c == order[0]:
+        if c == order[max(first_edged - 1, 0)]:
             start_all(outer)
     start()
     for n, c in enumerate(order):
@@ -559,7 +560,7 @@
         in_specs=[SCALARS, PLAIN, PLAIN] + [WHOLE] * 6,
         out_specs=(PLAIN,) * 3,
         scratch_shapes=vmem(padded_kind, near_kind, state, state, edge_kind, products_kind, turned_kind, turned_kind)
-        + [where_kind, SEMS(()), SEMS((pairs,)), SEMS((pairs,)), SEMS((pairs,)), SEMS((1,))],
+        + [where_kind, SEMS(()), SEMS((pairs,)), SEMS((pairs,)), SEMS((pairs,)), SEMS(edge_kind[0][:1])],
         compiler_params=small,
         cost_estimate=cost(near_flops, near_blocks.size * 2),
         name="local_one",

time: 59.6 us -> 59.4 us (level)
  no operation moved by 1% of the time
where the time goes in v9:
time: 59.4 us; the launch traced here: 59 us
  Pallas kernels  28 us (47%)
  starting transfers between devices  20.5 us (35%)
  blocking collectives  9.07 us (15%)
  between operations  0.85 us (1%)
    all_to_all x2, starting transfers between devices, exchange(): got = lax.all_to_all(slots, AXIS, 0, 0)  11.1 us
    all_to_all x1, blocking collectives, on_device(): totals = lax.all_to_all(parts, AXIS, 0, 0).sum(axis=0)  9.07 us
    ppermute x2, starting transfers between devices, exchange(): got_b = lax.ppermute(side_b, AXIS, pairs)  8.75 us
    pallas_call x1, Pallas kernels, on_device(): pl.pallas_call(first_local_kernel, out_shape=in_hbm(state, state, edge_ki...  7.39 us
    pallas_call x1, Pallas kernels, on_device(): pl.pallas_call(second_local_kernel, out_shape=in_hbm(state, state, state,...  7.13 us
    pallas_call x1, Pallas kernels, on_device(): pl.pallas_call(close_kernel, out_shape=in_hbm(state) + like(((devices, 2,...  5.68 us
    pallas_call x1, Pallas kernels, on_device(): pl.pallas_call(middle_kernel, out_shape=in_hbm(state, x_kind, slots_kind,...  5.17 us
    pallas_call x1, Pallas kernels, on_device(): pl.pallas_call(open_kernel, out_shape=in_hbm(x_kind, slots_kind, side_kin...  2.6 us
  transfers between devices with their start and end apart: 6, of which 0 were waited for; matrix products, arithmetic and copies ran while one was open for 0% of the time, Pallas kernels for 25%

profile of v9, /device:TPU:0, one launch (start us, length us, event | category | flops | bytes accessed | tf_op | source)
XLA Modules:
  0.0 59.0 jit_solution(16215403282263757446)
XLA Ops:
  0.6 0.0 copy-start
  0.6 0.0 copy-start.1
  0.7 0.0 copy-start.3
  0.7 0.0 copy-start.4
  0.7 0.0 copy-start.5
  0.7 0.0 copy-start.6
  0.7 0.0 copy-start.7
  0.7 2.6 %open.1 = (bf16[16,128,128]{2,1,0:T(8,128)(2,1)}, bf16[16,32,128]{2,1,0:T(8,128)(2,1)}, bf16[6,128,128]{2,1,0:T(8,128)(2,1)}, bf16[6,128,128]{2,1,0:T(8,128)(2,1)}) custom-call(f32[16,128,128]{2,1,0:T(8,128)} %bitcast.14, bf16[128,2048]{1,0:T(8,128)(2,1)} %bitcast.35), custom_call_target="tpu_custom_call" | custom-call | flops 10000000000 | tf_op jit(solution)/shard_map/open/pallas_call | solution.py:544
  3.3 0.0 copy-start.2
  3.3 7.6 %all-to-all-start = ((bf16[16,32,128]{2,1,0:T(8,128)(2,1)}), bf16[16,32,128]{2,1,0:T(8,128)(2,1)S(1)}, u32[]{:S(2)}, u32[]{:S(2)}) async-start(bf16[16,32,128]{2,1,0:T(8,128)(2,1)} %get-tuple-element.23), calls=%async_computation | async-start | bytes 262144 | tf_op jit(solution)/shard_map/all_to_all | solution.py:491
  10.9 0.4 collective-permute-start
  11.3 4.3 %collective-permute-start.1 = (bf16[6,128,128]{2,1,0:T(8,128)(2,1)}, bf16[6,128,128]{2,1,0:T(8,128)(2,1)S(1)}, u32[]{:S(2)}, u32[]{:S(2)}) collective-permute-start(bf16[6,128,128]{2,1,0:T(8,128)(2,1)} %get-tuple-element.22), channel_id=1, source_target_pairs={{0,15},{1,2},{2,1},{3,4},{4,3},{5,6},{6,5},{7,8},{8,7},{9,10},{10,... | collective-permute-start | bytes 589832 | tf_op jit(solution)/shard_map/ppermute | solution.py:490
  15.6 0.0 copy-done.4
  15.7 0.0 copy-done.5
  15.7 0.0 copy-done.6
  15.7 0.0 copy-done.7
  15.7 7.4 %local_one.1 = (f32[16,128,128]{2,1,0:T(8,128)}, f32[16,128,128]{2,1,0:T(8,128)}, bf16[12,256,256]{2,1,0:T(8,128)(2,1)}) custom-call(s32[16,12]{1,0:T(8,128)S(1)} %copy-done.3, bf16[16,128,128]{2,1,0:T(8,128)(2,1)} %get-tuple-element.24.x_in, bf16[192,128,128]{2,1,0:T(8,128)(2,1)} %bitcast.31, f32[16,128,128]{2,1,0:T(8,128)S(1)} %bitcast.15, ...), custom_call_target="tpu_custom_call" | custom-call | flops 805306368 | bytes 6291456 | tf_op jit(solution)/shard_map/local_one/pallas_call | solution.py:557
  23.1 0.0 collective-permute-done.got_a
  23.1 0.0 collective-permute-done.1.got_b
  23.1 0.0 all-to-all-done.got
  23.1 0.0 copy-start.8
  23.1 5.2 %middle.1 = (f32[16,128,128]{2,1,0:T(8,128)}, bf16[16,128,128]{2,1,0:T(8,128)(2,1)}, bf16[16,32,128]{2,1,0:T(8,128)(2,1)}, bf16[6,128,128]{2,1,0:T(8,128)(2,1)}, bf16[6,128,128]{2,1,0:T(8,128)(2,1)}) custom-call(bf16[6,128,128]{2,1,0:T(8,128)(2,1)S(1)} %collective-permute-done.got_a, bf16[6,128,128]{2,1,0:T(8,128)(2,1)S(1)} %collective-permute-done.1.got_b, ...), custom_call_target="tpu_custom_call" | custom-call | flops 10000000000 | tf_op jit(solution)/shard_map/middle/pallas_call | solution.py:569
  28.3 3.5 %all-to-all-start.1 = ((bf16[16,32,128]{2,1,0:T(8,128)(2,1)}), bf16[16,32,128]{2,1,0:T(8,128)(2,1)S(1)}, u32[]{:S(2)}, u32[]{:S(2)}) async-start(bf16[16,32,128]{2,1,0:T(8,128)(2,1)} %get-tuple-element.30), calls=%async_computation.1 | async-start | bytes 262144 | tf_op jit(solution)/shard_map/all_to_all | solution.py:491
  31.8 0.3 collective-permute-start.2
  32.1 4.4 %collective-permute-start.3 = (bf16[6,128,128]{2,1,0:T(8,128)(2,1)}, bf16[6,128,128]{2,1,0:T(8,128)(2,1)S(1)}, u32[]{:S(2)}, u32[]{:S(2)}) collective-permute-start(bf16[6,128,128]{2,1,0:T(8,128)(2,1)} %get-tuple-element.29), channel_id=1, source_target_pairs={{0,15},{1,2},{2,1},{3,4},{4,3},{5,6},{6,5},{7,8},{8,7},{9,10},{10,... | collective-permute-start | bytes 589832 | tf_op jit(solution)/shard_map/ppermute | solution.py:490
  36.5 7.1 %local_two.1 = (f32[16,128,128]{2,1,0:T(8,128)}, f32[16,128,128]{2,1,0:T(8,128)}, f32[16,128,128]{2,1,0:T(8,128)}, f32[128,128]{1,0:T(8,128)}) custom-call(s32[16,12]{1,0:T(8,128)S(1)} %copy-done.3, bf16[16,128,128]{2,1,0:T(8,128)(2,1)} %get-tuple-element.32.x_in, bf16[192,128,128]{2,1,0:T(8,128)(2,1)} %bitcast.32, f32[16,128,128]{2,1,0:T(8,128)S(1)} %bitcast.16, ...), custom_call_target="tpu_custom_call" | custom-call | flops 805306368 | bytes 6291456 | tf_op jit(solution)/shard_map/local_two/pallas_call | solution.py:582
  43.7 0.0 collective-permute-done.2.got_a
  43.7 0.0 collective-permute-done.3.got_b
  43.7 0.0 all-to-all-done.1.got
  43.7 5.7 %close.1 = (f32[16,128,128]{2,1,0:T(8,128)}, f32[16,2,128]{2,1,0:T(2,128)S(1)}) custom-call(bf16[6,128,128]{2,1,0:T(8,128)(2,1)S(1)} %collective-permute-done.2.got_a, bf16[6,128,128]{2,1,0:T(8,128)(2,1)S(1)} %collective-permute-done.3.got_b, bf16[16,32,128]{2,1,0:T(8,128)(2,1)S(1)} %all-to-all-done.1.got, bf16[12,256,256]{2,1,0:T(8,128)(2,1)} %get-tuple-element.25.edge_in, ...), custom_call_target="tpu_custom_call" | custom-call | tf_op jit(solution)/shard_map/close/pallas_call | solution.py:599
  49.4 9.1 %all_to_all.15 = f32[16,2,128]{2,1,0:T(2,128)S(1)} all-to-all(f32[16,2,128]{2,1,0:T(2,128)S(1)} %get-tuple-element.38), channel_id=1, replica_groups=mesh['member'=2,'patch'=16] {'patch'}, dimensions={0} | all-to-all | bytes 32768 | tf_op jit(solution)/shard_map/all_to_all | solution.py:613
  58.5 0.5 sqrt_bitcast_fusion
  (6 shorter events, 0.0 us)
Async XLA Ops:
  0.6 15.0 %copy-start = (f32[2048,128]{1,0:T(8,128)S(1)}, f32[2048,128]{1,0:T(8,128)}, u32[]{:S(2)}) copy-start(f32[2048,128]{1,0:T(8,128)} %param.11) | copy-start | bytes 3145732
  0.6 15.0 %copy-start.1 = (f32[2048,128]{1,0:T(8,128)S(1)}, f32[2048,128]{1,0:T(8,128)}, u32[]{:S(2)}) copy-start(f32[2048,128]{1,0:T(8,128)} %param.12) | copy-start | bytes 3145732
  0.7 15.0 %copy-start.3 = (s32[16,12]{1,0:T(8,128)S(1)}, s32[16,12]{1,0:T(8,128)}, u32[]{:S(2)}) copy-start(s32[16,12]{1,0:T(8,128)} %columns.3) | copy-start | bytes 2308
  0.7 15.0 %copy-start.4 = (f32[2048]{0:T(1024)S(1)}, f32[2048]{0:T(1024)}, u32[]{:S(2)}) copy-start(f32[2048]{0:T(1024)} %param.17) | copy-start | bytes 24580
  0.7 15.0 %copy-start.5 = (f32[2048]{0:T(1024)S(1)}, f32[2048]{0:T(1024)}, u32[]{:S(2)}) copy-start(f32[2048]{0:T(1024)} %param.18) | copy-start | bytes 24580
  0.7 15.0 %copy-start.6 = (f32[2048]{0:T(1024)S(1)}, f32[2048]{0:T(1024)}, u32[]{:S(2)}) copy-start(f32[2048]{0:T(1024)} %param.19) | copy-start | bytes 24580
  0.7 15.0 %copy-start.7 = (f32[2048]{0:T(1024)S(1)}, f32[2048]{0:T(1024)}, u32[]{:S(2)}) copy-start(f32[2048]{0:T(1024)} %param.20) | copy-start | bytes 24580
  3.3 19.8 %copy-start.2 = (bf16[4,32,2048]{2,1,0:T(8,128)(2,1)S(1)}, bf16[4,32,2048]{2,1,0:T(8,128)(2,1)}, u32[]{:S(2)}) copy-start(bf16[4,32,2048]{2,1,0:T(8,128)(2,1)} %param.16) | copy-start | bytes 1572868
  3.3 19.8 %all-to-all-start = ((bf16[16,32,128]{2,1,0:T(8,128)(2,1)}), bf16[16,32,128]{2,1,0:T(8,128)(2,1)S(1)}, u32[]{:S(2)}, u32[]{:S(2)}) async-start(bf16[16,32,128]{2,1,0:T(8,128)(2,1)} %get-tuple-element.23), calls=%async_computation | async-start | bytes 262144 | tf_op jit(solution)/shard_map/all_to_all | solution.py:491
  10.9 12.2 %collective-permute-start = (bf16[6,128,128]{2,1,0:T(8,128)(2,1)}, bf16[6,128,128]{2,1,0:T(8,128)(2,1)S(1)}, u32[]{:S(2)}, u32[]{:S(2)}) collective-permute-start(bf16[6,128,128]{2,1,0:T(8,128)(2,1)} %get-tuple-element.21), channel_id=1, source_target_pairs={{0,1},{1,0},{2,3},{3,2},{4,5},{5,4},{6,7},{7,6},{8,9},{9,8},{10,11... | collective-permute-start | bytes 589832 | tf_op jit(solution)/shard_map/ppermute | solution.py:488
  11.3 11.8 %collective-permute-start.1 = (bf16[6,128,128]{2,1,0:T(8,128)(2,1)}, bf16[6,128,128]{2,1,0:T(8,128)(2,1)S(1)}, u32[]{:S(2)}, u32[]{:S(2)}) collective-permute-start(bf16[6,128,128]{2,1,0:T(8,128)(2,1)} %get-tuple-element.22), channel_id=1, source_target_pairs={{0,15},{1,2},{2,1},{3,4},{4,3},{5,6},{6,5},{7,8},{8,7},{9,10},{10,... | collective-permute-start | bytes 589832 | tf_op jit(solution)/shard_map/ppermute | solution.py:490
  23.1 13.4 %copy-start.8 = (f32[2048]{0:T(1024)S(1)}, f32[2048]{0:T(1024)}, u32[]{:S(2)}) copy-start(f32[2048]{0:T(1024)} %param.21) | copy-start | bytes 24580
  28.3 15.4 %all-to-all-start.1 = ((bf16[16,32,128]{2,1,0:T(8,128)(2,1)}), bf16[16,32,128]{2,1,0:T(8,128)(2,1)S(1)}, u32[]{:S(2)}, u32[]{:S(2)}) async-start(bf16[16,32,128]{2,1,0:T(8,128)(2,1)} %get-tuple-element.30), calls=%async_computation.1 | async-start | bytes 262144 | tf_op jit(solution)/shard_map/all_to_all | solution.py:491
  31.8 11.9 %collective-permute-start.2 = (bf16[6,128,128]{2,1,0:T(8,128)(2,1)}, bf16[6,128,128]{2,1,0:T(8,128)(2,1)S(1)}, u32[]{:S(2)}, u32[]{:S(2)}) collective-permute-start(bf16[6,128,128]{2,1,0:T(8,128)(2,1)} %get-tuple-element.28), channel_id=1, source_target_pairs={{0,1},{1,0},{2,3},{3,2},{4,5},{5,4},{6,7},{7,6},{8,9},{9,8},{10,11... | collective-permute-start | bytes 589832 | tf_op jit(solution)/shard_map/ppermute | solution.py:488
  32.1 11.6 %collective-permute-start.3 = (bf16[6,128,128]{2,1,0:T(8,128)(2,1)}, bf16[6,128,128]{2,1,0:T(8,128)(2,1)S(1)}, u32[]{:S(2)}, u32[]{:S(2)}) collective-permute-start(bf16[6,128,128]{2,1,0:T(8,128)(2,1)} %get-tuple-element.29), channel_id=1, source_target_pairs={{0,15},{1,2},{2,1},{3,4},{4,3},{5,6},{6,5},{7,8},{8,7},{9,10},{10,... | collective-permute-start | bytes 589832 | tf_op jit(solution)/shard_map/ppermute | solution.py:490
